TPU v7x, 128 devices: a whole 4x4x4 slice. The times are simulated.
128 devices in a mesh: px: 8 (over x, core), py: 16 (over z, y).
Axes of the slice: x: 4, y: 4, z: 4, core: 2. Of those that a mesh axis runs over, the one named last changes fastest.
Arguments:
- theta: float32 [58, 128, 4096], P(None, 'px', 'py'), may hold values from 0.5 to 1.5
- vapor: float32 [58, 128, 4096], P(None, 'px', 'py'), may hold values from 0.1 to 1
- cloud: float32 [58, 128, 4096], P(None, 'px', 'py'), may hold values from 0 to 0.4
- divergence: float32 [58, 128, 4096], P(None, 'px', 'py'), may hold values from -6 to 6
- edge_weight: float32 [3, 128, 4096], P(None, 'px', 'py'), may hold values from 0.5 to 2
- inv_area: float32 [128, 4096], P('px', 'py'), may hold values from 0.7 to 1.4
- damping: float32 [3, 58], replicated, may hold values from 0.0005 to 0.004
- exner: float32 [58], replicated, may hold values from 0.6 to 1
- sat_scale: float32 [58], replicated, may hold values from 0.1 to 0.6
- layer_mass: float32 [58], replicated, may hold values from 0.02 to 0.1
- span_of: int32 [128, 4096], P('px', 'py'), may hold values from 0 to 65535, as said below
Outputs:
- theta_next: float32 [58, 128, 4096], P(None, 'px', 'py')
- vapor_next: float32 [58, 128, 4096], P(None, 'px', 'py')
- cloud_next: float32 [58, 128, 4096], P(None, 'px', 'py')
- divergence_next: float32 [58, 128, 4096], P(None, 'px', 'py')
- precip_spans: float32 [8, 65536], P('px', 'py')
Inputs may be any that keep to these rules, and one draw needn't show every extreme that they name: `span_of`: position p of px index a belongs to device p // 4096 of the py row of a. Within the 16 rows of one px index the entries are a permutation. The columns of one device take exactly 192 positions of every device of its row and 1024 more positions of one other device of that row, so each device receives exactly 4096 positions.
All inputs are finite; a program needn't handle non-finite values.
Results may differ from a plain program's by a relative error of at most 0.00002.
Values sent between devices are 32-bit elements; how exact they have to be, the bound alone decides.
No kernel may reach another device: no remote copies, remote signals or barrier semaphores. Data moves between devices by JAX's collectives and lax.ppermute only.
A program may use at most 128 MiB of HBM per device.

v0:
```python
import jax
import jax.numpy as jnp
from jax import lax
from jax.sharding import PartitionSpec as P

NSAT = 2


LATENT = 0.5
QCRIT = 0.2
AUTO_RATE = 0.5


def extended(cells, sides, width):
    for axis, dim in sides:
        count = lax.axis_size(axis)
        head = lax.slice_in_dim(cells, 0, width, axis=dim)
        tail = lax.slice_in_dim(cells, cells.shape[dim] - width, cells.shape[dim], axis=dim)
        cells = jnp.concatenate(
            [
                lax.ppermute(tail, axis, [(i, (i + 1) % count) for i in range(count)]),
                cells,
                lax.ppermute(head, axis, [((i + 1) % count, i) for i in range(count)]),
            ],
            axis=dim,
        )
    return cells


def shifted(array_in, step_row, step_col):
    height = array_in.shape[-2]
    breadth = array_in.shape[-1]
    return array_in[
        ..., 1 + step_row : height - 1 + step_row, 1 + step_col : breadth - 1 + step_col
    ]


def laplace(values, weights, inverse):
    centre = shifted(values, 0, 0)
    summed = shifted(weights[0], 0, 0) * (shifted(values, 1, 0) - centre)
    summed = summed + shifted(weights[0], -1, 0) * (shifted(values, -1, 0) - centre)
    summed = summed + shifted(weights[1], 0, 0) * (shifted(values, 0, 1) - centre)
    summed = summed + shifted(weights[1], 0, -1) * (shifted(values, 0, -1) - centre)
    summed = summed + shifted(weights[2], 0, 0) * (shifted(values, -1, 1) - centre)
    summed = summed + shifted(weights[2], 1, -1) * (shifted(values, 1, -1) - centre)
    return shifted(inverse, 0, 0) * summed


def adjust(theta_dyn, vapor_dyn, cloud, exner, sat_scale, layer_mass):
    temper = theta_dyn * exner
    condensed = jnp.zeros_like(theta_dyn)
    for repeat in range(NSAT):
        warmed = temper + LATENT * condensed
        saturation = sat_scale * jnp.exp(warmed)
        excess = vapor_dyn - condensed - saturation
        slope = -1.0 - LATENT * saturation
        condensed = condensed - excess / slope
    condensed = jnp.maximum(condensed, -cloud)
    theta_next = theta_dyn + LATENT * condensed / exner
    vapor_next = vapor_dyn - condensed
    liquid = cloud + condensed
    rained = AUTO_RATE * jnp.maximum(liquid - QCRIT, 0.0)
    cloud_next = liquid - rained
    precip = jnp.sum(layer_mass * rained, axis=0)
    return (theta_next, vapor_next, cloud_next, precip)


def on_device(
    theta,
    vapor,
    cloud,
    divergence,
    edge_weight,
    inv_area,
    damping,
    exner,
    sat_scale,
    layer_mass,
    span_of,
):
    levels = theta.shape[0]
    row_count = theta.shape[1]
    across = theta.shape[2]
    columns = row_count * across
    stacked = 3 * levels
    fields = jnp.concatenate([theta, vapor, divergence], 0)
    geometry = jnp.concatenate([edge_weight, inv_area[None]], 0)
    combined = jnp.concatenate([fields, geometry], 0)
    padded = extended(combined, (("px", 1), ("py", 2)), 1)
    geometry_pad = padded[stacked:]
    lap_once = laplace(padded[:stacked], geometry_pad[:3], geometry_pad[3])
    lap_padded = extended(lap_once, (("px", 1), ("py", 2)), 1)
    second = laplace(lap_padded, geometry_pad[:3], geometry_pad[3])
    damped = fields - damping.reshape(stacked)[:, None, None] * second
    flat_state = damped.reshape(stacked, columns)
    flat_cloud = cloud.reshape(levels, columns)
    peers = lax.axis_size("py")
    capacity = columns // 4 + 3 * columns // (4 * peers)
    positions = span_of.reshape(columns)
    target = positions // columns
    local_slot = positions % columns
    onehot = (target[:, None] == jnp.arange(peers, dtype=jnp.int32)[None, :]).astype(jnp.int32)
    pair_rank = jnp.sum((jnp.cumsum(onehot, axis=0) - onehot) * onehot, axis=1)
    send_slot = target * capacity + pair_rank
    slot_source = (
        jnp.full((peers * capacity,), columns, jnp.int32)
        .at[send_slot]
        .set(jnp.arange(columns, dtype=jnp.int32))
    )
    slot_live = slot_source < columns
    slot_clip = jnp.minimum(slot_source, columns - 1)
    slot_value = jnp.where(
        slot_live, jnp.take(local_slot, slot_clip).astype(jnp.float32), float(columns)
    )
    labels = slot_value.reshape(1, peers, capacity)
    exner_col = exner[:, None]
    scale_col = sat_scale[:, None]
    mass_col = layer_mass[:, None]
    theta_next, vapor_next, cloud_next, rainfall = adjust(
        flat_state[:levels],
        flat_state[levels : 2 * levels],
        flat_cloud,
        exner_col,
        scale_col,
        mass_col,
    )
    rain_send = jnp.where(slot_live, jnp.take(rainfall, slot_clip), 0.0).reshape(1, peers, capacity)
    rain_in, labels_in = (
        lax.all_to_all(rain_send, "py", split_axis=1, concat_axis=1, tiled=True),
        lax.all_to_all(labels, "py", split_axis=1, concat_axis=1, tiled=True),
    )
    span_index = labels_in.reshape(-1).astype(jnp.int32)
    arrived_at = (
        jnp.zeros((columns,), jnp.int32)
        .at[span_index]
        .set(jnp.arange(span_index.shape[0], dtype=jnp.int32), mode="drop")
    )
    precip_local = jnp.take(rain_in.reshape(-1), arrived_at)
    theta_out = theta_next.reshape(levels, row_count, across)
    vapor_out = vapor_next.reshape(levels, row_count, across)
    cloud_out = cloud_next.reshape(levels, row_count, across)
    divergence_next = damped[2 * levels :]
    return (theta_out, vapor_out, cloud_out, divergence_next, precip_local[None, :])


def solution(mesh):
    placed = (
        P(None, "px", "py"),
        P(None, "px", "py"),
        P(None, "px", "py"),
        P(None, "px", "py"),
        P(None, "px", "py"),
        P("px", "py"),
        P(),
        P(),
        P(),
        P(),
        P("px", "py"),
    )
    return jax.shard_map(
        on_device,
        mesh=mesh,
        in_specs=placed,
        out_specs=(
            P(None, "px", "py"),
            P(None, "px", "py"),
            P(None, "px", "py"),
            P(None, "px", "py"),
            P("px", "py"),
        ),
        check_vma=False,
    )
```

profile of v0, /device:TPU:0, one launch (start us, length us, event | category | flops | bytes accessed | tf_op | source)
XLA Modules:
  0.0 441.4 jit_solution(16138018173971515117)
XLA Ops:
  0.7 1.6 constant_dynamic-update-slice_fusion.7
  2.2 0.2 constant_dynamic-update-slice_fusion.6
  2.5 0.2 constant_dynamic-update-slice_fusion.5
  2.7 0.3 copy-done.14
  3.1 1.2 copy-done.6
  4.3 0.3 fusion.51
  4.6 0.7 copy.39
  5.3 0.7 copy.40
  5.9 3.0 collective-permute-start.1
  9.0 4.6 %reduce-window.6 = s32[16,32,128]{2,1,0:T(8,128)S(1)} reduce-window(s32[16,32,128]{2,1,0:T(8,128)S(1)} %fusion.37, s32[]{:T(128)} %constant.80.clone.1), window={size=1x1x128 pad=0_0x0_0x127_0}, to_apply=%region_0.1 | reduce-window | flops 8323072 | bytes 524292 | tf_op jit(solution)/shard_map/reduce-window
  13.6 0.5 slice_reduce_fusion
  14.0 0.2 reduce-window.9
  14.2 0.1 broadcast_add_fusion
  14.4 0.2 fusion.36
  14.6 0.1 compare_select_fusion.2
  14.8 15.5 %scatter_custom_fusion = s32[19456]{0:T(1024)S(1)} fusion(s32[4096]{0:T(1024)S(1)} %bitcast.51, s32[4096]{0:T(1024)S(1)} %iota.14, s32[]{:T(128)} %constant.81.clone.1), kind=kCustom, calls=%fused_computation.87 | custom fusion | bytes 77828 | tf_op jit(solution)/shard_map/scatter | solution.py:108
  30.4 107.4 %gather_fusion = s32[19456]{0:T(1024)S(1)} fusion(s32[4096]{0:T(1024)S(1)} %get-tuple-element.43, s32[19456]{0:T(1024)S(1)} %fusion.38), kind=kCustom, calls=%fused_computation | custom fusion | bytes 233472 | tf_op jit(solution)/shard_map/jit(_take)/gather | solution.py:113
  137.8 0.7 convert_select_fusion
  138.4 0.8 reshape.259
  139.2 8.1 %all-to-all-start = ((f32[1,16,1216]{2,0,1:T(1,128)}), f32[1,16,1216]{2,0,1:T(1,128)S(1)}, u32[]{:S(2)}, u32[]{:S(2)}) async-start(f32[1,16,1216]{2,0,1:T(1,128)} %reshape.259), calls=%async_computation | async-start | bytes 163840 | tf_op jit(solution)/shard_map/all_to_all | solution.py:130
  147.4 0.6 mul.200
  148.0 0.5 broadcast_multiply_fusion
  148.5 1.1 copy.41
  149.6 1.1 copy.42
  150.8 0.7 pad_maximum_fusion
  151.5 2.7 fusion.49
  154.2 2.5 copy.43
  156.8 2.0 collective-permute-start.2
  158.7 3.2 copy.44
  161.9 3.4 collective-permute-start.3
  165.3 0.2 convert_reduce_fusion
  165.6 0.1 convert_element_type.27
  165.7 3.1 copy.45
  168.8 3.1 copy.46
  171.8 1.1 maximum_bitcast_fusion.2
  172.9 0.6 copy-done
  173.5 0.7 copy-done.1
  174.5 1.5 copy-done.7
  176.0 11.8 %fusion.21 = f32[174,16,256]{2,1,0:T(8,128)S(1)} fusion(f32[174,16,256]{2,1,0:T(8,128)S(1)} %copy-done.7, f32[178,18,1]{2,1,0:T(8,128)S(1)} %copy-done, f32[178,1,256]{2,1,0:T(1,128)S(1)} %copy.42, f32[178,16,256]{2,1,0:T(8,128)S(1)} %constant_dynamic-update-slice_fusion.3, f32[178,1,256]{2,1,0:T(1,128)S(1)} %copy.41, f32[178,18,1]{2,1,0:T(8,128)S(1)} %copy-done.1, ...), kind=kLoop, calls=%fused_computation.39 | loop fusion | flops 22806528 | bytes 9122848 | tf_op jit(solution)/shard_map/mul | solution.py:46
  187.8 1.6 copy-done.2
  189.4 0.2 fusion.52
  189.7 0.5 collective-permute-start.5
  190.3 71.5 %scatter_custom_fusion.1 = s32[4096]{0:T(1024)S(1)} fusion(s32[19456]{0:T(1024)S(1)} %bitcast.44, s32[19456]{0:T(1024)S(1)} %iota.15, s32[]{:T(128)} %constant.80.clone.1), kind=kCustom, calls=%fused_computation.125 | custom fusion | bytes 16388 | tf_op jit(solution)/shard_map/scatter | solution.py:136
  261.8 0.2 copy.52
  262.0 0.2 copy.54
  262.2 2.5 pad_maximum_fusion.1
  264.7 2.0 fusion.50
  266.7 1.0 copy.57
  267.7 4.1 collective-permute-start.6
  271.8 2.7 copy.59
  274.5 0.3 collective-permute-start.7
  274.8 2.4 copy.58
  277.1 4.9 %collective-permute-done.7 = f32[174,18,1]{0,1,2:T(8,128)} collective-permute-done((f32[174,18,1]{0,1,2:T(8,128)S(1)}, f32[174,18,1]{0,1,2:T(8,128)}, u32[]{:S(2)}, u32[]{:S(2)}) %collective-permute-start.7) | collective-permute-done | bytes 12560 | tf_op jit(solution)/shard_map/ppermute | solution.py:21
  282.0 3.0 copy.60
  285.0 10.5 %fusion.5 = f32[174,16,256]{2,1,0:T(8,128)S(1)} fusion(f32[174,16,256]{2,1,0:T(8,128)} %copy-done.6, f32[174,16,256]{2,1,0:T(8,128)S(1)} %copy-done.3, f32[174,18,1]{2,1,0:T(8,128)} %copy.60, f32[174,1,256]{2,1,0:T(1,128)S(1)} %copy.52, f32[174,1,256]{2,1,0:T(1,128)S(1)} %copy.54, f32[174,18,1]{2,1,0:T(8,128)} %copy.58, f32[16,256]{1,0:T(8,128)S(1)} %get-tuple-element.41, ...), kind=kLoop, calls=%fused_computation.13 | loop fusion | flops 24231936 | bytes 9049240 | tf_op jit(solution)/shard_map/sub | solution.py:94
  295.6 2.4 multiply_reduce_fusion
  298.0 107.4 %gather_fusion.1 = f32[19456]{0:T(1024)S(1)} fusion(f32[4096]{0:T(1024)S(1)} %bitcast.40, s32[19456]{0:T(1024)S(1)} %fusion.38), kind=kCustom, calls=%fused_computation.1 | custom fusion | bytes 233472 | tf_op jit(solution)/shard_map/jit(_take)/gather | solution.py:127
  405.5 0.8 reshape.260
  406.2 3.5 all-to-all-start.1
  409.7 3.3 slice_subtract_fusion
  413.1 4.3 all-to-all-done.1
  417.4 0.2 reduce.3
  417.7 23.0 %gather_fusion.2 = f32[4096]{0:T(1024)S(1)} fusion(f32[19456]{0:T(1024)S(1)} %reshape.261, s32[4096]{0:T(1024)S(1)} %fusion.45), kind=kCustom, calls=%fused_computation.2 | custom fusion | bytes 49152 | tf_op jit(solution)/shard_map/jit(_take)/gather | solution.py:138
  440.8 0.6 and_select_fusion.1
  (70 shorter events, 0.8 us)
Async XLA Ops:
  0.6 1.6 copy-start.9
  0.6 1.9 copy-start.10
  2.2 0.8 copy-start.14
  2.2 2.1 copy-start.15
  2.5 6.4 %copy-start.11 = (s32[16,256]{1,0:T(8,128)S(1)}, s32[16,256]{1,0:T(8,128)}, u32[]{:S(2)}) copy-start(s32[16,256]{1,0:T(8,128)} %param.21) | copy-start | bytes 49156
  2.7 1.6 copy-start.6
  5.3 143.3 %collective-permute-start = (f32[178,1,256]{2,0,1:T(8,128)}, f32[178,1,256]{2,0,1:T(8,128)}, u32[]{:S(2)}, u32[]{:S(2)}) collective-permute-start(f32[178,1,256]{2,0,1:T(8,128)} %copy.39), channel_id=1, source_target_pairs={{0,16},{16,32},{32,48},{48,64},{64,80},{80,96},{96,112},{112,0},{1... | collective-permute-start | bytes 546824 | tf_op jit(solution)/shard_map/ppermute | solution.py:21
  5.9 143.7 %collective-permute-start.1 = (f32[178,1,256]{2,0,1:T(8,128)}, f32[178,1,256]{2,0,1:T(8,128)}, u32[]{:S(2)}, u32[]{:S(2)}) collective-permute-start(f32[178,1,256]{2,0,1:T(8,128)} %copy.40), channel_id=1, source_target_pairs={{16,0},{32,16},{48,32},{64,48},{80,64},{96,80},{112,96},{0,112},{1... | collective-permute-start | bytes 546824 | tf_op jit(solution)/shard_map/ppermute | solution.py:23
  30.3 117.0 %copy-start.17 = (f32[3,58]{1,0:T(4,128)S(1)}, f32[3,58]{1,0:T(4,128)}, u32[]{:S(2)}) copy-start(f32[3,58]{1,0:T(4,128)} %param.17) | copy-start | bytes 2092
  30.4 117.6 %copy-start.21 = (f32[58]{0:T(128)S(1)}, f32[58]{0:T(128)}, u32[]{:S(2)}) copy-start(f32[58]{0:T(128)} %param.20) | copy-start | bytes 700
  139.2 26.1 %all-to-all-start = ((f32[1,16,1216]{2,0,1:T(1,128)}), f32[1,16,1216]{2,0,1:T(1,128)S(1)}, u32[]{:S(2)}, u32[]{:S(2)}) async-start(f32[1,16,1216]{2,0,1:T(1,128)} %reshape.259), calls=%async_computation | async-start | bytes 163840 | tf_op jit(solution)/shard_map/all_to_all | solution.py:130
  156.8 8.9 %collective-permute-start.2 = (f32[178,18,1]{0,1,2:T(8,128)S(1)}, f32[178,18,1]{0,1,2:T(8,128)}, u32[]{:S(2)}, u32[]{:S(2)}) collective-permute-start(f32[178,18,1]{0,1,2:T(8,128)S(1)} %copy.43), channel_id=1, source_target_pairs={{0,1},{1,2},{2,3},{3,4},{4,5},{5,6},{6,7},{7,8},{8,9},{9,10},{10,1... | collective-permute-start | bytes 38456 | tf_op jit(solution)/shard_map/ppermute | solution.py:21
  161.9 6.9 %collective-permute-start.3 = (f32[178,18,1]{0,1,2:T(8,128)}, f32[178,18,1]{0,1,2:T(8,128)}, u32[]{:S(2)}, u32[]{:S(2)}) collective-permute-start(f32[178,18,1]{0,1,2:T(8,128)} %copy.44), channel_id=1, source_target_pairs={{1,0},{2,1},{3,2},{4,3},{5,4},{6,5},{7,6},{8,7},{9,8},{10,9},{11,1... | collective-permute-start | bytes 38456 | tf_op jit(solution)/shard_map/ppermute | solution.py:23
  171.8 1.7 copy-start
  171.8 2.4 copy-start.1
  174.2 1.8 copy-start.7
  187.8 1.6 copy-start.2
  189.6 72.2 %collective-permute-start.4 = (f32[174,1,256]{2,0,1:T(8,128)S(1)}, f32[174,1,256]{2,0,1:T(8,128)S(1)}, u32[]{:S(2)}, u32[]{:S(2)}) collective-permute-start(f32[174,1,256]{2,0,1:T(8,128)S(1)} %copy.51), channel_id=1, source_target_pairs={{16,0},{32,16},{48,32},{64,48},{80,64},{96,80},{112,96},{0,112},{1... | collective-permute-start | bytes 534536 | tf_op jit(solution)/shard_map/ppermute | solution.py:23
  189.7 72.3 %collective-permute-start.5 = (f32[174,1,256]{2,0,1:T(8,128)S(1)}, f32[174,1,256]{2,0,1:T(8,128)S(1)}, u32[]{:S(2)}, u32[]{:S(2)}) collective-permute-start(f32[174,1,256]{2,0,1:T(8,128)S(1)} %copy.53), channel_id=1, source_target_pairs={{0,16},{16,32},{32,48},{48,64},{64,80},{80,96},{96,112},{112,0},{1... | collective-permute-start | bytes 534536 | tf_op jit(solution)/shard_map/ppermute | solution.py:21
  267.7 7.1 %collective-permute-start.6 = (f32[174,18,1]{0,1,2:T(8,128)S(1)}, f32[174,18,1]{0,1,2:T(8,128)S(1)}, u32[]{:S(2)}, u32[]{:S(2)}) collective-permute-start(f32[174,18,1]{0,1,2:T(8,128)S(1)} %copy.57), channel_id=1, source_target_pairs={{1,0},{2,1},{3,2},{4,3},{5,4},{6,5},{7,6},{8,7},{9,8},{10,9},{11,1... | collective-permute-start | bytes 37592 | tf_op jit(solution)/shard_map/ppermute | solution.py:23
  271.8 13.2 %copy-start.3 = (f32[174,16,256]{2,1,0:T(8,128)S(1)}, f32[174,16,256]{2,1,0:T(8,128)}, u32[]{:S(2)}) copy-start(f32[174,16,256]{2,1,0:T(8,128)} %copy-done.2) | copy-start | bytes 8552452
  271.8 13.2 %copy-start.16 = (f32[174]{0:T(256)S(1)}, f32[174]{0:T(256)}, u32[]{:S(2)}) copy-start(f32[174]{0:T(256)} %mul.200) | copy-start | bytes 2092
  274.5 7.5 %collective-permute-start.7 = (f32[174,18,1]{0,1,2:T(8,128)S(1)}, f32[174,18,1]{0,1,2:T(8,128)}, u32[]{:S(2)}, u32[]{:S(2)}) collective-permute-start(f32[174,18,1]{0,1,2:T(8,128)S(1)} %copy.59), channel_id=1, source_target_pairs={{0,1},{1,2},{2,3},{3,4},{4,5},{5,6},{6,7},{7,8},{8,9},{9,10},{10,1... | collective-permute-start | bytes 37592 | tf_op jit(solution)/shard_map/ppermute | solution.py:21
  285.0 10.5 %copy-start.8 = (f32[58,16,256]{2,1,0:T(8,128)S(1)}, f32[58,16,256]{2,1,0:T(8,128)}, u32[]{:S(2)}) copy-start(f32[58,16,256]{2,1,0:T(8,128)} %param.13) | copy-start | bytes 2850820
  285.0 10.5 %copy-start.18 = (f32[58]{0:T(128)S(1)}, f32[58]{0:T(128)}, u32[]{:S(2)}) copy-start(f32[58]{0:T(128)} %param.18) | copy-start | bytes 700
  285.0 10.5 %copy-start.19 = (f32[58]{0:T(128)S(1)}, f32[58]{0:T(128)}, u32[]{:S(2)}) copy-start(f32[58]{0:T(128)} %param.19) | copy-start | bytes 700
  285.0 10.5 %copy-start.20 = (f32[58]{0:T(128)S(1)}, f32[58]{0:T(128)}, u32[]{:S(2)}) copy-start(f32[58]{0:T(128)} %broadcast_multiply_fusion) | copy-start | bytes 700
  295.6 2.4 copy-start.4
  298.0 107.5 %copy-start.12 = (pred[19456]{0:T(1024)(128)(4,1)S(1)}, pred[19456]{0:T(1024)(128)(4,1)}, u32[]{:S(2)}) copy-start(pred[19456]{0:T(1024)(128)(4,1)} %get-tuple-element.11) | copy-start | bytes 58372
  298.0 107.5 %copy-start.13 = (pred[19456]{0:T(1024)(128)(4,1)S(1)}, pred[19456]{0:T(1024)(128)(4,1)}, u32[]{:S(2)}) copy-start(pred[19456]{0:T(1024)(128)(4,1)} %get-tuple-element.12) | copy-start | bytes 58372
  298.0 111.7 %copy-start.5 = (f32[174,16,256]{2,1,0:T(8,128)S(1)}, f32[174,16,256]{2,1,0:T(8,128)}, u32[]{:S(2)}) copy-start(f32[174,16,256]{2,1,0:T(8,128)} %copy-done.4) | copy-start | bytes 8552452
  406.2 11.2 %all-to-all-start.1 = ((f32[1,16,1216]{2,0,1:T(1,128)}), f32[1,16,1216]{2,0,1:T(1,128)S(1)}, u32[]{:S(2)}, u32[]{:S(2)}) async-start(f32[1,16,1216]{2,0,1:T(1,128)} %reshape.260), calls=%async_computation.1 | async-start | bytes 163840 | tf_op jit(solution)/shard_map/all_to_all | solution.py:129
where the time goes:
time: 442 us; the launch traced here: 441 us
  local copies, waits for them, and re-layouts  366 us (83%)
  other arithmetic  40 us (9%)
  starting transfers between devices  24.8 us (6%)
  waiting for transfers between devices  9.23 us (2%)
    gather x1, local copies, waits for them, and re-layouts, on_device(): jnp.take(local_slot, slot_clip).astype(jnp.float32)  107 us
    gather x1, local copies, waits for them, and re-layouts, on_device(): jnp.take(rainfall, slot_clip)  107 us
    scatter x1, local copies, waits for them, and re-layouts, on_device(): arrived_at = jnp.zeros((columns,), jnp.int32).at[span_index].set(jnp.aran...  71.5 us
    gather x1, local copies, waits for them, and re-layouts, on_device(): precip_local = jnp.take(rain_in.reshape(-1), arrived_at)  23 us
    scatter x1, local copies, waits for them, and re-layouts, on_device(): slot_source = jnp.full((peers * capacity,), columns, jnp.int32).at[send_s...  15.5 us
    mul x1, other arithmetic, laplace(): return shifted(inverse, 0, 0) * summed  11.8 us
    sub x1, other arithmetic, on_device(): damped = fields - damping.reshape(stacked)[:, None, None] * second  10.5 us
    ppermute x4, starting transfers between devices, extended(): lax.ppermute(head, axis, [((i + 1) % count, i) for i in range(count)])  10.5 us
  transfers between devices with their start and end apart: 10, of which 2 were waited for; matrix products, arithmetic and copies ran while one was open for 51% of the time, Pallas kernels for 0%

commit v1 on v0

v1 whole, which is shorter than its diff:
```python
import functools

import jax
import jax.numpy as jnp
from jax import lax
from jax.experimental import pallas as pl
from jax.experimental.pallas import tpu as pltpu
from jax.sharding import PartitionSpec as P

LATENT = 0.5
QCRIT = 0.2
AUTO_RATE = 0.5

LANES = 128
BLOCK_LEVELS = 15


def pack_kernel(theta_ref, vapor_ref, div_ref, edge_ref, inv_ref, top_ref, bot_ref, left_ref, right_ref):
    levels = theta_ref.shape[0] // 16
    total = 3 * levels + 4
    fields = (theta_ref, vapor_ref, div_ref)
    for out_ref, first in ((top_ref, 0), (bot_ref, 14)):
        for row in range(2):
            for g in range(3):
                out_ref[pl.ds(row * total + 3 * levels + g, 1), :] = edge_ref[
                    pl.ds(16 * g + first + row, 1), :
                ]
            out_ref[pl.ds(row * total + 3 * levels + 3, 1), :] = inv_ref[pl.ds(first + row, 1), :]
    lane = lax.broadcasted_iota(jnp.int32, (16, LANES), 1)

    def place(acc, value, slot, side):
        shift = 2 * slot if side == 0 else 2 * slot + 2
        moved = pltpu.roll(value, lax.rem(shift, LANES), 1)
        return jnp.where((lane >> 1) == slot, moved, acc)

    def body(l, accs):
        out = []
        for field, ref in enumerate(fields):
            base = pl.multiple_of(l * 16, 16)
            for row in range(2):
                at = pl.ds(row * total + field * levels + l, 1)
                top_ref[at, :] = ref[pl.ds(base + row, 1), :]
                bot_ref[at, :] = ref[pl.ds(base + 14 + row, 1), :]
            for side in range(2):
                value = ref[pl.ds(base, 16), side * LANES : (side + 1) * LANES]
                out.append(place(accs[2 * field + side], value, l, side))
        return tuple(out)

    zero = jnp.zeros((16, LANES), jnp.float32)
    accs = list(lax.fori_loop(0, levels, body, (zero,) * 6))
    for g in range(4):
        for side in range(2):
            cols = slice(side * LANES, (side + 1) * LANES)
            value = edge_ref[16 * g : 16 * g + 16, cols] if g < 3 else inv_ref[:, cols]
            accs[side] = place(accs[side], value, jnp.int32(levels + g), side)
    for field in range(3):
        left_ref[:, field * LANES : (field + 1) * LANES] = accs[2 * field]
        right_ref[:, field * LANES : (field + 1) * LANES] = accs[2 * field + 1]


def pack(theta, vapor, divergence, edge, inv):
    levels = theta.shape[0] // 16
    total = 3 * levels + 4
    rows = jax.ShapeDtypeStruct((2 * total, 256), jnp.float32)
    cols = jax.ShapeDtypeStruct((16, 3 * LANES), jnp.float32)
    return pl.pallas_call(
        pack_kernel,
        out_shape=(rows, rows, cols, cols),
        name="pack",
    )(theta, vapor, divergence, edge, inv)


def up(v):
    return pltpu.roll(v, v.shape[0] - 1, 0)


def down(v):
    return pltpu.roll(v, 1, 0)


def ahead(v):
    return pltpu.roll(v, v.shape[1] - 1, 1)


def behind(v):
    return pltpu.roll(v, 1, 1)


def main_kernel(
    peers,
    levels,
    params_ref,
    theta_ref,
    vapor_ref,
    cloud_ref,
    div_ref,
    edge_ref,
    inv_ref,
    span_ref,
    below_ref,
    above_ref,
    colr_ref,
    coll_ref,
    corner_below_ref,
    corner_above_ref,
    theta_out,
    vapor_out,
    cloud_out,
    div_out,
    send_out,
    coef_ref,
    rain_ref,
    hi_ref,
    lo_ref,
):
    total = 3 * levels + 4
    step = pl.program_id(0)
    steps = pl.num_programs(0)

    lane = lax.broadcasted_iota(jnp.int32, (8, LANES), 1)
    sub = lax.broadcasted_iota(jnp.int32, (8, 256), 0)
    sub_c = lax.broadcasted_iota(jnp.int32, (8, LANES), 0)
    lane16 = lax.broadcasted_iota(jnp.int32, (16, LANES), 1)

    def side_tile(field, slot):
        cols = slice(field * LANES, (field + 1) * LANES)
        to_right = lax.rem(LANES - 2 * slot, LANES)
        to_left = lax.rem(2 * LANES - 2 - 2 * slot, LANES)
        right = pltpu.roll(colr_ref[:, cols], to_right, 1)
        left = pltpu.roll(coll_ref[:, cols], to_left, 1)
        tile = jnp.where(lane16 < 64, right, left)
        wide = slice((3 + field) * LANES, (4 + field) * LANES)
        corner_r = jnp.where(sub_c < 4, corner_below_ref[:, cols], corner_above_ref[:, cols])
        corner_l = jnp.where(sub_c < 4, corner_below_ref[:, wide], corner_above_ref[:, wide])
        corner = jnp.where(
            lane < 64, pltpu.roll(corner_r, to_right, 1), pltpu.roll(corner_l, to_left, 1)
        )
        return tile, corner

    def row_tile(index):
        def row(ref, r):
            return jnp.broadcast_to(ref[pl.ds(r * total + index, 1), :], (8, 256))

        low = jnp.where(sub < 1, row(below_ref, 0), row(below_ref, 1))
        high = jnp.where(sub < 7, row(above_ref, 0), row(above_ref, 1))
        return jnp.where(sub < 4, low, high)

    def extend(centre, index, field, slot):
        tile, corner = side_tile(field, slot)
        upper = jnp.concatenate([centre, tile], axis=1)
        lower = jnp.concatenate([row_tile(index), corner], axis=1)
        return jnp.concatenate([upper, lower], axis=0)

    @pl.when(step == 0)
    def _():
        geo = []
        for g in range(4):
            centre = edge_ref[16 * g : 16 * g + 16, :] if g < 3 else inv_ref[...]
            geo.append(extend(centre, 3 * levels + g, 0, jnp.int32(levels + g)))
        w0, w1, w2, inv = geo
        c1 = inv * w0
        c2 = inv * down(w0)
        c3 = inv * w1
        c4 = inv * behind(w1)
        c5 = inv * w2
        c6 = inv * behind(up(w2))
        coef_ref[0] = c1 + c2 + c3 + c4 + c5 + c6
        coef_ref[1] = c1
        coef_ref[2] = c2
        coef_ref[3] = behind(c3)
        coef_ref[4] = ahead(c4)
        coef_ref[5] = behind(c5)
        coef_ref[6] = ahead(c6)
        rain_ref[...] = jnp.zeros_like(rain_ref)

    def lap(v, high, wide):
        v_up = up(v)[:high]
        v_dn = down(v)[:high]
        v = v[:high]
        a = coef_ref[3, :high] * v + coef_ref[5, :high] * v_dn
        b = coef_ref[4, :high] * v + coef_ref[6, :high] * v_up
        a = ahead(a)[:, :wide]
        b = behind(b)[:, :wide]
        c = (
            coef_ref[1, :high, :wide] * v_up[:, :wide]
            + coef_ref[2, :high, :wide] * v_dn[:, :wide]
            - coef_ref[0, :high, :wide] * v[:, :wide]
        )
        return (a + b) + c

    def damp(centre, field, l):
        first = lap(extend(centre, field * levels + l, field, l), 24, 384)
        second = lap(first, 16, 256)
        return centre - params_ref[field * levels + l] * second

    def body(k, carry):
        l = step * BLOCK_LEVELS + k
        div_out[k] = damp(div_ref[k], 2, l)
        theta = damp(theta_ref[k], 0, l)
        vapor = damp(vapor_ref[k], 1, l)
        exner = params_ref[3 * levels + l]
        scale = params_ref[4 * levels + l]
        mass = params_ref[5 * levels + l]
        cloud = cloud_ref[k]
        temper = theta * exner
        saturation = scale * jnp.exp(temper)
        condensed = (vapor - saturation) / (1.0 + LATENT * saturation)
        saturation = scale * jnp.exp(temper + LATENT * condensed)
        condensed = condensed + (vapor - condensed - saturation) / (1.0 + LATENT * saturation)
        condensed = jnp.maximum(condensed, -cloud)
        ratio = jnp.full((1, 256), LATENT, jnp.float32) / jnp.full((1, 256), exner, jnp.float32)
        theta_out[k] = theta + condensed * ratio
        vapor_out[k] = vapor - condensed
        liquid = cloud + condensed
        rained = AUTO_RATE * jnp.maximum(liquid - QCRIT, 0.0)
        cloud_out[k] = liquid - rained
        rain_ref[...] += mass * rained
        return carry

    lax.fori_loop(0, jnp.minimum(BLOCK_LEVELS, levels - step * BLOCK_LEVELS), body, 0)

    @pl.when(step == steps - 1)
    def _():
        tall = lax.broadcasted_iota(jnp.int32, (peers * 32, 256), 0)
        short = lax.broadcasted_iota(jnp.int32, (LANES, 256), 0)
        for r in range(16):
            span = span_ref[r : r + 1, :]
            value = rain_ref[r : r + 1, :]
            coarse = value.astype(jnp.bfloat16).astype(jnp.float32)
            fine = value - coarse
            cols = slice(r * 256, (r + 1) * 256)
            hi_ref[:, cols] = jnp.where(tall == (span >> 7), 1.0, 0.0).astype(jnp.bfloat16)
            here = short == (span & 127)
            lo_ref[:LANES, cols] = jnp.where(here, coarse, 0.0).astype(jnp.bfloat16)
            lo_ref[LANES:, cols] = jnp.where(here, fine, 0.0).astype(jnp.bfloat16)
        placed = lax.dot_general(
            hi_ref[...], lo_ref[...], (((1,), (1,)), ((), ())), preferred_element_type=jnp.float32
        )
        send_out[...] = placed[:, :LANES] + placed[:, LANES:]


def physics(peers, params, theta, vapor, cloud, divergence, edge, inv, span, halos):
    levels = theta.shape[0]
    steps = pl.cdiv(levels, BLOCK_LEVELS)
    block = pl.BlockSpec((BLOCK_LEVELS, 16, 256), lambda s: (s, 0, 0))
    whole = lambda a: pl.BlockSpec(a.shape, lambda s: (0,) * a.ndim)
    field = jax.ShapeDtypeStruct(theta.shape, jnp.float32)
    sent = jax.ShapeDtypeStruct((peers * 32, LANES), jnp.float32)
    return pl.pallas_call(
        functools.partial(main_kernel, peers, levels),
        grid=(steps,),
        in_specs=[pl.BlockSpec(memory_space=pltpu.SMEM), block, block, block, block]
        + [whole(a) for a in (edge, inv, span) + halos],
        out_specs=[block, block, block, block, whole(sent)],
        out_shape=[field, field, field, field, sent],
        scratch_shapes=[
            pltpu.VMEM((7, 24, 384), jnp.float32),
            pltpu.VMEM((16, 256), jnp.float32),
            pltpu.VMEM((peers * 32, 4096), jnp.bfloat16),
            pltpu.VMEM((2 * LANES, 4096), jnp.bfloat16),
        ],
        name="physics",
    )(params, theta, vapor, cloud, divergence, edge, inv, span, *halos)


def on_device(
    theta,
    vapor,
    cloud,
    divergence,
    edge_weight,
    inv_area,
    damping,
    exner,
    sat_scale,
    layer_mass,
    span_of,
):
    levels = theta.shape[0]
    n_px = lax.axis_size("px")
    peers = lax.axis_size("py")

    def from_next(x, axis, count):
        return lax.ppermute(x, axis, [((i + 1) % count, i) for i in range(count)])

    def from_prev(x, axis, count):
        return lax.ppermute(x, axis, [(i, (i + 1) % count) for i in range(count)])

    flat = lambda x: x.reshape(-1, 256)
    edge = flat(edge_weight)
    top, bot, left, right = pack(flat(theta), flat(vapor), flat(divergence), edge, inv_area)
    colr = from_next(left, "py", peers)
    coll = from_prev(right, "py", peers)
    below = from_next(top, "px", n_px)
    above = from_prev(bot, "px", n_px)
    sides = jnp.concatenate([colr, coll], axis=1)
    corner_below = from_next(sides[:8], "px", n_px)
    corner_above = from_prev(sides[8:], "px", n_px)
    params = jnp.concatenate([damping.reshape(-1), exner, sat_scale, layer_mass])
    theta_next, vapor_next, cloud_next, divergence_next, send = physics(
        peers,
        params,
        theta,
        vapor,
        cloud,
        divergence,
        edge,
        inv_area,
        span_of,
        (below, above, colr, coll, corner_below, corner_above),
    )
    got = lax.all_to_all(send.reshape(peers, 32, LANES), "py", split_axis=0, concat_axis=0, tiled=True)
    precip = jnp.sum(got, axis=0).reshape(1, 4096)
    return (theta_next, vapor_next, cloud_next, divergence_next, precip)


def solution(mesh):
    field = P(None, "px", "py")
    plane = P("px", "py")
    return jax.shard_map(
        on_device,
        mesh=mesh,
        in_specs=(field, field, field, field, field, plane, P(), P(), P(), P(), plane),
        out_specs=(field, field, field, field, plane),
        check_vma=False,
    )
```

time: 442 us -> 67.8 us (0.15)
  local copies, waits for them, and re-layouts: 366 us -> 2.77 us
  other arithmetic: 40 us -> 1.28 us
  Pallas kernels: 0 us -> 32.5 us
  starting transfers between devices: 24.8 us -> 11.5 us
  blocking collectives: 0 us -> 13.2 us
    gather x3 -> x0, local copies, waits for them, and re-layouts: 238 us -> none  [the longest x1 107 us: on_device(): jnp.take(local_slot, slot_clip).astype(jnp.float32)]
    scatter x2 -> x0, local copies, waits for them, and re-layouts: 87.1 us -> none  [the longest x1 71.5 us: on_device(): arrived_at = jnp.zeros((columns,), jnp.int32).at[span_index].set(jnp.aran...]
    pallas_call x0 -> x2, Pallas kernels: none -> 32.5 us  [the longest x1 24.4 us: physics(): pl.pallas_call(functools.partial(main_kernel, peers, levels), grid=(steps...]
    slice x16 -> x1, local copies, waits for them, and re-layouts: 16.7 us -> 0.01 us  [on_device(): corner_above = from_prev(sides[8:], 'px', n_px)]
    ppermute x8 -> x0, local copies, waits for them, and re-layouts: 14.1 us -> none  [the longest x4 7.37 us: extended(): lax.ppermute(tail, axis, [(i, (i + 1) % count) for i in range(count)])]
    sub x2 -> x0, other arithmetic: 13.8 us -> none  [the longest x1 10.5 us: on_device(): damped = fields - damping.reshape(stacked)[:, None, None] * second]
    all_to_all x0 -> x1, blocking collectives: none -> 13.2 us  [on_device(): lax.all_to_all(send.reshape(peers, 32, LANES), 'py', split_axis=0, concat...]
    mul x2 -> x0, other arithmetic: 12.3 us -> none  [the longest x1 11.8 us: laplace(): return shifted(inverse, 0, 0) * summed]
  transfers between devices with their start and end apart: 10 -> 6, of which waited for: 2 -> 2; matrix products, arithmetic and copies ran while one was open for 51% -> 1% of each run, Pallas kernels for 0% -> 0%
where the time goes in v1:
time: 67.8 us; the launch traced here: 67.5 us
  Pallas kernels  32.5 us (48%)
  blocking collectives  13.2 us (19%)
  starting transfers between devices  11.5 us (17%)
  waiting for transfers between devices  5.6 us (8%)
  local copies, waits for them, and re-layouts  2.77 us (4%)
  other arithmetic  1.28 us (2%)
  between operations  0.68 us (1%)
    pallas_call x1, Pallas kernels, physics(): pl.pallas_call(functools.partial(main_kernel, peers, levels), grid=(steps...  24.4 us
    all_to_all x1, blocking collectives, on_device(): lax.all_to_all(send.reshape(peers, 32, LANES), 'py', split_axis=0, concat...  13.2 us
    ppermute x3, starting transfers between devices, from_next(): return lax.ppermute(x, axis, [((i + 1) % count, i) for i in range(count)])  11.4 us
    pallas_call x1, Pallas kernels, pack(): pl.pallas_call(pack_kernel, out_shape=(rows, rows, cols, cols), name='pack')  8.14 us
    ppermute x3, waiting for transfers between devices, from_prev(): return lax.ppermute(x, axis, [(i, (i + 1) % count) for i in range(count)])  5.59 us
    unnamed x21, local copies, waits for them, and re-layouts  2.68 us
  transfers between devices with their start and end apart: 6, of which 2 were waited for; matrix products, arithmetic and copies ran while one was open for 1% of the time, Pallas kernels for 0%

profile of v1, /device:TPU:0, one launch (start us, length us, event | category | flops | bytes accessed | tf_op | source)
XLA Modules:
  0.0 67.5 jit_solution(10937164178992870910)
XLA Ops:
  0.6 8.1 %pack.1 = (f32[356,256]{1,0:T(8,128)}, f32[356,256]{1,0:T(8,128)}, f32[16,384]{1,0:T(8,128)}, f32[16,384]{1,0:T(8,128)}) custom-call(f32[928,256]{1,0:T(8,128)} %bitcast.6, f32[928,256]{1,0:T(8,128)} %bitcast.7, f32[928,256]{1,0:T(8,128)} %bitcast.8, f32[48,256]{1,0:T(8,128)} %bitcast.10, f32[16,256]{1,0:T(8,128)} %inv_ref.3), custom_call_target="tpu_custom_call" | custom-call | tf_op jit(solution)/shard_map/pack/pallas_call | solution.py:66
  8.8 6.6 %collective-permute-start.2 = (f32[16,384]{1,0:T(8,128)}, f32[16,384]{1,0:T(8,128)S(1)}, u32[]{:S(2)}, u32[]{:S(2)}) collective-permute-start(f32[16,384]{1,0:T(8,128)} %get-tuple-element.16), channel_id=1, source_target_pairs={{1,0},{2,1},{3,2},{4,3},{5,4},{6,5},{7,6},{8,7},{9,8},{10,9},{11,1... | collective-permute-start | bytes 73736 | tf_op jit(solution)/shard_map/ppermute | solution.py:284
  15.3 0.0 copy-start.6
  15.3 0.0 collective-permute-start.3
  15.4 1.9 %collective-permute-start = (f32[356,256]{1,0:T(8,128)}, f32[356,256]{1,0:T(8,128)S(1)}, u32[]{:S(2)}, u32[]{:S(2)}) collective-permute-start(f32[356,256]{1,0:T(8,128)} %get-tuple-element.14), channel_id=1, source_target_pairs={{16,0},{32,16},{48,32},{64,48},{80,64},{96,80},{112,96},{0,112},{1... | collective-permute-start | bytes 1093640 | tf_op jit(solution)/shard_map/ppermute | solution.py:284
  17.3 0.0 collective-permute-start.1
  17.3 0.0 copy-done.6
  17.3 0.1 reshape.31
  17.4 0.0 collective-permute-done.2.colr_ref
  17.4 0.0 copy-start.2
  17.4 0.6 copy-done.2
  18.0 4.7 %collective-permute-done.3.coll_ref = f32[16,384]{1,0:T(8,128)S(1)} collective-permute-done((f32[16,384]{1,0:T(8,128)}, f32[16,384]{1,0:T(8,128)S(1)}, u32[]{:S(2)}, u32[]{:S(2)}) %collective-permute-start.3) | collective-permute-done | bytes 24608 | tf_op jit(solution)/shard_map/ppermute | solution.py:287
  22.7 0.0 copy-start.3
  22.7 0.6 copy-done.3
  23.3 0.0 copy-start.7
  23.3 0.0 copy-start.8
  23.3 0.0 copy-start.9
  23.3 0.0 collective-permute-start.5
  23.4 2.9 %collective-permute-start.4 = (f32[8,768]{1,0:T(8,128)S(1)}, f32[8,768]{1,0:T(8,128)S(1)}, u32[]{:S(2)}, u32[]{:S(2)}) collective-permute-start(f32[8,768]{1,0:T(8,128)S(1)} %get-tuple-element.24), channel_id=1, source_target_pairs={{16,0},{32,16},{48,32},{64,48},{80,64},{96,80},{112,96},{0,112},{1... | collective-permute-start | bytes 73736 | tf_op jit(solution)/shard_map/ppermute | solution.py:284
  26.3 0.0 copy-done.7
  26.3 0.0 copy-done.8
  26.3 0.0 copy-done.9
  26.3 0.7 pad_maximum_fusion.params_ref
  27.0 0.8 %collective-permute-done.5.corner_above_ref = f32[8,768]{1,0:T(8,128)S(1)} collective-permute-done((f32[8,768]{1,0:T(8,128)S(1)}, f32[8,768]{1,0:T(8,128)S(1)}, u32[]{:S(2)}, u32[]{:S(2)}) %collective-permute-start.5) | collective-permute-done | bytes 24608 | tf_op jit(solution)/shard_map/ppermute | solution.py:287
  27.8 0.0 copy-start.4
  27.8 0.0 collective-permute-done.4.corner_below_ref
  27.8 0.0 copy-start.5
  27.8 0.0 collective-permute-done.below_ref
  27.8 0.0 copy-start
  27.8 0.0 collective-permute-done.1.above_ref
  27.8 0.6 copy-done.4
  28.4 0.0 copy-done.5
  28.4 0.1 copy-done
  28.6 0.0 copy-start.1
  28.6 0.7 %copy-done.1 = f32[356,256]{1,0:T(8,128)} copy-done((f32[356,256]{1,0:T(8,128)}, f32[356,256]{1,0:T(8,128)S(1)}, u32[]{:S(2)}) %copy-start.1) | copy-done | bytes 364568
  29.3 24.4 %physics.1 = (f32[58,16,256]{2,1,0:T(8,128)}, f32[58,16,256]{2,1,0:T(8,128)}, f32[58,16,256]{2,1,0:T(8,128)}, f32[58,16,256]{2,1,0:T(8,128)}, f32[512,128]{1,0:T(8,128)}) custom-call(f32[348]{0:T(512)} %pad_maximum_fusion.params_ref, f32[58,16,256]{2,1,0:T(8,128)} %theta_ref.1, f32[58,16,256]{2,1,0:T(8,128)} %vapor_ref.1, f32[58,16,256]{2,1,0:T(8,128)} %cloud_ref.1, ...), custom_call_target="tpu_custom_call" | custom-call | tf_op jit(solution)/shard_map/physics/pallas_call | solution.py:249
  53.7 13.2 %all_to_all.5 = f32[16,32,128]{2,1,0:T(8,128)S(1)} all-to-all(f32[16,32,128]{2,1,0:T(8,128)} %bitcast.9), channel_id=1, replica_groups=mesh['px'=8,'py'=16] {'py'}, dimensions={0} | all-to-all | bytes 524288 | tf_op jit(solution)/shard_map/all_to_all | solution.py:312
  66.9 0.6 reduce_sum.9
  (3 shorter events, 0.0 us)
Async XLA Ops:
  8.8 8.6 %collective-permute-start.2 = (f32[16,384]{1,0:T(8,128)}, f32[16,384]{1,0:T(8,128)S(1)}, u32[]{:S(2)}, u32[]{:S(2)}) collective-permute-start(f32[16,384]{1,0:T(8,128)} %get-tuple-element.16), channel_id=1, source_target_pairs={{1,0},{2,1},{3,2},{4,3},{5,4},{6,5},{7,6},{8,7},{9,8},{10,9},{11,1... | collective-permute-start | bytes 73736 | tf_op jit(solution)/shard_map/ppermute | solution.py:284
  15.3 1.9 %copy-start.6 = (f32[3,58]{1,0:T(4,128)S(1)}, f32[3,58]{1,0:T(4,128)}, u32[]{:S(2)}) copy-start(f32[3,58]{1,0:T(4,128)} %param.17) | copy-start | bytes 2092
  15.3 7.4 %collective-permute-start.3 = (f32[16,384]{1,0:T(8,128)}, f32[16,384]{1,0:T(8,128)S(1)}, u32[]{:S(2)}, u32[]{:S(2)}) collective-permute-start(f32[16,384]{1,0:T(8,128)} %get-tuple-element.17), channel_id=1, source_target_pairs={{0,1},{1,2},{2,3},{3,4},{4,5},{5,6},{6,7},{7,8},{8,9},{9,10},{10,1... | collective-permute-start | bytes 73736 | tf_op jit(solution)/shard_map/ppermute | solution.py:287
  15.4 12.5 %collective-permute-start = (f32[356,256]{1,0:T(8,128)}, f32[356,256]{1,0:T(8,128)S(1)}, u32[]{:S(2)}, u32[]{:S(2)}) collective-permute-start(f32[356,256]{1,0:T(8,128)} %get-tuple-element.14), channel_id=1, source_target_pairs={{16,0},{32,16},{48,32},{64,48},{80,64},{96,80},{112,96},{0,112},{1... | collective-permute-start | bytes 1093640 | tf_op jit(solution)/shard_map/ppermute | solution.py:284
  17.3 10.6 %collective-permute-start.1 = (f32[356,256]{1,0:T(8,128)}, f32[356,256]{1,0:T(8,128)S(1)}, u32[]{:S(2)}, u32[]{:S(2)}) collective-permute-start(f32[356,256]{1,0:T(8,128)} %get-tuple-element.15), channel_id=1, source_target_pairs={{0,16},{16,32},{32,48},{48,64},{64,80},{80,96},{96,112},{112,0},{1... | collective-permute-start | bytes 1093640 | tf_op jit(solution)/shard_map/ppermute | solution.py:287
  17.4 0.6 copy-start.2
  22.7 0.6 copy-start.3
  23.3 3.0 %copy-start.7 = (f32[58]{0:T(128)S(1)}, f32[58]{0:T(128)}, u32[]{:S(2)}) copy-start(f32[58]{0:T(128)} %param.20) | copy-start | bytes 700
  23.3 3.0 %copy-start.8 = (f32[58]{0:T(128)S(1)}, f32[58]{0:T(128)}, u32[]{:S(2)}) copy-start(f32[58]{0:T(128)} %param.19) | copy-start | bytes 700
  23.3 3.0 %copy-start.9 = (f32[58]{0:T(128)S(1)}, f32[58]{0:T(128)}, u32[]{:S(2)}) copy-start(f32[58]{0:T(128)} %param.18) | copy-start | bytes 700
  23.3 4.5 %collective-permute-start.5 = (f32[8,768]{1,0:T(8,128)S(1)}, f32[8,768]{1,0:T(8,128)S(1)}, u32[]{:S(2)}, u32[]{:S(2)}) collective-permute-start(f32[8,768]{1,0:T(8,128)S(1)} %get-tuple-element.23), channel_id=1, source_target_pairs={{0,16},{16,32},{32,48},{48,64},{64,80},{80,96},{96,112},{112,0},{1... | collective-permute-start | bytes 73736 | tf_op jit(solution)/shard_map/ppermute | solution.py:287
  23.4 4.5 %collective-permute-start.4 = (f32[8,768]{1,0:T(8,128)S(1)}, f32[8,768]{1,0:T(8,128)S(1)}, u32[]{:S(2)}, u32[]{:S(2)}) collective-permute-start(f32[8,768]{1,0:T(8,128)S(1)} %get-tuple-element.24), channel_id=1, source_target_pairs={{16,0},{32,16},{48,32},{64,48},{80,64},{96,80},{112,96},{0,112},{1... | collective-permute-start | bytes 73736 | tf_op jit(solution)/shard_map/ppermute | solution.py:284
  27.8 0.6 copy-start.4
  27.8 0.6 copy-start.5
  27.8 0.7 %copy-start = (f32[356,256]{1,0:T(8,128)}, f32[356,256]{1,0:T(8,128)S(1)}, u32[]{:S(2)}) copy-start(f32[356,256]{1,0:T(8,128)S(1)} %collective-permute-done.below_ref) | copy-start | bytes 1093636
  28.6 0.7 %copy-start.1 = (f32[356,256]{1,0:T(8,128)}, f32[356,256]{1,0:T(8,128)S(1)}, u32[]{:S(2)}) copy-start(f32[356,256]{1,0:T(8,128)S(1)} %collective-permute-done.1.above_ref) | copy-start | bytes 1093636

commit v2 on v1

v2 whole, which is shorter than its diff:
```python
import functools

import jax
import jax.numpy as jnp
from jax import lax
from jax.experimental import pallas as pl
from jax.experimental.pallas import tpu as pltpu
from jax.sharding import PartitionSpec as P

LATENT = 0.5
QCRIT = 0.2
AUTO_RATE = 0.5

LANES = 128
BLOCK_LEVELS = 16
UNROLL = 2


def pack_kernel(
    theta0, theta1, vapor0, vapor1, div0, div1, edge_ref, inv_ref,
    top_ref, bot_ref, left_ref, right_ref, left_low, left_high, right_low, right_high,
):
    levels = theta0.shape[0] // 16
    total = 3 * levels + 4
    fields = ((theta0, theta1), (vapor0, vapor1), (div0, div1))
    for out_ref, first in ((top_ref, 0), (bot_ref, 14)):
        for row in range(2):
            for field, halves in enumerate(fields):
                at = pl.ds(row * total + field * levels, levels)
                for half, ref in enumerate(halves):
                    cols = slice(half * LANES, (half + 1) * LANES)
                    out_ref[at, cols] = ref[pl.ds(first + row, levels, stride=16), :]
            for g in range(3):
                out_ref[pl.ds(row * total + 3 * levels + g, 1), :] = edge_ref[
                    pl.ds(16 * g + first + row, 1), :
                ]
            out_ref[pl.ds(row * total + 3 * levels + 3, 1), :] = inv_ref[pl.ds(first + row, 1), :]
    pair = lax.broadcasted_iota(jnp.int32, (16, LANES), 1) >> 1
    low_base = 2 * total + 4

    def place(acc, value, slot, side):
        moved = pltpu.roll(value, (2 * slot + 2 * side) % LANES, 1)
        return jnp.where(pair == slot, moved, acc)

    for field, halves in enumerate(fields):
        for side in range(2):
            acc = jnp.zeros((16, LANES), jnp.float32)
            for l in range(levels):
                acc = place(acc, halves[side][16 * l : 16 * l + 16, :], l, side)
            if field == 0:
                cols = slice(side * LANES, (side + 1) * LANES)
                for g in range(4):
                    value = edge_ref[16 * g : 16 * g + 16, cols] if g < 3 else inv_ref[:, cols]
                    acc = place(acc, value, levels + g, side)
            cols = slice(field * LANES, (field + 1) * LANES)
            whole, low, high = (
                (left_ref, left_low, left_high) if side == 0 else (right_ref, right_low, right_high)
            )
            whole[:, cols] = acc
            low[:, cols] = acc[:8]
            high[:, cols] = acc[8:]
            slot = 3 * side + field
            rows = pl.ds(low_base + 8 * (slot // 2), 8)
            cols = slice((slot % 2) * LANES, (slot % 2 + 1) * LANES)
            top_ref[rows, cols] = acc[:8]
            bot_ref[rows, cols] = acc[8:]


def pack(theta, vapor, divergence, edge, inv):
    levels = theta.shape[0] // 16
    total = 3 * levels + 4
    rows = jax.ShapeDtypeStruct((2 * total + 28, 256), jnp.float32)
    cols = jax.ShapeDtypeStruct((16, 3 * LANES), jnp.float32)
    half = jax.ShapeDtypeStruct((8, 3 * LANES), jnp.float32)
    sides = [pl.BlockSpec((16 * levels, LANES), lambda s, c=c: (0, c)) for c in range(2)]
    whole = lambda a: pl.BlockSpec(a.shape, lambda s: (0,) * len(a.shape))
    outs = (rows, rows, cols, cols, half, half, half, half)
    return pl.pallas_call(
        pack_kernel,
        grid=(1,),
        in_specs=sides * 3 + [whole(edge), whole(inv)],
        out_specs=[whole(o) for o in outs],
        out_shape=outs,
        name="pack",
    )(theta, theta, vapor, vapor, divergence, divergence, edge, inv)


def onehot_kernel(high, span_ref, out_ref):
    def count(rows, shift):
        index = lax.broadcasted_iota(jnp.int32, (rows, 256), 0) - shift
        return index.astype(jnp.float32).astype(jnp.bfloat16)

    tall = count(high, high // 2)
    short = count(LANES, 0)
    one = jnp.bfloat16(1.0)
    zero = jnp.bfloat16(0.0)
    for r in range(span_ref.shape[0]):
        span = span_ref[r : r + 1, :]
        hi = ((span >> 7) - high // 2).astype(jnp.float32).astype(jnp.bfloat16)
        lo = (span & 127).astype(jnp.float32).astype(jnp.bfloat16)
        cols = slice(r * 256, (r + 1) * 256)
        out_ref[:high, cols] = jnp.where(tall == hi, one, zero)
        out_ref[high:, cols] = jnp.where(short == lo, one, zero)


def onehot(span, high):
    shape = jax.ShapeDtypeStruct((high + LANES, 4096), jnp.bfloat16)
    return pl.pallas_call(
        functools.partial(onehot_kernel, high),
        grid=(2,),
        in_specs=[pl.BlockSpec((8, 256), lambda s: (s, 0))],
        out_specs=pl.BlockSpec((high + LANES, 2048), lambda s: (0, s)),
        out_shape=shape,
        name="onehot",
        cost_estimate=pl.CostEstimate(flops=10**9, transcendentals=0, bytes_accessed=5 * 2**20),
    )(span)


def up(v):
    return pltpu.roll(v, v.shape[0] - 1, 0)


def down(v):
    return pltpu.roll(v, 1, 0)


def ahead(v):
    return pltpu.roll(v, v.shape[1] - 1, 1)


def behind(v):
    return pltpu.roll(v, 1, 1)


def main_kernel(
    peers, levels,
    damping_ref, exner_ref, scale_ref, mass_ref,
    theta_ref, vapor_ref, cloud_ref, div_ref, edge_ref, inv_ref, onehot_hbm,
    below_ref, above_ref, colr_ref, coll_ref, ownl_ref, ownr_ref,
    diag_br, diag_ar, diag_bl, diag_al,
    theta_out, vapor_out, cloud_out, div_out, send_out,
    coef_ref, edge_a, edge_b, rain_ref, onehot_ref, lo_ref, sem,
):
    total = 3 * levels + 4
    high = peers * 32
    step = pl.program_id(0)
    steps = pl.num_programs(0)
    fetch = pltpu.make_async_copy(onehot_hbm, onehot_ref, sem)

    sub = lax.broadcasted_iota(jnp.int32, (8, 256), 0)
    sub_half = sub[:, :LANES]

    def row_tile(index):
        def row(ref, r):
            return jnp.broadcast_to(ref[pl.ds(r * total + index, 1), :], (8, 256))

        low = jnp.where(sub < 1, row(below_ref, 0), row(below_ref, 1))
        top = jnp.where(sub < 7, row(above_ref, 0), row(above_ref, 1))
        tile = jnp.where(sub < 4, low, top)
        return tile[:, :LANES], tile[:, LANES:]

    @pl.when(step == 0)
    def _():
        fetch.start()
        lane24 = lax.broadcasted_iota(jnp.int32, (24, LANES), 1)
        even = (lane24 & 1) == 0

        def packed(own, low, top, cols):
            corner = jnp.where(sub_half < 4, low, top)
            return jnp.concatenate([own[:, cols], corner], axis=0)

        def side_packs(field):
            cols = slice(field * LANES, (field + 1) * LANES)

            def inner(ref, slot):
                rows = pl.ds(2 * total + 4 + 8 * (slot // 2), 8)
                return ref[rows, (slot % 2) * LANES : (slot % 2 + 1) * LANES]

            v_r = packed(colr_ref, diag_br[:, cols], diag_ar[:, cols], cols)
            v_l = packed(coll_ref, diag_bl[:, cols], diag_al[:, cols], cols)
            o_l = packed(ownl_ref, inner(below_ref, field), inner(above_ref, field), cols)
            o_r = packed(ownr_ref, inner(below_ref, 3 + field), inner(above_ref, 3 + field), cols)
            return v_r, v_l, o_l, o_r

        packs = [side_packs(field) for field in range(3)]
        geo = []
        for g in range(4):
            slot = levels + g
            right = pltpu.roll(packs[0][0], (LANES - 2 * slot) % LANES, 1)
            left = pltpu.roll(packs[0][1], (2 * LANES - 2 - 2 * slot) % LANES, 1)
            side = jnp.where(lane24 < 64, right, left)
            centre = edge_ref[16 * g : 16 * g + 16, :] if g < 3 else inv_ref[...]
            tiles = row_tile(3 * levels + g)
            halves = [
                jnp.concatenate([centre[:, h * LANES : (h + 1) * LANES], tiles[h]], axis=0)
                for h in range(2)
            ]
            geo.append(jnp.concatenate(halves + [side], axis=1))
        w0, w1, w2, inv = geo
        c1 = inv * w0
        c2 = inv * down(w0)
        c3 = inv * w1
        c4 = inv * behind(w1)
        c5 = inv * w2
        c6 = inv * behind(up(w2))
        c0 = c1 + c2 + c3 + c4 + c5 + c6
        shifted = (c0, c1, c2, behind(c3), ahead(c4), behind(c5), ahead(c6))
        for k, c in enumerate(shifted):
            coef_ref[k] = c[:, :256]
        rain_ref[...] = jnp.zeros_like(rain_ref)

        def pick(c, col):
            return jnp.broadcast_to(c[:, col : col + 1], (24, LANES))

        k0, k1, k2, k3, k4, k5, k6 = (
            jnp.where(even, pick(c, 256), pick(c, 383)) for c in (c0, c1, c2, c3, c4, c5, c6)
        )
        x3 = jnp.where(even, pick(c3, 255), pick(c4, 0))
        x5 = jnp.where(even, pick(c5, 255), 0.0)
        x6 = jnp.where(even, 0.0, pick(c6, 0))
        for field in range(3):
            v_r, v_l, o_l, o_r = packs[field]
            v = jnp.where(even, v_r, v_l)
            v_up = up(v)
            v_dn = down(v)
            edge_a[field] = x3 * v + x5 * v_dn + x6 * v_up
            nxt = jnp.where(even, ahead(v_r), behind(o_l))
            prv = jnp.where(even, ahead(o_r), behind(v_l))
            first = (k1 * v_up + k2 * v_dn - k0 * v) + (
                (k3 * nxt + k5 * down(nxt)) + (k4 * prv + k6 * up(prv))
            )
            edge_b[field] = x3 * first + x5 * down(first) + x6 * up(first)

    def lap(halves, edge, rows):
        lane = lax.broadcasted_iota(jnp.int32, (rows, LANES), 1)
        a, b, c = [], [], []
        for h in range(2):
            cols = slice(h * LANES, (h + 1) * LANES)
            v_up = up(halves[h])[:rows]
            v_dn = down(halves[h])[:rows]
            v = halves[h][:rows]
            a.append(ahead(coef_ref[3, :rows, cols] * v + coef_ref[5, :rows, cols] * v_dn))
            b.append(behind(coef_ref[4, :rows, cols] * v + coef_ref[6, :rows, cols] * v_up))
            c.append(
                coef_ref[1, :rows, cols] * v_up
                + coef_ref[2, :rows, cols] * v_dn
                - coef_ref[0, :rows, cols] * v
            )
        last = lane == LANES - 1
        zero = lane == 0
        left = (jnp.where(last, a[1], a[0]) + jnp.where(zero, edge, b[0])) + c[0]
        right = (jnp.where(last, edge, a[1]) + jnp.where(zero, b[0], b[1])) + c[1]
        return left, right

    def damp(ref, k, field, l):
        turn = lax.rem(2 * LANES - 1 - 2 * l, LANES)
        centre = [ref[k, :, h * LANES : (h + 1) * LANES] for h in range(2)]
        tiles = row_tile(field * levels + l)
        first = lap(
            [jnp.concatenate([centre[h], tiles[h]], axis=0) for h in range(2)],
            pltpu.roll(edge_a[field], turn, 1),
            24,
        )
        second = lap(first, pltpu.roll(edge_b[field, :16], turn, 1), 16)
        rate = damping_ref[field, l]
        return [centre[h] - rate * second[h] for h in range(2)]

    def level(k):
        l = step * BLOCK_LEVELS + k
        div = damp(div_ref, k, 2, l)
        thetas = damp(theta_ref, k, 0, l)
        vapors = damp(vapor_ref, k, 1, l)
        exner = exner_ref[l]
        scale = scale_ref[l]
        mass = mass_ref[l]
        ratio = jnp.full((1, LANES), LATENT, jnp.float32) / jnp.full((1, LANES), exner, jnp.float32)
        for h in range(2):
            cols = slice(h * LANES, (h + 1) * LANES)
            theta, vapor = thetas[h], vapors[h]
            div_out[k, :, cols] = div[h]
            cloud = cloud_ref[k, :, cols]
            temper = theta * exner
            saturation = scale * jnp.exp(temper)
            condensed = (vapor - saturation) / (1.0 + LATENT * saturation)
            saturation = scale * jnp.exp(temper + LATENT * condensed)
            condensed = condensed + (vapor - condensed - saturation) / (1.0 + LATENT * saturation)
            condensed = jnp.maximum(condensed, -cloud)
            theta_out[k, :, cols] = theta + condensed * ratio
            vapor_out[k, :, cols] = vapor - condensed
            liquid = cloud + condensed
            rained = AUTO_RATE * jnp.maximum(liquid - QCRIT, 0.0)
            cloud_out[k, :, cols] = liquid - rained
            rain_ref[:, cols] += mass * rained

    def body(m, carry):
        for j in range(UNROLL):
            level(m * UNROLL + j)
        return carry

    count = jnp.minimum(BLOCK_LEVELS, levels - step * BLOCK_LEVELS)
    lax.fori_loop(0, lax.div(count, UNROLL), body, 0)

    @pl.when(step == steps - 1)
    def _():
        fetch.wait()
        for r in range(16):
            value = rain_ref[r : r + 1, :]
            coarse = value.astype(jnp.bfloat16)
            fine = (value - coarse.astype(jnp.float32)).astype(jnp.bfloat16)
            cols = slice(r * 256, (r + 1) * 256)
            here = onehot_ref[high:, cols]
            lo_ref[:LANES, cols] = here * coarse
            lo_ref[LANES:, cols] = here * fine
        placed = lax.dot_general(
            onehot_ref[:high, :],
            lo_ref[...],
            (((1,), (1,)), ((), ())),
            preferred_element_type=jnp.float32,
        )
        send_out[...] = placed[:, :LANES] + placed[:, LANES:]


def physics(peers, scalars, fields, whole_args, marks, halos):
    levels = fields[0].shape[0]
    steps = pl.cdiv(levels, BLOCK_LEVELS)
    high = peers * 32
    block = pl.BlockSpec((BLOCK_LEVELS, 16, 256), lambda s: (s, 0, 0))
    whole = lambda a: pl.BlockSpec(a.shape, lambda s: (0,) * len(a.shape))
    field = jax.ShapeDtypeStruct(fields[0].shape, jnp.float32)
    sent = jax.ShapeDtypeStruct((high, LANES), jnp.float32)
    return pl.pallas_call(
        functools.partial(main_kernel, peers, levels),
        grid=(steps,),
        in_specs=[pl.BlockSpec(memory_space=pltpu.SMEM)] * 4
        + [block] * 4
        + [whole(a) for a in whole_args]
        + [pl.BlockSpec(memory_space=pl.ANY)]
        + [whole(a) for a in halos],
        out_specs=[block, block, block, block, whole(sent)],
        out_shape=[field, field, field, field, sent],
        scratch_shapes=[
            pltpu.VMEM((7, 24, 256), jnp.float32),
            pltpu.VMEM((3, 24, LANES), jnp.float32),
            pltpu.VMEM((3, 24, LANES), jnp.float32),
            pltpu.VMEM((16, 256), jnp.float32),
            pltpu.VMEM((high + LANES, 4096), jnp.bfloat16),
            pltpu.VMEM((2 * LANES, 4096), jnp.bfloat16),
            pltpu.SemaphoreType.DMA(()),
        ],
        name="physics",
    )(*scalars, *fields, *whole_args, marks, *halos)


def on_device(
    theta,
    vapor,
    cloud,
    divergence,
    edge_weight,
    inv_area,
    damping,
    exner,
    sat_scale,
    layer_mass,
    span_of,
):
    n_px = lax.axis_size("px")
    peers = lax.axis_size("py")

    def fetch(x, row, col):
        moves = [
            (((i + row) % n_px) * peers + (j + col) % peers, i * peers + j)
            for i in range(n_px)
            for j in range(peers)
        ]
        return lax.ppermute(x, ("px", "py"), moves)

    flat = lambda x: x.reshape(-1, 256)
    edge = flat(edge_weight)
    top, bot, left, right, left_low, left_high, right_low, right_high = pack(
        flat(theta), flat(vapor), flat(divergence), edge, inv_area
    )
    below = fetch(top, 1, 0)
    above = fetch(bot, -1, 0)
    colr = fetch(left, 0, 1)
    coll = fetch(right, 0, -1)
    diag_br = fetch(left_low, 1, 1)
    diag_ar = fetch(left_high, -1, 1)
    diag_bl = fetch(right_low, 1, -1)
    diag_al = fetch(right_high, -1, -1)
    marks = onehot(span_of, peers * 32)
    theta_next, vapor_next, cloud_next, divergence_next, send = physics(
        peers,
        (damping, exner, sat_scale, layer_mass),
        (theta, vapor, cloud, divergence),
        (edge, inv_area),
        marks,
        (below, above, colr, coll, left, right, diag_br, diag_ar, diag_bl, diag_al),
    )
    got = lax.all_to_all(send.reshape(peers, 32, LANES), "py", split_axis=0, concat_axis=0, tiled=True)
    precip = jnp.sum(got, axis=0).reshape(1, 4096)
    return (theta_next, vapor_next, cloud_next, divergence_next, precip)


def solution(mesh):
    field = P(None, "px", "py")
    plane = P("px", "py")
    return jax.shard_map(
        on_device,
        mesh=mesh,
        in_specs=(field, field, field, field, field, plane, P(), P(), P(), P(), plane),
        out_specs=(field, field, field, field, plane),
        check_vma=False,
    )
```

time: 67.8 us -> 60.4 us (0.89)
  Pallas kernels: 32.5 us -> 20.4 us
  starting transfers between devices: 11.5 us -> 19.1 us
  local copies, waits for them, and re-layouts: 2.77 us -> 1.49 us
  blocking collectives: 13.2 us -> 12.2 us
    pallas_call x1, Pallas kernels: 24.4 us -> 13.4 us  [physics(): pl.pallas_call(functools.partial(main_kernel, peers, levels), grid=(steps...]
    ppermute x6 -> x8, starting transfers between devices: 11.5 us -> 19.1 us  [fetch(): return lax.ppermute(x, ('px', 'py'), moves)]
    unnamed x21 -> x16, local copies, waits for them, and re-layouts: 2.68 us -> 1.49 us
    pallas_call x1 -> x2, Pallas kernels: 8.14 us -> 6.98 us  [the longest x1 3.6 us: pack(): pl.pallas_call(pack_kernel, grid=(1,), in_specs=sides * 3 + [whole(edge),...]
    all_to_all x1, blocking collectives: 13.2 us -> 12.2 us  [on_device(): lax.all_to_all(send.reshape(peers, 32, LANES), 'py', split_axis=0, concat...]
    ppermute x6 -> x8, waiting for transfers between devices: 5.6 us -> 5.54 us  [fetch(): return lax.ppermute(x, ('px', 'py'), moves)]
  transfers between devices with their start and end apart: 6 -> 8, of which waited for: 2 -> 2; matrix products, arithmetic and copies ran while one was open for 1% -> 0% of each run, Pallas kernels for 0% -> 6%
where the time goes in v2:
time: 60.4 us; the launch traced here: 60.1 us
  Pallas kernels  20.4 us (34%)
  starting transfers between devices  19.1 us (32%)
  blocking collectives  12.2 us (20%)
  waiting for transfers between devices  5.54 us (9%)
  local copies, waits for them, and re-layouts  1.49 us (2%)
  between operations  0.71 us (1%)
  other arithmetic  0.63 us (1%)
    ppermute x8, starting transfers between devices, fetch(): return lax.ppermute(x, ('px', 'py'), moves)  19.1 us
    pallas_call x1, Pallas kernels, physics(): pl.pallas_call(functools.partial(main_kernel, peers, levels), grid=(steps...  13.4 us
    all_to_all x1, blocking collectives, on_device(): lax.all_to_all(send.reshape(peers, 32, LANES), 'py', split_axis=0, concat...  12.2 us
    ppermute x8, waiting for transfers between devices, fetch(): return lax.ppermute(x, ('px', 'py'), moves)  5.54 us
    pallas_call x1, Pallas kernels, pack(): pl.pallas_call(pack_kernel, grid=(1,), in_specs=sides * 3 + [whole(edge),...  3.6 us
    pallas_call x1, Pallas kernels, onehot(): pl.pallas_call(functools.partial(onehot_kernel, high), grid=(2,), in_spec...  3.38 us
    unnamed x16, local copies, waits for them, and re-layouts  1.49 us
  transfers between devices with their start and end apart: 8, of which 2 were waited for; matrix products, arithmetic and copies ran while one was open for 0% of the time, Pallas kernels for 6%

profile of v2, /device:TPU:0, one launch (start us, length us, event | category | flops | bytes accessed | tf_op | source)
XLA Modules:
  0.0 60.1 jit_solution(7178861879976030073)
XLA Ops:
  0.6 3.6 %pack.1 = (f32[384,256]{1,0:T(8,128)}, f32[384,256]{1,0:T(8,128)}, f32[16,384]{1,0:T(8,128)}, f32[16,384]{1,0:T(8,128)}, f32[8,384]{1,0:T(8,128)}, /*index=5*/f3...) custom-call(f32[928,256]{1,0:T(8,128)} %bitcast.6, f32[928,256]{1,0:T(8,128)} %bitcast.7, f32[928,256]{1,0:T(8,128)} %bitcast.8, ...), custom_call_target="tpu_custom_call" | custom-call | tf_op jit(solution)/shard_map/pack/pallas_call | solution.py:78
  4.2 2.3 %collective-permute-start = (f32[384,256]{1,0:T(8,128)}, f32[384,256]{1,0:T(8,128)S(1)}, u32[]{:S(2)}, u32[]{:S(2)}) collective-permute-start(f32[384,256]{1,0:T(8,128)} %get-tuple-element.18), channel_id=1, source_target_pairs={{16,0},{17,1},{18,2},{19,3},{20,4},{21,5},{22,6},{23,7},{24,8},{25... | collective-permute-start | bytes 1179656 | tf_op jit(solution)/shard_map/ppermute | solution.py:376
  6.5 0.0 collective-permute-start.1
  6.5 8.9 %collective-permute-start.4 = (f32[8,384]{1,0:T(8,128)}, f32[8,384]{1,0:T(8,128)S(1)}, u32[]{:S(2)}, u32[]{:S(2)}) collective-permute-start(f32[8,384]{1,0:T(8,128)} %get-tuple-element.22), channel_id=1, source_target_pairs={{17,0},{18,1},{19,2},{20,3},{21,4},{22,5},{23,6},{24,7},{25,8},{26... | collective-permute-start | bytes 36872 | tf_op jit(solution)/shard_map/ppermute | solution.py:376
  15.4 0.0 collective-permute-start.5
  15.4 3.9 %collective-permute-start.6 = (f32[8,384]{1,0:T(8,128)}, f32[8,384]{1,0:T(8,128)S(1)}, u32[]{:S(2)}, u32[]{:S(2)}) collective-permute-start(f32[8,384]{1,0:T(8,128)} %get-tuple-element.24), channel_id=1, source_target_pairs={{31,0},{16,1},{17,2},{18,3},{19,4},{20,5},{21,6},{22,7},{23,8},{24... | collective-permute-start | bytes 36872 | tf_op jit(solution)/shard_map/ppermute | solution.py:376
  19.3 0.0 collective-permute-done.4.diag_br
  19.3 0.0 copy-start.4
  19.3 0.0 collective-permute-start.7
  19.3 1.6 %collective-permute-done.5.diag_ar = f32[8,384]{1,0:T(8,128)S(1)} collective-permute-done((f32[8,384]{1,0:T(8,128)}, f32[8,384]{1,0:T(8,128)S(1)}, u32[]{:S(2)}, u32[]{:S(2)}) %collective-permute-start.5) | collective-permute-done | bytes 12320 | tf_op jit(solution)/shard_map/ppermute | solution.py:376
  20.8 0.0 copy-start.5
  20.9 4.1 %collective-permute-start.2 = (f32[16,384]{1,0:T(8,128)}, f32[16,384]{1,0:T(8,128)S(1)}, u32[]{:S(2)}, u32[]{:S(2)}) collective-permute-start(f32[16,384]{1,0:T(8,128)} %get-tuple-element.20.ownl_ref), channel_id=1, source_target_pairs={{1,0},{2,1},{3,2},{4,3},{5,4},{6,5},{7,6},{8,7},{9,8},{10,9},{11,1... | collective-permute-start | bytes 73736 | tf_op jit(solution)/shard_map/ppermute | solution.py:376
  24.9 0.0 collective-permute-done.6.diag_bl
  24.9 0.0 copy-start.6
  24.9 0.0 collective-permute-start.3
  24.9 3.4 %onehot.1.onehot_hbm = bf16[640,4096]{1,0:T(8,128)(2,1)} custom-call(s32[16,256]{1,0:T(8,128)} %span_ref.1), custom_call_target="tpu_custom_call" | custom-call | flops 1000000000 | bytes 5242880 | tf_op jit(solution)/shard_map/onehot/pallas_call | solution.py:108
  28.3 0.0 collective-permute-done.7.diag_al
  28.3 0.0 copy-start.7
  28.3 0.0 collective-permute-done.2.colr_ref
  28.3 0.0 copy-start.2
  28.3 4.0 %collective-permute-done.3.coll_ref = f32[16,384]{1,0:T(8,128)S(1)} collective-permute-done((f32[16,384]{1,0:T(8,128)}, f32[16,384]{1,0:T(8,128)S(1)}, u32[]{:S(2)}, u32[]{:S(2)}) %collective-permute-start.3) | collective-permute-done | bytes 24608 | tf_op jit(solution)/shard_map/ppermute | solution.py:376
  32.3 0.0 copy-start.3
  32.3 0.0 collective-permute-done.below_ref
  32.3 0.0 copy-start
  32.3 0.0 collective-permute-done.1.above_ref
  32.3 0.0 copy-done.4
  32.3 0.0 copy-done.5
  32.3 0.0 copy-done.6
  32.3 0.0 copy-done.7
  32.3 0.0 copy-done.2
  32.3 0.5 copy-done.3
  32.9 0.2 copy-done
  33.1 0.0 copy-start.1
  33.1 0.8 %copy-done.1 = f32[384,256]{1,0:T(8,128)} copy-done((f32[384,256]{1,0:T(8,128)}, f32[384,256]{1,0:T(8,128)S(1)}, u32[]{:S(2)}) %copy-start.1) | copy-done | bytes 393240
  33.8 13.4 %physics.1 = (f32[58,16,256]{2,1,0:T(8,128)}, f32[58,16,256]{2,1,0:T(8,128)}, f32[58,16,256]{2,1,0:T(8,128)}, f32[58,16,256]{2,1,0:T(8,128)}, f32[512,128]{1,0:T(8,128)}) custom-call(f32[3,58]{1,0:T(4,128)} %damping_ref.1, f32[58]{0:T(128)} %exner_ref.1, f32[58]{0:T(128)} %scale_ref.1, f32[58]{0:T(128)} %mass_ref.1, f32[58,16,256]{2,1,0:T(8,128)} %theta_ref.1, ...), custom_call_target="tpu_custom_call" | custom-call | tf_op jit(solution)/shard_map/physics/pallas_call | solution.py:331
  47.3 12.2 %all_to_all.5 = f32[16,32,128]{2,1,0:T(8,128)S(1)} all-to-all(f32[16,32,128]{2,1,0:T(8,128)} %bitcast.12), channel_id=1, replica_groups=mesh['px'=8,'py'=16] {'py'}, dimensions={0} | all-to-all | bytes 524288 | tf_op jit(solution)/shard_map/all_to_all | solution.py:400
  59.4 0.6 %reduce_sum.9 = f32[32,128]{1,0:T(8,128)} reduce(f32[16,32,128]{2,1,0:T(8,128)S(1)} %all_to_all.5, f32[]{:T(128)} %constant.0.clone.1), dimensions={0}, to_apply=%region_0.0 | reduce | flops 61440 | bytes 278532 | tf_op jit(solution)/shard_map/reduce_sum | solution.py:401
Async XLA Ops:
  4.2 28.0 %collective-permute-start = (f32[384,256]{1,0:T(8,128)}, f32[384,256]{1,0:T(8,128)S(1)}, u32[]{:S(2)}, u32[]{:S(2)}) collective-permute-start(f32[384,256]{1,0:T(8,128)} %get-tuple-element.18), channel_id=1, source_target_pairs={{16,0},{17,1},{18,2},{19,3},{20,4},{21,5},{22,6},{23,7},{24,8},{25... | collective-permute-start | bytes 1179656 | tf_op jit(solution)/shard_map/ppermute | solution.py:376
  6.5 25.8 %collective-permute-start.1 = (f32[384,256]{1,0:T(8,128)}, f32[384,256]{1,0:T(8,128)S(1)}, u32[]{:S(2)}, u32[]{:S(2)}) collective-permute-start(f32[384,256]{1,0:T(8,128)} %get-tuple-element.19), channel_id=1, source_target_pairs={{112,0},{113,1},{114,2},{115,3},{116,4},{117,5},{118,6},{119,7},{1... | collective-permute-start | bytes 1179656 | tf_op jit(solution)/shard_map/ppermute | solution.py:376
  6.5 12.7 %collective-permute-start.4 = (f32[8,384]{1,0:T(8,128)}, f32[8,384]{1,0:T(8,128)S(1)}, u32[]{:S(2)}, u32[]{:S(2)}) collective-permute-start(f32[8,384]{1,0:T(8,128)} %get-tuple-element.22), channel_id=1, source_target_pairs={{17,0},{18,1},{19,2},{20,3},{21,4},{22,5},{23,6},{24,7},{25,8},{26... | collective-permute-start | bytes 36872 | tf_op jit(solution)/shard_map/ppermute | solution.py:376
  15.4 5.4 %collective-permute-start.5 = (f32[8,384]{1,0:T(8,128)}, f32[8,384]{1,0:T(8,128)S(1)}, u32[]{:S(2)}, u32[]{:S(2)}) collective-permute-start(f32[8,384]{1,0:T(8,128)} %get-tuple-element.23), channel_id=1, source_target_pairs={{113,0},{114,1},{115,2},{116,3},{117,4},{118,5},{119,6},{120,7},{1... | collective-permute-start | bytes 36872 | tf_op jit(solution)/shard_map/ppermute | solution.py:376
  15.4 9.5 %collective-permute-start.6 = (f32[8,384]{1,0:T(8,128)}, f32[8,384]{1,0:T(8,128)S(1)}, u32[]{:S(2)}, u32[]{:S(2)}) collective-permute-start(f32[8,384]{1,0:T(8,128)} %get-tuple-element.24), channel_id=1, source_target_pairs={{31,0},{16,1},{17,2},{18,3},{19,4},{20,5},{21,6},{22,7},{23,8},{24... | collective-permute-start | bytes 36872 | tf_op jit(solution)/shard_map/ppermute | solution.py:376
  19.3 13.0 %copy-start.4 = (f32[8,384]{1,0:T(8,128)}, f32[8,384]{1,0:T(8,128)S(1)}, u32[]{:S(2)}) copy-start(f32[8,384]{1,0:T(8,128)S(1)} %collective-permute-done.4.diag_br) | copy-start | bytes 36868
  19.3 9.0 %collective-permute-start.7 = (f32[8,384]{1,0:T(8,128)}, f32[8,384]{1,0:T(8,128)S(1)}, u32[]{:S(2)}, u32[]{:S(2)}) collective-permute-start(f32[8,384]{1,0:T(8,128)} %get-tuple-element.25), channel_id=1, source_target_pairs={{127,0},{112,1},{113,2},{114,3},{115,4},{116,5},{117,6},{118,7},{1... | collective-permute-start | bytes 36872 | tf_op jit(solution)/shard_map/ppermute | solution.py:376
  20.8 11.5 %copy-start.5 = (f32[8,384]{1,0:T(8,128)}, f32[8,384]{1,0:T(8,128)S(1)}, u32[]{:S(2)}) copy-start(f32[8,384]{1,0:T(8,128)S(1)} %collective-permute-done.5.diag_ar) | copy-start | bytes 36868
  20.9 7.5 %collective-permute-start.2 = (f32[16,384]{1,0:T(8,128)}, f32[16,384]{1,0:T(8,128)S(1)}, u32[]{:S(2)}, u32[]{:S(2)}) collective-permute-start(f32[16,384]{1,0:T(8,128)} %get-tuple-element.20.ownl_ref), channel_id=1, source_target_pairs={{1,0},{2,1},{3,2},{4,3},{5,4},{6,5},{7,6},{8,7},{9,8},{10,9},{11,1... | collective-permute-start | bytes 73736 | tf_op jit(solution)/shard_map/ppermute | solution.py:376
  24.9 7.4 %copy-start.6 = (f32[8,384]{1,0:T(8,128)}, f32[8,384]{1,0:T(8,128)S(1)}, u32[]{:S(2)}) copy-start(f32[8,384]{1,0:T(8,128)S(1)} %collective-permute-done.6.diag_bl) | copy-start | bytes 36868
  24.9 7.4 %collective-permute-start.3 = (f32[16,384]{1,0:T(8,128)}, f32[16,384]{1,0:T(8,128)S(1)}, u32[]{:S(2)}, u32[]{:S(2)}) collective-permute-start(f32[16,384]{1,0:T(8,128)} %get-tuple-element.21.ownr_ref), channel_id=1, source_target_pairs={{15,0},{0,1},{1,2},{2,3},{3,4},{4,5},{5,6},{6,7},{7,8},{8,9},{9,10... | collective-permute-start | bytes 73736 | tf_op jit(solution)/shard_map/ppermute | solution.py:376
  28.3 4.0 %copy-start.7 = (f32[8,384]{1,0:T(8,128)}, f32[8,384]{1,0:T(8,128)S(1)}, u32[]{:S(2)}) copy-start(f32[8,384]{1,0:T(8,128)S(1)} %collective-permute-done.7.diag_al) | copy-start | bytes 36868
  28.3 4.0 %copy-start.2 = (f32[16,384]{1,0:T(8,128)}, f32[16,384]{1,0:T(8,128)S(1)}, u32[]{:S(2)}) copy-start(f32[16,384]{1,0:T(8,128)S(1)} %collective-permute-done.2.colr_ref) | copy-start | bytes 73732
  32.3 0.6 %copy-start.3 = (f32[16,384]{1,0:T(8,128)}, f32[16,384]{1,0:T(8,128)S(1)}, u32[]{:S(2)}) copy-start(f32[16,384]{1,0:T(8,128)S(1)} %collective-permute-done.3.coll_ref) | copy-start | bytes 73732
  32.3 0.8 %copy-start = (f32[384,256]{1,0:T(8,128)}, f32[384,256]{1,0:T(8,128)S(1)}, u32[]{:S(2)}) copy-start(f32[384,256]{1,0:T(8,128)S(1)} %collective-permute-done.below_ref) | copy-start | bytes 1179652
  33.1 0.8 %copy-start.1 = (f32[384,256]{1,0:T(8,128)}, f32[384,256]{1,0:T(8,128)S(1)}, u32[]{:S(2)}) copy-start(f32[384,256]{1,0:T(8,128)S(1)} %collective-permute-done.1.above_ref) | copy-start | bytes 1179652

commit v3 on v2

--- a/solution.py
+++ b/solution.py
@@ -18,7 +18,7 @@
 
 def pack_kernel(
     theta0, theta1, vapor0, vapor1, div0, div1, edge_ref, inv_ref,
-    top_ref, bot_ref, left_ref, right_ref, left_low, left_high, right_low, right_high,
+    top_ref, bot_ref, left_ref, right_ref,
 ):
     levels = theta0.shape[0] // 16
     total = 3 * levels + 4
@@ -53,12 +53,8 @@
                     value = edge_ref[16 * g : 16 * g + 16, cols] if g < 3 else inv_ref[:, cols]
                     acc = place(acc, value, levels + g, side)
             cols = slice(field * LANES, (field + 1) * LANES)
-            whole, low, high = (
-                (left_ref, left_low, left_high) if side == 0 else (right_ref, right_low, right_high)
-            )
+            whole = left_ref if side == 0 else right_ref
             whole[:, cols] = acc
-            low[:, cols] = acc[:8]
-            high[:, cols] = acc[8:]
             slot = 3 * side + field
             rows = pl.ds(low_base + 8 * (slot // 2), 8)
             cols = slice((slot % 2) * LANES, (slot % 2 + 1) * LANES)
@@ -71,10 +67,9 @@
     total = 3 * levels + 4
     rows = jax.ShapeDtypeStruct((2 * total + 28, 256), jnp.float32)
     cols = jax.ShapeDtypeStruct((16, 3 * LANES), jnp.float32)
-    half = jax.ShapeDtypeStruct((8, 3 * LANES), jnp.float32)
     sides = [pl.BlockSpec((16 * levels, LANES), lambda s, c=c: (0, c)) for c in range(2)]
     whole = lambda a: pl.BlockSpec(a.shape, lambda s: (0,) * len(a.shape))
-    outs = (rows, rows, cols, cols, half, half, half, half)
+    outs = (rows, rows, cols, cols)
     return pl.pallas_call(
         pack_kernel,
         grid=(1,),
@@ -137,7 +132,7 @@
     damping_ref, exner_ref, scale_ref, mass_ref,
     theta_ref, vapor_ref, cloud_ref, div_ref, edge_ref, inv_ref, onehot_hbm,
     below_ref, above_ref, colr_ref, coll_ref, ownl_ref, ownr_ref,
-    diag_br, diag_ar, diag_bl, diag_al,
+    corner_below, corner_above,
     theta_out, vapor_out, cloud_out, div_out, send_out,
     coef_ref, edge_a, edge_b, rain_ref, onehot_ref, lo_ref, sem,
 ):
@@ -176,8 +171,9 @@
                 rows = pl.ds(2 * total + 4 + 8 * (slot // 2), 8)
                 return ref[rows, (slot % 2) * LANES : (slot % 2 + 1) * LANES]
 
-            v_r = packed(colr_ref, diag_br[:, cols], diag_ar[:, cols], cols)
-            v_l = packed(coll_ref, diag_bl[:, cols], diag_al[:, cols], cols)
+            far = slice((3 + field) * LANES, (4 + field) * LANES)
+            v_r = packed(colr_ref, corner_below[:, cols], corner_above[:, cols], cols)
+            v_l = packed(coll_ref, corner_below[:, far], corner_above[:, far], cols)
             o_l = packed(ownl_ref, inner(below_ref, field), inner(above_ref, field), cols)
             o_r = packed(ownr_ref, inner(below_ref, 3 + field), inner(above_ref, 3 + field), cols)
             return v_r, v_l, o_l, o_r
@@ -335,7 +331,9 @@
         + [block] * 4
         + [whole(a) for a in whole_args]
         + [pl.BlockSpec(memory_space=pl.ANY)]
-        + [whole(a) for a in halos],
+        + [pl.BlockSpec(memory_space=pltpu.VMEM)] * 4
+        + [whole(a) for a in halos[4:6]]
+        + [pl.BlockSpec(memory_space=pltpu.VMEM)] * 2,
         out_specs=[block, block, block, block, whole(sent)],
         out_shape=[field, field, field, field, sent],
         scratch_shapes=[
@@ -364,30 +362,26 @@
     layer_mass,
     span_of,
 ):
-    n_px = lax.axis_size("px")
     peers = lax.axis_size("py")
 
-    def fetch(x, row, col):
-        moves = [
-            (((i + row) % n_px) * peers + (j + col) % peers, i * peers + j)
-            for i in range(n_px)
-            for j in range(peers)
-        ]
-        return lax.ppermute(x, ("px", "py"), moves)
+    def fetch(x, axis, step):
+        count = lax.axis_size(axis)
+        return lax.ppermute(x, axis, [((i + step) % count, i) for i in range(count)])
 
     flat = lambda x: x.reshape(-1, 256)
     edge = flat(edge_weight)
-    top, bot, left, right, left_low, left_high, right_low, right_high = pack(
-        flat(theta), flat(vapor), flat(divergence), edge, inv_area
+    top, bot, left, right = pack(flat(theta), flat(vapor), flat(divergence), edge, inv_area)
+    colr = fetch(left, "py", 1)
+    coll = fetch(right, "py", -1)
+    below = fetch(top, "px", 1)
+    above = fetch(bot, "px", -1)
+    sides = jnp.concatenate([colr, coll], axis=1)
+    corner_below = fetch(sides[:8], "px", 1)
+    corner_above = fetch(sides[8:], "px", -1)
+    halos = tuple(
+        pltpu.with_memory_space_constraint(x, pltpu.VMEM)
+        for x in (below, above, colr, coll, corner_below, corner_above)
     )
-    below = fetch(top, 1, 0)
-    above = fetch(bot, -1, 0)
-    colr = fetch(left, 0, 1)
-    coll = fetch(right, 0, -1)
-    diag_br = fetch(left_low, 1, 1)
-    diag_ar = fetch(left_high, -1, 1)
-    diag_bl = fetch(right_low, 1, -1)
-    diag_al = fetch(right_high, -1, -1)
     marks = onehot(span_of, peers * 32)
     theta_next, vapor_next, cloud_next, divergence_next, send = physics(
         peers,
@@ -395,7 +389,7 @@
         (theta, vapor, cloud, divergence),
         (edge, inv_area),
         marks,
-        (below, above, colr, coll, left, right, diag_br, diag_ar, diag_bl, diag_al),
+        halos[:4] + (left, right) + halos[4:],
     )
     got = lax.all_to_all(send.reshape(peers, 32, LANES), "py", split_axis=0, concat_axis=0, tiled=True)
     precip = jnp.sum(got, axis=0).reshape(1, 4096)

time: 60.4 us -> 50.9 us (0.84)
  starting transfers between devices: 19.1 us -> 11.5 us
  local copies, waits for them, and re-layouts: 1.49 us -> 0.01 us
    ppermute x8 -> x6, starting transfers between devices: 19.1 us -> 11.5 us  [fetch(): lax.ppermute(x, axis, [((i + step) % count, i) for i in range(count)])]
    unnamed x16 -> x1, local copies, waits for them, and re-layouts: 1.49 us -> 0.01 us
    ppermute x8 -> x6, waiting for transfers between devices: 5.54 us -> 5.44 us  [fetch(): lax.ppermute(x, axis, [((i + step) % count, i) for i in range(count)])]
  transfers between devices with their start and end apart: 8 -> 6, of which waited for: 2 -> 1; matrix products, arithmetic and copies ran while one was open for 0% -> 0% of each run, Pallas kernels for 6% -> 7%
where the time goes in v3:
time: 50.9 us; the launch traced here: 50.6 us
  Pallas kernels  20.2 us (40%)
  blocking collectives  12.2 us (24%)
  starting transfers between devices  11.5 us (23%)
  waiting for transfers between devices  5.44 us (11%)
  between operations  0.67 us (1%)
  other arithmetic  0.63 us (1%)
    pallas_call x1, Pallas kernels, physics(): pl.pallas_call(functools.partial(main_kernel, peers, levels), grid=(steps...  13.2 us
    all_to_all x1, blocking collectives, on_device(): lax.all_to_all(send.reshape(peers, 32, LANES), 'py', split_axis=0, concat...  12.2 us
    ppermute x6, starting transfers between devices, fetch(): lax.ppermute(x, axis, [((i + step) % count, i) for i in range(count)])  11.5 us
    ppermute x6, waiting for transfers between devices, fetch(): lax.ppermute(x, axis, [((i + step) % count, i) for i in range(count)])  5.44 us
    pallas_call x1, Pallas kernels, pack(): pl.pallas_call(pack_kernel, grid=(1,), in_specs=sides * 3 + [whole(edge),...  3.59 us
    pallas_call x1, Pallas kernels, onehot(): pl.pallas_call(functools.partial(onehot_kernel, high), grid=(2,), in_spec...  3.42 us
  transfers between devices with their start and end apart: 6, of which 1 were waited for; matrix products, arithmetic and copies ran while one was open for 0% of the time, Pallas kernels for 7%

profile of v3, /device:TPU:0, one launch (start us, length us, event | category | flops | bytes accessed | tf_op | source)
XLA Modules:
  0.0 50.6 jit_solution(2653375682012515327)
XLA Ops:
  0.6 3.6 %pack.1 = (f32[384,256]{1,0:T(8,128)}, f32[384,256]{1,0:T(8,128)}, f32[16,384]{1,0:T(8,128)}, f32[16,384]{1,0:T(8,128)}) custom-call(f32[928,256]{1,0:T(8,128)} %bitcast.6, f32[928,256]{1,0:T(8,128)} %bitcast.7, f32[928,256]{1,0:T(8,128)} %bitcast.8, f32[928,256]{1,0:T(8,128)} %bitcast.9, f32[928,256]{1,0:T(8,128)} %bitcast.10, f32[928,256]{1,0:T(8,128)} %bitcast.11, ...), custom_call_target="tpu_custom_call" | custom-call | tf_op jit(solution)/shard_map/pack/pallas_call | solution.py:73
  4.2 6.6 %collective-permute-start.2 = (f32[16,384]{1,0:T(8,128)}, f32[16,384]{1,0:T(8,128)S(1)}, u32[]{:S(2)}, u32[]{:S(2)}) collective-permute-start(f32[16,384]{1,0:T(8,128)} %get-tuple-element.16.ownl_ref), channel_id=1, source_target_pairs={{1,0},{2,1},{3,2},{4,3},{5,4},{6,5},{7,6},{8,7},{9,8},{10,9},{11,1... | collective-permute-start | bytes 73736 | tf_op jit(solution)/shard_map/ppermute | solution.py:369
  10.8 0.0 collective-permute-start.3
  10.8 1.9 %collective-permute-start = (f32[384,256]{1,0:T(8,128)}, f32[384,256]{1,0:T(8,128)S(1)}, u32[]{:S(2)}, u32[]{:S(2)}) collective-permute-start(f32[384,256]{1,0:T(8,128)} %get-tuple-element.14), channel_id=1, source_target_pairs={{16,0},{32,16},{48,32},{64,48},{80,64},{96,80},{112,96},{0,112},{1... | collective-permute-start | bytes 1179656 | tf_op jit(solution)/shard_map/ppermute | solution.py:369
  12.7 0.0 collective-permute-start.1
  12.7 0.0 collective-permute-done.2.colr_ref
  12.7 5.4 %collective-permute-done.3.coll_ref = f32[16,384]{1,0:T(8,128)S(1)} collective-permute-done((f32[16,384]{1,0:T(8,128)}, f32[16,384]{1,0:T(8,128)S(1)}, u32[]{:S(2)}, u32[]{:S(2)}) %collective-permute-start.3) | collective-permute-done | bytes 24608 | tf_op jit(solution)/shard_map/ppermute | solution.py:369
  18.2 0.0 collective-permute-start.5
  18.2 2.9 %collective-permute-start.4 = (f32[8,768]{1,0:T(8,128)S(1)}, f32[8,768]{1,0:T(8,128)S(1)}, u32[]{:S(2)}, u32[]{:S(2)}) collective-permute-start(f32[8,768]{1,0:T(8,128)S(1)} %get-tuple-element.24), channel_id=1, source_target_pairs={{16,0},{32,16},{48,32},{64,48},{80,64},{96,80},{112,96},{0,112},{1... | collective-permute-start | bytes 73736 | tf_op jit(solution)/shard_map/ppermute | solution.py:369
  21.1 3.4 %onehot.1.onehot_hbm = bf16[640,4096]{1,0:T(8,128)(2,1)} custom-call(s32[16,256]{1,0:T(8,128)} %span_ref.1), custom_call_target="tpu_custom_call" | custom-call | flops 1000000000 | bytes 5242880 | tf_op jit(solution)/shard_map/onehot/pallas_call | solution.py:103
  24.6 0.0 collective-permute-done.5.corner_above
  24.6 0.0 collective-permute-done.4.corner_below
  24.6 0.0 collective-permute-done.below_ref
  24.6 0.0 collective-permute-done.1.above_ref
  24.6 13.2 %physics.1 = (f32[58,16,256]{2,1,0:T(8,128)}, f32[58,16,256]{2,1,0:T(8,128)}, f32[58,16,256]{2,1,0:T(8,128)}, f32[58,16,256]{2,1,0:T(8,128)}, f32[512,128]{1,0:T(8,128)}) custom-call(f32[3,58]{1,0:T(4,128)} %damping_ref.1, f32[58]{0:T(128)} %exner_ref.1, f32[58]{0:T(128)} %scale_ref.1, f32[58]{0:T(128)} %mass_ref.1, f32[58,16,256]{2,1,0:T(8,128)} %theta_ref.1, ...), custom_call_target="tpu_custom_call" | custom-call | tf_op jit(solution)/shard_map/physics/pallas_call | solution.py:327
  37.8 12.2 %all_to_all.5 = f32[16,32,128]{2,1,0:T(8,128)S(1)} all-to-all(f32[16,32,128]{2,1,0:T(8,128)} %bitcast.12), channel_id=1, replica_groups=mesh['px'=8,'py'=16] {'py'}, dimensions={0} | all-to-all | bytes 524288 | tf_op jit(solution)/shard_map/all_to_all | solution.py:394
  50.0 0.6 %reduce_sum.9 = f32[32,128]{1,0:T(8,128)} reduce(f32[16,32,128]{2,1,0:T(8,128)S(1)} %all_to_all.5, f32[]{:T(128)} %constant.0.clone.1), dimensions={0}, to_apply=%region_0.0 | reduce | flops 61440 | bytes 278532 | tf_op jit(solution)/shard_map/reduce_sum | solution.py:395
  (3 shorter events, 0.0 us)
Async XLA Ops:
  4.2 8.5 %collective-permute-start.2 = (f32[16,384]{1,0:T(8,128)}, f32[16,384]{1,0:T(8,128)S(1)}, u32[]{:S(2)}, u32[]{:S(2)}) collective-permute-start(f32[16,384]{1,0:T(8,128)} %get-tuple-element.16.ownl_ref), channel_id=1, source_target_pairs={{1,0},{2,1},{3,2},{4,3},{5,4},{6,5},{7,6},{8,7},{9,8},{10,9},{11,1... | collective-permute-start | bytes 73736 | tf_op jit(solution)/shard_map/ppermute | solution.py:369
  10.8 7.4 %collective-permute-start.3 = (f32[16,384]{1,0:T(8,128)}, f32[16,384]{1,0:T(8,128)S(1)}, u32[]{:S(2)}, u32[]{:S(2)}) collective-permute-start(f32[16,384]{1,0:T(8,128)} %get-tuple-element.17.ownr_ref), channel_id=1, source_target_pairs={{15,0},{0,1},{1,2},{2,3},{3,4},{4,5},{5,6},{6,7},{7,8},{8,9},{9,10... | collective-permute-start | bytes 73736 | tf_op jit(solution)/shard_map/ppermute | solution.py:369
  10.8 13.8 %collective-permute-start = (f32[384,256]{1,0:T(8,128)}, f32[384,256]{1,0:T(8,128)S(1)}, u32[]{:S(2)}, u32[]{:S(2)}) collective-permute-start(f32[384,256]{1,0:T(8,128)} %get-tuple-element.14), channel_id=1, source_target_pairs={{16,0},{32,16},{48,32},{64,48},{80,64},{96,80},{112,96},{0,112},{1... | collective-permute-start | bytes 1179656 | tf_op jit(solution)/shard_map/ppermute | solution.py:369
  12.7 11.8 %collective-permute-start.1 = (f32[384,256]{1,0:T(8,128)}, f32[384,256]{1,0:T(8,128)S(1)}, u32[]{:S(2)}, u32[]{:S(2)}) collective-permute-start(f32[384,256]{1,0:T(8,128)} %get-tuple-element.15), channel_id=1, source_target_pairs={{112,0},{0,16},{16,32},{32,48},{48,64},{64,80},{80,96},{96,112},{1... | collective-permute-start | bytes 1179656 | tf_op jit(solution)/shard_map/ppermute | solution.py:369
  18.2 6.4 %collective-permute-start.5 = (f32[8,768]{1,0:T(8,128)S(1)}, f32[8,768]{1,0:T(8,128)S(1)}, u32[]{:S(2)}, u32[]{:S(2)}) collective-permute-start(f32[8,768]{1,0:T(8,128)S(1)} %get-tuple-element.23), channel_id=1, source_target_pairs={{112,0},{0,16},{16,32},{32,48},{48,64},{64,80},{80,96},{96,112},{1... | collective-permute-start | bytes 73736 | tf_op jit(solution)/shard_map/ppermute | solution.py:369
  18.2 6.4 %collective-permute-start.4 = (f32[8,768]{1,0:T(8,128)S(1)}, f32[8,768]{1,0:T(8,128)S(1)}, u32[]{:S(2)}, u32[]{:S(2)}) collective-permute-start(f32[8,768]{1,0:T(8,128)S(1)} %get-tuple-element.24), channel_id=1, source_target_pairs={{16,0},{32,16},{48,32},{64,48},{80,64},{96,80},{112,96},{0,112},{1... | collective-permute-start | bytes 73736 | tf_op jit(solution)/shard_map/ppermute | solution.py:369

commit v4 on v3

--- a/solution.py
+++ b/solution.py
@@ -77,6 +77,7 @@
         out_specs=[whole(o) for o in outs],
         out_shape=outs,
         name="pack",
+        compiler_params=pltpu.CompilerParams(vmem_limit_bytes=32 * 2**20),
     )(theta, theta, vapor, vapor, divergence, divergence, edge, inv)
 
 
@@ -107,6 +108,7 @@
         out_specs=pl.BlockSpec((high + LANES, 2048), lambda s: (0, s)),
         out_shape=shape,
         name="onehot",
+        compiler_params=pltpu.CompilerParams(vmem_limit_bytes=32 * 2**20),
         cost_estimate=pl.CostEstimate(flops=10**9, transcendentals=0, bytes_accessed=5 * 2**20),
     )(span)
 
@@ -127,20 +129,24 @@
     return pltpu.roll(v, 1, 1)
 
 
-def main_kernel(
-    peers, levels,
-    damping_ref, exner_ref, scale_ref, mass_ref,
-    theta_ref, vapor_ref, cloud_ref, div_ref, edge_ref, inv_ref, onehot_hbm,
-    below_ref, above_ref, colr_ref, coll_ref, ownl_ref, ownr_ref,
-    corner_below, corner_above,
-    theta_out, vapor_out, cloud_out, div_out, send_out,
-    coef_ref, edge_a, edge_b, rain_ref, onehot_ref, lo_ref, sem,
-):
+def main_kernel(peers, levels, wet, *refs):
     total = 3 * levels + 4
     high = peers * 32
     step = pl.program_id(0)
     steps = pl.num_programs(0)
-    fetch = pltpu.make_async_copy(onehot_hbm, onehot_ref, sem)
+    if wet:
+        damping_ref, exner_ref, scale_ref, mass_ref, theta_ref, vapor_ref, cloud_ref = refs[:7]
+        onehot_ref = refs[7]
+        theta_out, vapor_out, cloud_out, send_out = refs[18:22]
+        coef_ref, edge_a, edge_b, rain_ref, lo_ref = refs[22:]
+        halo_refs = refs[8:18]
+    else:
+        damping_ref, div_ref = refs[:2]
+        halo_refs = refs[2:12]
+        div_out, coef_ref, edge_a, edge_b = refs[12:]
+    edge_ref, inv_ref, below_ref, above_ref, colr_ref, coll_ref = halo_refs[:6]
+    ownl_ref, ownr_ref, corner_below, corner_above = halo_refs[6:]
+    kinds = (0, 1) if wet else (2,)
 
     sub = lax.broadcasted_iota(jnp.int32, (8, 256), 0)
     sub_half = sub[:, :LANES]
@@ -156,7 +162,6 @@
 
     @pl.when(step == 0)
     def _():
-        fetch.start()
         lane24 = lax.broadcasted_iota(jnp.int32, (24, LANES), 1)
         even = (lane24 & 1) == 0
 
@@ -178,7 +183,7 @@
             o_r = packed(ownr_ref, inner(below_ref, 3 + field), inner(above_ref, 3 + field), cols)
             return v_r, v_l, o_l, o_r
 
-        packs = [side_packs(field) for field in range(3)]
+        packs = {field: side_packs(field) for field in {0, *kinds}}
         geo = []
         for g in range(4):
             slot = levels + g
@@ -203,7 +208,8 @@
         shifted = (c0, c1, c2, behind(c3), ahead(c4), behind(c5), ahead(c6))
         for k, c in enumerate(shifted):
             coef_ref[k] = c[:, :256]
-        rain_ref[...] = jnp.zeros_like(rain_ref)
+        if wet:
+            rain_ref[...] = jnp.zeros_like(rain_ref)
 
         def pick(c, col):
             return jnp.broadcast_to(c[:, col : col + 1], (24, LANES))
@@ -214,7 +220,7 @@
         x3 = jnp.where(even, pick(c3, 255), pick(c4, 0))
         x5 = jnp.where(even, pick(c5, 255), 0.0)
         x6 = jnp.where(even, 0.0, pick(c6, 0))
-        for field in range(3):
+        for field in kinds:
             v_r, v_l, o_l, o_r = packs[field]
             v = jnp.where(even, v_r, v_l)
             v_up = up(v)
@@ -261,9 +267,13 @@
         rate = damping_ref[field, l]
         return [centre[h] - rate * second[h] for h in range(2)]
 
-    def level(k):
+    def dry(k):
+        div = damp(div_ref, k, 2, step * BLOCK_LEVELS + k)
+        for h in range(2):
+            div_out[k, :, h * LANES : (h + 1) * LANES] = div[h]
+
+    def moist(k):
         l = step * BLOCK_LEVELS + k
-        div = damp(div_ref, k, 2, l)
         thetas = damp(theta_ref, k, 0, l)
         vapors = damp(vapor_ref, k, 1, l)
         exner = exner_ref[l]
@@ -273,7 +283,6 @@
         for h in range(2):
             cols = slice(h * LANES, (h + 1) * LANES)
             theta, vapor = thetas[h], vapors[h]
-            div_out[k, :, cols] = div[h]
             cloud = cloud_ref[k, :, cols]
             temper = theta * exner
             saturation = scale * jnp.exp(temper)
@@ -290,15 +299,17 @@
 
     def body(m, carry):
         for j in range(UNROLL):
-            level(m * UNROLL + j)
+            (moist if wet else dry)(m * UNROLL + j)
         return carry
 
     count = jnp.minimum(BLOCK_LEVELS, levels - step * BLOCK_LEVELS)
     lax.fori_loop(0, lax.div(count, UNROLL), body, 0)
 
+    if not wet:
+        return
+
     @pl.when(step == steps - 1)
     def _():
-        fetch.wait()
         for r in range(16):
             value = rain_ref[r : r + 1, :]
             coarse = value.astype(jnp.bfloat16)
@@ -316,37 +327,51 @@
         send_out[...] = placed[:, :LANES] + placed[:, LANES:]
 
 
-def physics(peers, scalars, fields, whole_args, marks, halos):
+SMEM = pl.BlockSpec(memory_space=pltpu.SMEM)
+VMEM = pl.BlockSpec(memory_space=pltpu.VMEM)
+
+
+def whole(a):
+    return pl.BlockSpec(a.shape, lambda s: (0,) * len(a.shape))
+
+
+def update(peers, wet, scalars, fields, marks, geometry, halos):
     levels = fields[0].shape[0]
-    steps = pl.cdiv(levels, BLOCK_LEVELS)
     high = peers * 32
     block = pl.BlockSpec((BLOCK_LEVELS, 16, 256), lambda s: (s, 0, 0))
-    whole = lambda a: pl.BlockSpec(a.shape, lambda s: (0,) * len(a.shape))
     field = jax.ShapeDtypeStruct(fields[0].shape, jnp.float32)
     sent = jax.ShapeDtypeStruct((high, LANES), jnp.float32)
+    scratch = [
+        pltpu.VMEM((7, 24, 256), jnp.float32),
+        pltpu.VMEM((3, 24, LANES), jnp.float32),
+        pltpu.VMEM((3, 24, LANES), jnp.float32),
+    ]
+    out_shape = [field] * len(fields)
+    out_specs = [block] * len(fields)
+    if wet:
+        out_shape.append(sent)
+        out_specs.append(whole(sent))
+        scratch.append(pltpu.VMEM((16, 256), jnp.float32))
+        scratch.append(pltpu.VMEM((2 * LANES, 4096), jnp.bfloat16))
     return pl.pallas_call(
-        functools.partial(main_kernel, peers, levels),
-        grid=(steps,),
-        in_specs=[pl.BlockSpec(memory_space=pltpu.SMEM)] * 4
-        + [block] * 4
-        + [whole(a) for a in whole_args]
-        + [pl.BlockSpec(memory_space=pl.ANY)]
-        + [pl.BlockSpec(memory_space=pltpu.VMEM)] * 4
+        functools.partial(main_kernel, peers, levels, wet),
+        grid=(pl.cdiv(levels, BLOCK_LEVELS),),
+        in_specs=[SMEM] * len(scalars)
+        + [block] * len(fields)
+        + [VMEM] * len(marks)
+        + [whole(a) for a in geometry]
+        + [VMEM] * 4
         + [whole(a) for a in halos[4:6]]
-        + [pl.BlockSpec(memory_space=pltpu.VMEM)] * 2,
-        out_specs=[block, block, block, block, whole(sent)],
-        out_shape=[field, field, field, field, sent],
-        scratch_shapes=[
-            pltpu.VMEM((7, 24, 256), jnp.float32),
-            pltpu.VMEM((3, 24, LANES), jnp.float32),
-            pltpu.VMEM((3, 24, LANES), jnp.float32),
-            pltpu.VMEM((16, 256), jnp.float32),
-            pltpu.VMEM((high + LANES, 4096), jnp.bfloat16),
-            pltpu.VMEM((2 * LANES, 4096), jnp.bfloat16),
-            pltpu.SemaphoreType.DMA(()),
-        ],
-        name="physics",
-    )(*scalars, *fields, *whole_args, marks, *halos)
+        + [VMEM] * 2,
+        out_specs=out_specs,
+        out_shape=out_shape,
+        scratch_shapes=scratch,
+        name="moist" if wet else "dry",
+        compiler_params=pltpu.CompilerParams(vmem_limit_bytes=32 * 2**20),
+        cost_estimate=pl.CostEstimate(
+            flops=10**8 * len(fields), transcendentals=0, bytes_accessed=2 * 2**20 * len(fields)
+        ),
+    )(*scalars, *fields, *marks, *geometry, *halos)
 
 
 def on_device(
@@ -375,6 +400,8 @@
     coll = fetch(right, "py", -1)
     below = fetch(top, "px", 1)
     above = fetch(bot, "px", -1)
+    marks = pltpu.with_memory_space_constraint(onehot(span_of, peers * 32), pltpu.VMEM)
+    colr, coll, marks = lax.optimization_barrier((colr, coll, marks))
     sides = jnp.concatenate([colr, coll], axis=1)
     corner_below = fetch(sides[:8], "px", 1)
     corner_above = fetch(sides[8:], "px", -1)
@@ -382,16 +409,21 @@
         pltpu.with_memory_space_constraint(x, pltpu.VMEM)
         for x in (below, above, colr, coll, corner_below, corner_above)
     )
-    marks = onehot(span_of, peers * 32)
-    theta_next, vapor_next, cloud_next, divergence_next, send = physics(
+    halos = halos[:4] + (left, right) + halos[4:]
+    geometry = (edge, inv_area)
+    theta_next, vapor_next, cloud_next, send = update(
         peers,
+        True,
         (damping, exner, sat_scale, layer_mass),
-        (theta, vapor, cloud, divergence),
-        (edge, inv_area),
-        marks,
-        halos[:4] + (left, right) + halos[4:],
+        (theta, vapor, cloud),
+        (marks,),
+        geometry,
+        halos,
     )
     got = lax.all_to_all(send.reshape(peers, 32, LANES), "py", split_axis=0, concat_axis=0, tiled=True)
+    (divergence_next,) = update(
+        peers, False, (damping,), (divergence,), (), geometry, halos
+    )
     precip = jnp.sum(got, axis=0).reshape(1, 4096)
     return (theta_next, vapor_next, cloud_next, divergence_next, precip)
 

time: 50.9 us -> 51.2 us (level)
  blocking collectives: 12.2 us -> 0 us
  starting transfers between devices: 11.5 us -> 16.9 us
  local copies, waits for them, and re-layouts: 0.01 us -> 5.14 us
  waiting for transfers between devices: 5.44 us -> 6.95 us
    all_to_all x1 -> x0, blocking collectives: 12.2 us -> none  [on_device(): lax.all_to_all(send.reshape(peers, 32, LANES), 'py', split_axis=0, concat...]
    all_to_all x0 -> x1, starting transfers between devices: none -> 5.41 us  [on_device(): lax.all_to_all(send.reshape(peers, 32, LANES), 'py', split_axis=0, concat...]
    unnamed x1 -> x31, local copies, waits for them, and re-layouts: 0.01 us -> 5.13 us
    pallas_call x1 -> x2, Pallas kernels: 13.2 us -> 18.2 us  [update(): pl.pallas_call(functools.partial(main_kernel, peers, levels, wet), grid=(...]
    pallas_call x1, Pallas kernels: 3.59 us -> 0.98 us  [pack(): pl.pallas_call(pack_kernel, grid=(1,), in_specs=sides * 3 + [whole(edge),...]
    pallas_call x1, Pallas kernels: 3.42 us -> 1.14 us  [onehot(): pl.pallas_call(functools.partial(onehot_kernel, high), grid=(2,), in_spec...]
    all_to_all x0 -> x1, waiting for transfers between devices: none -> 1.4 us  [on_device(): lax.all_to_all(send.reshape(peers, 32, LANES), 'py', split_axis=0, concat...]
  transfers between devices with their start and end apart: 6 -> 7, of which waited for: 1 -> 3; matrix products, arithmetic and copies ran while one was open for 0% -> 0% of each run, Pallas kernels for 7% -> 17%
where the time goes in v4:
time: 51.2 us; the launch traced here: 50.7 us
  Pallas kernels  20.3 us (40%)
  starting transfers between devices  16.9 us (33%)
  waiting for transfers between devices  6.95 us (14%)
  local copies, waits for them, and re-layouts  5.14 us (10%)
  between operations  0.82 us (2%)
  other arithmetic  0.63 us (1%)
    pallas_call x2, Pallas kernels, update(): pl.pallas_call(functools.partial(main_kernel, peers, levels, wet), grid=(...  18.2 us
    ppermute x6, starting transfers between devices, fetch(): lax.ppermute(x, axis, [((i + step) % count, i) for i in range(count)])  11.5 us
    ppermute x6, waiting for transfers between devices, fetch(): lax.ppermute(x, axis, [((i + step) % count, i) for i in range(count)])  5.55 us
    all_to_all x1, starting transfers between devices, on_device(): lax.all_to_all(send.reshape(peers, 32, LANES), 'py', split_axis=0, concat...  5.41 us
    unnamed x31, local copies, waits for them, and re-layouts  5.13 us
    all_to_all x1, waiting for transfers between devices, on_device(): lax.all_to_all(send.reshape(peers, 32, LANES), 'py', split_axis=0, concat...  1.4 us
    pallas_call x1, Pallas kernels, onehot(): pl.pallas_call(functools.partial(onehot_kernel, high), grid=(2,), in_spec...  1.14 us
  transfers between devices with their start and end apart: 7, of which 3 were waited for; matrix products, arithmetic and copies ran while one was open for 0% of the time, Pallas kernels for 17%

profile of v4, /device:TPU:0, one launch (start us, length us, event | category | flops | bytes accessed | tf_op | source)
XLA Modules:
  0.0 50.7 jit_solution(8283404314712991610)
XLA Ops:
  0.6 0.0 copy-start
  0.6 1.2 %copy-done = f32[58,16,256]{2,1,0:T(8,128)S(1)} copy-done((f32[58,16,256]{2,1,0:T(8,128)S(1)}, f32[58,16,256]{2,1,0:T(8,128)}, u32[]{:S(2)}) %copy-start) | copy-done | bytes 950296
  1.8 0.0 copy-start.2
  1.8 1.2 %copy-done.2 = f32[58,16,256]{2,1,0:T(8,128)S(1)} copy-done((f32[58,16,256]{2,1,0:T(8,128)S(1)}, f32[58,16,256]{2,1,0:T(8,128)}, u32[]{:S(2)}) %copy-start.2) | copy-done | bytes 950296
  3.0 0.0 copy-start.4
  3.0 1.2 %copy-done.4 = f32[58,16,256]{2,1,0:T(8,128)S(1)} copy-done((f32[58,16,256]{2,1,0:T(8,128)S(1)}, f32[58,16,256]{2,1,0:T(8,128)}, u32[]{:S(2)}) %copy-start.4) | copy-done | bytes 950296
  4.2 0.0 copy-start.6
  4.2 0.8 %copy-done.6 = f32[3,16,256]{2,1,0:T(8,128)S(1)} copy-done((f32[3,16,256]{2,1,0:T(8,128)S(1)}, f32[3,16,256]{2,1,0:T(8,128)}, u32[]{:S(2)}) %copy-start.6) | copy-done | bytes 49176
  5.0 0.0 copy-start.8
  5.0 0.7 %copy-done.8 = f32[16,256]{1,0:T(8,128)S(1)} copy-done((f32[16,256]{1,0:T(8,128)S(1)}, f32[16,256]{1,0:T(8,128)}, u32[]{:S(2)}) %copy-start.8) | copy-done | bytes 16408
  5.7 0.0 copy-start.10
  5.7 0.0 copy-start.3
  5.7 0.0 copy-start.5
  5.7 0.0 copy-start.11
  5.7 0.0 copy-start.12
  5.7 0.0 copy-start.13
  5.8 0.0 copy-start.14
  5.8 1.0 %pack.1 = (f32[384,256]{1,0:T(8,128)S(1)}, f32[384,256]{1,0:T(8,128)S(1)}, f32[16,384]{1,0:T(8,128)S(1)}, f32[16,384]{1,0:T(8,128)S(1)}) custom-call(f32[928,256]{1,0:T(8,128)S(1)} %bitcast.8, f32[928,256]{1,0:T(8,128)S(1)} %bitcast.9, f32[928,256]{1,0:T(8,128)S(1)} %bitcast.10, f32[928,256]{1,0:T(8,128)S(1)} %bitcast.11, f32[928,256]{1,0:T(8,128)S(1)} %bitcast.6, ...), custom_call_target="tpu_custom_call" | custom-call | tf_op jit(solution)/shard_map/pack/pallas_call | solution.py:73
  6.7 6.6 %collective-permute-start = (f32[16,384]{1,0:T(8,128)S(1)}, f32[16,384]{1,0:T(8,128)S(1)}, u32[]{:S(2)}, u32[]{:S(2)}) collective-permute-start(f32[16,384]{1,0:T(8,128)S(1)} %get-tuple-element.16.refs_14_.refs_8_), channel_id=1, source_target_pairs={{1,0},{2,1},{3,2},{4,3},{5,4},{6,5},{7,6},{8,7},{9,8},{10,9},{11,1... | collective-permute-start | bytes 73736 | tf_op jit(solution)/shard_map/ppermute | solution.py:394
  13.4 0.0 collective-permute-start.1
  13.4 1.9 %collective-permute-start.2 = (f32[384,256]{1,0:T(8,128)S(1)}, f32[384,256]{1,0:T(8,128)S(1)}, u32[]{:S(2)}, u32[]{:S(2)}) collective-permute-start(f32[384,256]{1,0:T(8,128)S(1)} %get-tuple-element.19), channel_id=1, source_target_pairs={{16,0},{32,16},{48,32},{64,48},{80,64},{96,80},{112,96},{0,112},{1... | collective-permute-start | bytes 1179656 | tf_op jit(solution)/shard_map/ppermute | solution.py:394
  15.3 0.0 collective-permute-start.3
  15.3 0.0 copy-done.10
  15.3 1.1 %onehot.1.refs_7_ = bf16[640,4096]{1,0:T(8,128)(2,1)S(1)} custom-call(s32[16,256]{1,0:T(8,128)S(1)} %copy-done.10), custom_call_target="tpu_custom_call" | custom-call | flops 1000000000 | bytes 5242880 | tf_op jit(solution)/shard_map/onehot/pallas_call | solution.py:104
  16.5 0.0 copy-start.1
  16.5 0.0 copy-start.7
  16.5 0.0 copy-start.9
  16.5 0.0 collective-permute-done.refs_12_.refs_6_
  16.5 4.0 %collective-permute-done.1.refs_13_.refs_7_ = f32[16,384]{1,0:T(8,128)S(1)} collective-permute-done((f32[16,384]{1,0:T(8,128)S(1)}, f32[16,384]{1,0:T(8,128)S(1)}, u32[]{:S(2)}, u32[]{:S(2)}) %collective-permute-start.1) | collective-permute-done | bytes 24608 | tf_op jit(solution)/shard_map/ppermute | solution.py:394
  20.6 0.0 collective-permute-start.5
  20.6 2.9 %collective-permute-start.4 = (f32[8,768]{1,0:T(8,128)S(1)}, f32[8,768]{1,0:T(8,128)S(1)}, u32[]{:S(2)}, u32[]{:S(2)}) collective-permute-start(f32[8,768]{1,0:T(8,128)S(1)} %get-tuple-element.28), channel_id=1, source_target_pairs={{16,0},{32,16},{48,32},{64,48},{80,64},{96,80},{112,96},{0,112},{1... | collective-permute-start | bytes 73736 | tf_op jit(solution)/shard_map/ppermute | solution.py:394
  23.5 1.5 %collective-permute-done.5.refs_17_.refs_11_ = f32[8,768]{1,0:T(8,128)S(1)} collective-permute-done((f32[8,768]{1,0:T(8,128)S(1)}, f32[8,768]{1,0:T(8,128)S(1)}, u32[]{:S(2)}, u32[]{:S(2)}) %collective-permute-start.5) | collective-permute-done | bytes 24608 | tf_op jit(solution)/shard_map/ppermute | solution.py:394
  25.0 0.0 collective-permute-done.4.refs_16_.refs_10_
  25.0 0.0 collective-permute-done.2.refs_10_.refs_4_
  25.0 0.0 collective-permute-done.3.refs_11_.refs_5_
  25.0 0.0 copy-done.3
  25.1 0.0 copy-done.5
  25.1 0.0 copy-done.11
  25.1 0.0 copy-done.12
  25.1 0.0 copy-done.13
  25.1 0.0 copy-done.14
  25.1 10.9 %moist.1 = (f32[58,16,256]{2,1,0:T(8,128)}, f32[58,16,256]{2,1,0:T(8,128)}, f32[58,16,256]{2,1,0:T(8,128)}, f32[512,128]{1,0:T(8,128)}) custom-call(f32[3,58]{1,0:T(4,128)S(1)} %copy-done.11, f32[58]{0:T(128)S(1)} %copy-done.12, f32[58]{0:T(128)S(1)} %copy-done.13, f32[58]{0:T(128)S(1)} %copy-done.14, f32[58,16,256]{2,1,0:T(8,128)S(1)} %copy-done.3, ...), custom_call_target="tpu_custom_call" | custom-call | flops 300000000 | bytes 6291456 | tf_op jit(solution)/shard_map/moist/pallas_call | solution.py:356
  36.0 5.4 %all-to-all-start = ((f32[16,32,128]{2,1,0:T(8,128)}), f32[16,32,128]{2,1,0:T(8,128)S(1)}, u32[]{:S(2)}, u32[]{:S(2)}) async-start(f32[16,32,128]{2,1,0:T(8,128)} %bitcast.4), calls=%async_computation | async-start | bytes 524288 | tf_op jit(solution)/shard_map/all_to_all | solution.py:423
  41.4 0.0 copy-done.1
  41.4 0.0 copy-done.7
  41.4 0.0 copy-done.9
  41.4 7.3 %dry.1 = f32[58,16,256]{2,1,0:T(8,128)} custom-call(f32[3,58]{1,0:T(4,128)S(1)} %copy-done.11, f32[58,16,256]{2,1,0:T(8,128)S(1)} %copy-done.1, f32[48,256]{1,0:T(8,128)S(1)} %bitcast.14, f32[16,256]{1,0:T(8,128)S(1)} %copy-done.9, f32[384,256]{1,0:T(8,128)S(1)} %collective-permute-done.2.refs_10_.refs_4_, ...), custom_call_target="tpu_custom_call" | custom-call | flops 100000000 | bytes 2097152 | tf_op jit(solution)/shard_map/dry/pallas_call | solution.py:356
  48.7 1.4 %all-to-all-done = f32[16,32,128]{2,1,0:T(8,128)S(1)} async-done(((f32[16,32,128]{2,1,0:T(8,128)}), f32[16,32,128]{2,1,0:T(8,128)S(1)}, u32[]{:S(2)}, u32[]{:S(2)}) %all-to-all-start) | async-done | bytes 262176 | tf_op jit(solution)/shard_map/all_to_all | solution.py:423
  50.1 0.6 %reduce_sum.9 = f32[32,128]{1,0:T(8,128)} reduce(f32[16,32,128]{2,1,0:T(8,128)S(1)} %all-to-all-done, f32[]{:T(128)} %constant.0.clone.1), dimensions={0}, to_apply=%region_0.0 | reduce | flops 61440 | bytes 278532 | tf_op jit(solution)/shard_map/reduce_sum | solution.py:427
  (3 shorter events, 0.0 us)
Async XLA Ops:
  0.6 1.2 %copy-start = (f32[58,16,256]{2,1,0:T(8,128)S(1)}, f32[58,16,256]{2,1,0:T(8,128)}, u32[]{:S(2)}) copy-start(f32[58,16,256]{2,1,0:T(8,128)} %refs_1_.3) | copy-start | bytes 2850820
  1.8 1.2 %copy-start.2 = (f32[58,16,256]{2,1,0:T(8,128)S(1)}, f32[58,16,256]{2,1,0:T(8,128)}, u32[]{:S(2)}) copy-start(f32[58,16,256]{2,1,0:T(8,128)} %refs_4_.1) | copy-start | bytes 2850820
  3.0 1.2 %copy-start.4 = (f32[58,16,256]{2,1,0:T(8,128)S(1)}, f32[58,16,256]{2,1,0:T(8,128)}, u32[]{:S(2)}) copy-start(f32[58,16,256]{2,1,0:T(8,128)} %refs_5_.1) | copy-start | bytes 2850820
  4.2 0.8 %copy-start.6 = (f32[3,16,256]{2,1,0:T(8,128)S(1)}, f32[3,16,256]{2,1,0:T(8,128)}, u32[]{:S(2)}) copy-start(f32[3,16,256]{2,1,0:T(8,128)} %param.15) | copy-start | bytes 147460
  5.0 0.7 %copy-start.8 = (f32[16,256]{1,0:T(8,128)S(1)}, f32[16,256]{1,0:T(8,128)}, u32[]{:S(2)}) copy-start(f32[16,256]{1,0:T(8,128)} %refs_3_.3) | copy-start | bytes 49156
  5.7 9.6 %copy-start.10 = (s32[16,256]{1,0:T(8,128)S(1)}, s32[16,256]{1,0:T(8,128)}, u32[]{:S(2)}) copy-start(s32[16,256]{1,0:T(8,128)} %span_ref.1) | copy-start | bytes 49156
  5.7 19.3 %copy-start.3 = (f32[58,16,256]{2,1,0:T(8,128)S(1)}, f32[58,16,256]{2,1,0:T(8,128)}, u32[]{:S(2)}) copy-start(f32[58,16,256]{2,1,0:T(8,128)} %refs_4_.1) | copy-start | bytes 2850820
  5.7 19.3 %copy-start.5 = (f32[58,16,256]{2,1,0:T(8,128)S(1)}, f32[58,16,256]{2,1,0:T(8,128)}, u32[]{:S(2)}) copy-start(f32[58,16,256]{2,1,0:T(8,128)} %refs_6_.1) | copy-start | bytes 2850820
  5.7 19.3 %copy-start.11 = (f32[3,58]{1,0:T(4,128)S(1)}, f32[3,58]{1,0:T(4,128)}, u32[]{:S(2)}) copy-start(f32[3,58]{1,0:T(4,128)} %refs_0_.3) | copy-start | bytes 2092
  5.7 19.3 %copy-start.12 = (f32[58]{0:T(128)S(1)}, f32[58]{0:T(128)}, u32[]{:S(2)}) copy-start(f32[58]{0:T(128)} %refs_1_.2) | copy-start | bytes 700
  5.7 19.3 %copy-start.13 = (f32[58]{0:T(128)S(1)}, f32[58]{0:T(128)}, u32[]{:S(2)}) copy-start(f32[58]{0:T(128)} %refs_2_.1) | copy-start | bytes 700
  5.8 19.3 %copy-start.14 = (f32[58]{0:T(128)S(1)}, f32[58]{0:T(128)}, u32[]{:S(2)}) copy-start(f32[58]{0:T(128)} %refs_3_.2) | copy-start | bytes 700
  6.7 9.8 %collective-permute-start = (f32[16,384]{1,0:T(8,128)S(1)}, f32[16,384]{1,0:T(8,128)S(1)}, u32[]{:S(2)}, u32[]{:S(2)}) collective-permute-start(f32[16,384]{1,0:T(8,128)S(1)} %get-tuple-element.16.refs_14_.refs_8_), channel_id=1, source_target_pairs={{1,0},{2,1},{3,2},{4,3},{5,4},{6,5},{7,6},{8,7},{9,8},{10,9},{11,1... | collective-permute-start | bytes 73736 | tf_op jit(solution)/shard_map/ppermute | solution.py:394
  13.4 7.1 %collective-permute-start.1 = (f32[16,384]{1,0:T(8,128)S(1)}, f32[16,384]{1,0:T(8,128)S(1)}, u32[]{:S(2)}, u32[]{:S(2)}) collective-permute-start(f32[16,384]{1,0:T(8,128)S(1)} %get-tuple-element.17.refs_15_.refs_9_), channel_id=1, source_target_pairs={{15,0},{0,1},{1,2},{2,3},{3,4},{4,5},{5,6},{6,7},{7,8},{8,9},{9,10... | collective-permute-start | bytes 73736 | tf_op jit(solution)/shard_map/ppermute | solution.py:394
  13.4 11.7 %collective-permute-start.2 = (f32[384,256]{1,0:T(8,128)S(1)}, f32[384,256]{1,0:T(8,128)S(1)}, u32[]{:S(2)}, u32[]{:S(2)}) collective-permute-start(f32[384,256]{1,0:T(8,128)S(1)} %get-tuple-element.19), channel_id=1, source_target_pairs={{16,0},{32,16},{48,32},{64,48},{80,64},{96,80},{112,96},{0,112},{1... | collective-permute-start | bytes 1179656 | tf_op jit(solution)/shard_map/ppermute | solution.py:394
  15.3 9.7 %collective-permute-start.3 = (f32[384,256]{1,0:T(8,128)S(1)}, f32[384,256]{1,0:T(8,128)S(1)}, u32[]{:S(2)}, u32[]{:S(2)}) collective-permute-start(f32[384,256]{1,0:T(8,128)S(1)} %get-tuple-element.20), channel_id=1, source_target_pairs={{112,0},{0,16},{16,32},{32,48},{48,64},{64,80},{80,96},{96,112},{1... | collective-permute-start | bytes 1179656 | tf_op jit(solution)/shard_map/ppermute | solution.py:394
  16.5 25.0 %copy-start.1 = (f32[58,16,256]{2,1,0:T(8,128)S(1)}, f32[58,16,256]{2,1,0:T(8,128)}, u32[]{:S(2)}) copy-start(f32[58,16,256]{2,1,0:T(8,128)} %refs_1_.3) | copy-start | bytes 2850820
  16.5 25.0 %copy-start.7 = (f32[3,16,256]{2,1,0:T(8,128)S(1)}, f32[3,16,256]{2,1,0:T(8,128)}, u32[]{:S(2)}) copy-start(f32[3,16,256]{2,1,0:T(8,128)} %param.15) | copy-start | bytes 147460
  16.5 25.0 %copy-start.9 = (f32[16,256]{1,0:T(8,128)S(1)}, f32[16,256]{1,0:T(8,128)}, u32[]{:S(2)}) copy-start(f32[16,256]{1,0:T(8,128)} %refs_3_.3) | copy-start | bytes 49156
  20.6 4.5 %collective-permute-start.5 = (f32[8,768]{1,0:T(8,128)S(1)}, f32[8,768]{1,0:T(8,128)S(1)}, u32[]{:S(2)}, u32[]{:S(2)}) collective-permute-start(f32[8,768]{1,0:T(8,128)S(1)} %get-tuple-element.27), channel_id=1, source_target_pairs={{112,0},{0,16},{16,32},{32,48},{48,64},{64,80},{80,96},{96,112},{1... | collective-permute-start | bytes 73736 | tf_op jit(solution)/shard_map/ppermute | solution.py:394
  20.6 4.5 %collective-permute-start.4 = (f32[8,768]{1,0:T(8,128)S(1)}, f32[8,768]{1,0:T(8,128)S(1)}, u32[]{:S(2)}, u32[]{:S(2)}) collective-permute-start(f32[8,768]{1,0:T(8,128)S(1)} %get-tuple-element.28), channel_id=1, source_target_pairs={{16,0},{32,16},{48,32},{64,48},{80,64},{96,80},{112,96},{0,112},{1... | collective-permute-start | bytes 73736 | tf_op jit(solution)/shard_map/ppermute | solution.py:394
  36.0 14.1 %all-to-all-start = ((f32[16,32,128]{2,1,0:T(8,128)}), f32[16,32,128]{2,1,0:T(8,128)S(1)}, u32[]{:S(2)}, u32[]{:S(2)}) async-start(f32[16,32,128]{2,1,0:T(8,128)} %bitcast.4), calls=%async_computation | async-start | bytes 524288 | tf_op jit(solution)/shard_map/all_to_all | solution.py:423

commit v5 on v4

--- a/solution.py
+++ b/solution.py
@@ -13,23 +13,33 @@
 
 LANES = 128
 BLOCK_LEVELS = 16
-UNROLL = 2
+WET_UNROLL = 4
+DRY_UNROLL = 2
 
 
 def pack_kernel(
-    theta0, theta1, vapor0, vapor1, div0, div1, edge_ref, inv_ref,
+    theta_hbm, vapor_hbm, div_hbm, edge_hbm, inv_hbm,
     top_ref, bot_ref, left_ref, right_ref,
+    theta0, theta1, vapor0, vapor1, div0, div1, edge_ref, inv_ref, sems,
 ):
     levels = theta0.shape[0] // 16
     total = 3 * levels + 4
     fields = ((theta0, theta1), (vapor0, vapor1), (div0, div1))
+    copies = []
+    for field, source in enumerate((theta_hbm, vapor_hbm, div_hbm)):
+        for half, ref in enumerate(fields[field]):
+            part = source.at[:, half * LANES : (half + 1) * LANES]
+            copies.append(pltpu.make_async_copy(part, ref, sems.at[2 * field + half]))
+    geometry = [
+        pltpu.make_async_copy(edge_hbm, edge_ref, sems.at[6]),
+        pltpu.make_async_copy(inv_hbm, inv_ref, sems.at[7]),
+    ]
+    for copy in geometry + copies:
+        copy.start()
+    for copy in geometry:
+        copy.wait()
     for out_ref, first in ((top_ref, 0), (bot_ref, 14)):
         for row in range(2):
-            for field, halves in enumerate(fields):
-                at = pl.ds(row * total + field * levels, levels)
-                for half, ref in enumerate(halves):
-                    cols = slice(half * LANES, (half + 1) * LANES)
-                    out_ref[at, cols] = ref[pl.ds(first + row, levels, stride=16), :]
             for g in range(3):
                 out_ref[pl.ds(row * total + 3 * levels + g, 1), :] = edge_ref[
                     pl.ds(16 * g + first + row, 1), :
@@ -44,6 +54,13 @@
 
     for field, halves in enumerate(fields):
         for side in range(2):
+            copies[2 * field + side].wait()
+            cols = slice(side * LANES, (side + 1) * LANES)
+            for out_ref, first in ((top_ref, 0), (bot_ref, 14)):
+                for row in range(2):
+                    out_ref[pl.ds(row * total + field * levels, levels), cols] = halves[side][
+                        pl.ds(first + row, levels, stride=16), :
+                    ]
             acc = jnp.zeros((16, LANES), jnp.float32)
             for l in range(levels):
                 acc = place(acc, halves[side][16 * l : 16 * l + 16, :], l, side)
@@ -67,18 +84,22 @@
     total = 3 * levels + 4
     rows = jax.ShapeDtypeStruct((2 * total + 28, 256), jnp.float32)
     cols = jax.ShapeDtypeStruct((16, 3 * LANES), jnp.float32)
-    sides = [pl.BlockSpec((16 * levels, LANES), lambda s, c=c: (0, c)) for c in range(2)]
-    whole = lambda a: pl.BlockSpec(a.shape, lambda s: (0,) * len(a.shape))
     outs = (rows, rows, cols, cols)
+    vmem = pl.BlockSpec(memory_space=pltpu.VMEM)
     return pl.pallas_call(
         pack_kernel,
-        grid=(1,),
-        in_specs=sides * 3 + [whole(edge), whole(inv)],
-        out_specs=[whole(o) for o in outs],
+        in_specs=[pl.BlockSpec(memory_space=pltpu.HBM)] * 5,
+        out_specs=[vmem] * 4,
         out_shape=outs,
+        scratch_shapes=[pltpu.VMEM((16 * levels, LANES), jnp.float32)] * 6
+        + [
+            pltpu.VMEM(edge.shape, jnp.float32),
+            pltpu.VMEM(inv.shape, jnp.float32),
+            pltpu.SemaphoreType.DMA((8,)),
+        ],
         name="pack",
         compiler_params=pltpu.CompilerParams(vmem_limit_bytes=32 * 2**20),
-    )(theta, theta, vapor, vapor, divergence, divergence, edge, inv)
+    )(theta, vapor, divergence, edge, inv)
 
 
 def onehot_kernel(high, span_ref, out_ref):
@@ -297,13 +318,21 @@
             cloud_out[k, :, cols] = liquid - rained
             rain_ref[:, cols] += mass * rained
 
-    def body(m, carry):
-        for j in range(UNROLL):
-            (moist if wet else dry)(m * UNROLL + j)
-        return carry
-
     count = jnp.minimum(BLOCK_LEVELS, levels - step * BLOCK_LEVELS)
-    lax.fori_loop(0, lax.div(count, UNROLL), body, 0)
+    unroll = WET_UNROLL if wet else DRY_UNROLL
+
+    def sweep(start, stop, width):
+        def body(m, carry):
+            for j in range(width):
+                (moist if wet else dry)(m * width + j)
+            return carry
+
+        lax.fori_loop(start, stop, body, 0)
+
+    full = lax.div(count, unroll)
+    sweep(0, full, unroll)
+    if unroll > 2:
+        sweep(full * (unroll // 2), lax.div(count, 2), 2)
 
     if not wet:
         return
@@ -395,7 +424,12 @@
 
     flat = lambda x: x.reshape(-1, 256)
     edge = flat(edge_weight)
-    top, bot, left, right = pack(flat(theta), flat(vapor), flat(divergence), edge, inv_area)
+    top, bot, left, right = pack(
+        *(
+            pltpu.with_memory_space_constraint(flat(x), pltpu.HBM)
+            for x in (theta, vapor, divergence, edge_weight, inv_area)
+        )
+    )
     colr = fetch(left, "py", 1)
     coll = fetch(right, "py", -1)
     below = fetch(top, "px", 1)

time: 51.2 us -> 46.2 us (0.902)
  local copies, waits for them, and re-layouts: 5.14 us -> 0.77 us
  waiting for transfers between devices: 6.95 us -> 6.28 us
    unnamed x31 -> x23, local copies, waits for them, and re-layouts: 5.13 us -> 0.76 us
    pallas_call x1, Pallas kernels: 0.98 us -> 2.58 us  [pack(): pl.pallas_call(pack_kernel, in_specs=[pl.BlockSpec(memory_space=pltpu.HBM...]
    pallas_call x2, Pallas kernels: 18.2 us -> 16.7 us  [update(): pl.pallas_call(functools.partial(main_kernel, peers, levels, wet), grid=(...]
    ppermute x6, waiting for transfers between devices: 5.55 us -> 4.86 us  [fetch(): lax.ppermute(x, axis, [((i + step) % count, i) for i in range(count)])]
  transfers between devices with their start and end apart: 7 -> 7, of which waited for: 3 -> 3; matrix products, arithmetic and copies ran while one was open for 0% -> 0% of each run, Pallas kernels for 17% -> 18%
where the time goes in v5:
time: 46.2 us; the launch traced here: 45.8 us
  Pallas kernels  20.4 us (44%)
  starting transfers between devices  16.9 us (37%)
  waiting for transfers between devices  6.28 us (14%)
  between operations  0.84 us (2%)
  local copies, waits for them, and re-layouts  0.77 us (2%)
  other arithmetic  0.63 us (1%)
    pallas_call x2, Pallas kernels, update(): pl.pallas_call(functools.partial(main_kernel, peers, levels, wet), grid=(...  16.7 us
    ppermute x6, starting transfers between devices, fetch(): lax.ppermute(x, axis, [((i + step) % count, i) for i in range(count)])  11.5 us
    all_to_all x1, starting transfers between devices, on_device(): lax.all_to_all(send.reshape(peers, 32, LANES), 'py', split_axis=0, concat...  5.41 us
    ppermute x6, waiting for transfers between devices, fetch(): lax.ppermute(x, axis, [((i + step) % count, i) for i in range(count)])  4.86 us
    pallas_call x1, Pallas kernels, pack(): pl.pallas_call(pack_kernel, in_specs=[pl.BlockSpec(memory_space=pltpu.HBM...  2.58 us
    all_to_all x1, waiting for transfers between devices, on_device(): lax.all_to_all(send.reshape(peers, 32, LANES), 'py', split_axis=0, concat...  1.42 us
    pallas_call x1, Pallas kernels, onehot(): pl.pallas_call(functools.partial(onehot_kernel, high), grid=(2,), in_spec...  1.14 us
  transfers between devices with their start and end apart: 7, of which 3 were waited for; matrix products, arithmetic and copies ran while one was open for 0% of the time, Pallas kernels for 18%

profile of v5, /device:TPU:0, one launch (start us, length us, event | category | flops | bytes accessed | tf_op | source)
XLA Modules:
  0.0 45.8 jit_solution(5559644940823396769)
XLA Ops:
  0.6 0.0 copy-start.5
  0.6 0.0 copy-start.1
  0.7 0.0 copy-start.2
  0.7 0.0 copy-start.4
  0.7 0.0 copy-start.7
  0.7 0.0 copy-start.10
  0.7 0.0 copy-start.9
  0.7 0.0 copy-start.8
  0.7 0.0 copy-start.3
  0.7 2.6 %pack.1 = (f32[384,256]{1,0:T(8,128)S(1)}, f32[384,256]{1,0:T(8,128)S(1)}, f32[16,384]{1,0:T(8,128)S(1)}, f32[16,384]{1,0:T(8,128)S(1)}) custom-call(f32[928,256]{1,0:T(8,128)} %bitcast.7, f32[928,256]{1,0:T(8,128)} %bitcast.8, f32[928,256]{1,0:T(8,128)} %bitcast.6, f32[48,256]{1,0:T(8,128)} %bitcast.9, f32[16,256]{1,0:T(8,128)} %refs_3_.3), custom_call_target="tpu_custom_call" | custom-call | tf_op jit(solution)/shard_map/pack/pallas_call | solution.py:89
  3.3 6.6 %collective-permute-start = (f32[16,384]{1,0:T(8,128)S(1)}, f32[16,384]{1,0:T(8,128)S(1)}, u32[]{:S(2)}, u32[]{:S(2)}) collective-permute-start(f32[16,384]{1,0:T(8,128)S(1)} %get-tuple-element.16.refs_14_.refs_8_), channel_id=1, source_target_pairs={{1,0},{2,1},{3,2},{4,3},{5,4},{6,5},{7,6},{8,7},{9,8},{10,9},{11,1... | collective-permute-start | bytes 73736 | tf_op jit(solution)/shard_map/ppermute | solution.py:423
  10.0 0.0 collective-permute-start.1
  10.0 1.9 %collective-permute-start.2 = (f32[384,256]{1,0:T(8,128)S(1)}, f32[384,256]{1,0:T(8,128)S(1)}, u32[]{:S(2)}, u32[]{:S(2)}) collective-permute-start(f32[384,256]{1,0:T(8,128)S(1)} %get-tuple-element.19), channel_id=1, source_target_pairs={{16,0},{32,16},{48,32},{64,48},{80,64},{96,80},{112,96},{0,112},{1... | collective-permute-start | bytes 1179656 | tf_op jit(solution)/shard_map/ppermute | solution.py:423
  11.9 0.0 collective-permute-start.3
  11.9 0.0 copy-start.6
  11.9 0.7 %copy-done.6 = s32[16,256]{1,0:T(8,128)S(1)} copy-done((s32[16,256]{1,0:T(8,128)S(1)}, s32[16,256]{1,0:T(8,128)}, u32[]{:S(2)}) %copy-start.6) | copy-done | bytes 16408
  12.6 1.1 %onehot.1.refs_7_ = bf16[640,4096]{1,0:T(8,128)(2,1)S(1)} custom-call(s32[16,256]{1,0:T(8,128)S(1)} %copy-done.6), custom_call_target="tpu_custom_call" | custom-call | flops 1000000000 | bytes 5242880 | tf_op jit(solution)/shard_map/onehot/pallas_call | solution.py:125
  13.7 0.0 copy-start
  13.8 0.0 collective-permute-done.refs_12_.refs_6_
  13.8 3.3 %collective-permute-done.1.refs_13_.refs_7_ = f32[16,384]{1,0:T(8,128)S(1)} collective-permute-done((f32[16,384]{1,0:T(8,128)S(1)}, f32[16,384]{1,0:T(8,128)S(1)}, u32[]{:S(2)}, u32[]{:S(2)}) %collective-permute-start.1) | collective-permute-done | bytes 24608 | tf_op jit(solution)/shard_map/ppermute | solution.py:423
  17.1 0.0 collective-permute-start.5
  17.1 2.9 %collective-permute-start.4 = (f32[8,768]{1,0:T(8,128)S(1)}, f32[8,768]{1,0:T(8,128)S(1)}, u32[]{:S(2)}, u32[]{:S(2)}) collective-permute-start(f32[8,768]{1,0:T(8,128)S(1)} %get-tuple-element.28), channel_id=1, source_target_pairs={{16,0},{32,16},{48,32},{64,48},{80,64},{96,80},{112,96},{0,112},{1... | collective-permute-start | bytes 73736 | tf_op jit(solution)/shard_map/ppermute | solution.py:423
  20.1 1.5 %collective-permute-done.5.refs_17_.refs_11_ = f32[8,768]{1,0:T(8,128)S(1)} collective-permute-done((f32[8,768]{1,0:T(8,128)S(1)}, f32[8,768]{1,0:T(8,128)S(1)}, u32[]{:S(2)}, u32[]{:S(2)}) %collective-permute-start.5) | collective-permute-done | bytes 24608 | tf_op jit(solution)/shard_map/ppermute | solution.py:423
  21.6 0.0 collective-permute-done.4.refs_16_.refs_10_
  21.6 0.0 collective-permute-done.2.refs_10_.refs_4_
  21.6 0.0 collective-permute-done.3.refs_11_.refs_5_
  21.6 0.0 copy-done.5
  21.6 0.0 copy-done.1
  21.6 0.0 copy-done.2
  21.6 0.0 copy-done.4
  21.6 0.0 copy-done.7
  21.7 0.0 copy-done.10
  21.7 0.0 copy-done.9
  21.7 0.0 copy-done.8
  21.7 0.0 copy-done.3
  21.7 9.4 %moist.1 = (f32[58,16,256]{2,1,0:T(8,128)}, f32[58,16,256]{2,1,0:T(8,128)}, f32[58,16,256]{2,1,0:T(8,128)}, f32[512,128]{1,0:T(8,128)}) custom-call(f32[3,58]{1,0:T(4,128)S(1)} %copy-done.7, f32[58]{0:T(128)S(1)} %copy-done.8, f32[58]{0:T(128)S(1)} %copy-done.9, f32[58]{0:T(128)S(1)} %copy-done.10, f32[58,16,256]{2,1,0:T(8,128)S(1)} %copy-done.1, ...), custom_call_target="tpu_custom_call" | custom-call | flops 300000000 | bytes 6291456 | tf_op jit(solution)/shard_map/moist/pallas_call | solution.py:385
  31.1 5.4 %all-to-all-start = ((f32[16,32,128]{2,1,0:T(8,128)}), f32[16,32,128]{2,1,0:T(8,128)S(1)}, u32[]{:S(2)}, u32[]{:S(2)}) async-start(f32[16,32,128]{2,1,0:T(8,128)} %bitcast.4), calls=%async_computation | async-start | bytes 524288 | tf_op jit(solution)/shard_map/all_to_all | solution.py:457
  36.5 0.0 copy-done
  36.5 7.3 %dry.1 = f32[58,16,256]{2,1,0:T(8,128)} custom-call(f32[3,58]{1,0:T(4,128)S(1)} %copy-done.7, f32[58,16,256]{2,1,0:T(8,128)S(1)} %copy-done, f32[48,256]{1,0:T(8,128)S(1)} %bitcast.11, f32[16,256]{1,0:T(8,128)S(1)} %copy-done.5, f32[384,256]{1,0:T(8,128)S(1)} %collective-permute-done.2.refs_10_.refs_4_, ...), custom_call_target="tpu_custom_call" | custom-call | flops 100000000 | bytes 2097152 | tf_op jit(solution)/shard_map/dry/pallas_call | solution.py:385
  43.8 1.4 %all-to-all-done = f32[16,32,128]{2,1,0:T(8,128)S(1)} async-done(((f32[16,32,128]{2,1,0:T(8,128)}), f32[16,32,128]{2,1,0:T(8,128)S(1)}, u32[]{:S(2)}, u32[]{:S(2)}) %all-to-all-start) | async-done | bytes 262176 | tf_op jit(solution)/shard_map/all_to_all | solution.py:457
  45.2 0.6 %reduce_sum.9 = f32[32,128]{1,0:T(8,128)} reduce(f32[16,32,128]{2,1,0:T(8,128)S(1)} %all-to-all-done, f32[]{:T(128)} %constant.0.clone.1), dimensions={0}, to_apply=%region_0.0 | reduce | flops 61440 | bytes 278532 | tf_op jit(solution)/shard_map/reduce_sum | solution.py:461
  (3 shorter events, 0.0 us)
Async XLA Ops:
  0.6 21.0 %copy-start.5 = (f32[16,256]{1,0:T(8,128)S(1)}, f32[16,256]{1,0:T(8,128)}, u32[]{:S(2)}) copy-start(f32[16,256]{1,0:T(8,128)} %refs_3_.3) | copy-start | bytes 49156
  0.6 21.0 %copy-start.1 = (f32[58,16,256]{2,1,0:T(8,128)S(1)}, f32[58,16,256]{2,1,0:T(8,128)}, u32[]{:S(2)}) copy-start(f32[58,16,256]{2,1,0:T(8,128)} %refs_4_.1) | copy-start | bytes 2850820
  0.7 21.0 %copy-start.2 = (f32[58,16,256]{2,1,0:T(8,128)S(1)}, f32[58,16,256]{2,1,0:T(8,128)}, u32[]{:S(2)}) copy-start(f32[58,16,256]{2,1,0:T(8,128)} %refs_5_.1) | copy-start | bytes 2850820
  0.7 21.0 %copy-start.4 = (f32[3,16,256]{2,1,0:T(8,128)S(1)}, f32[3,16,256]{2,1,0:T(8,128)}, u32[]{:S(2)}) copy-start(f32[3,16,256]{2,1,0:T(8,128)} %param.15) | copy-start | bytes 147460
  0.7 21.0 %copy-start.7 = (f32[3,58]{1,0:T(4,128)S(1)}, f32[3,58]{1,0:T(4,128)}, u32[]{:S(2)}) copy-start(f32[3,58]{1,0:T(4,128)} %refs_0_.3) | copy-start | bytes 2092
  0.7 21.0 %copy-start.10 = (f32[58]{0:T(128)S(1)}, f32[58]{0:T(128)}, u32[]{:S(2)}) copy-start(f32[58]{0:T(128)} %refs_3_.2) | copy-start | bytes 700
  0.7 21.0 %copy-start.9 = (f32[58]{0:T(128)S(1)}, f32[58]{0:T(128)}, u32[]{:S(2)}) copy-start(f32[58]{0:T(128)} %refs_2_.1) | copy-start | bytes 700
  0.7 21.0 %copy-start.8 = (f32[58]{0:T(128)S(1)}, f32[58]{0:T(128)}, u32[]{:S(2)}) copy-start(f32[58]{0:T(128)} %refs_1_.2) | copy-start | bytes 700
  0.7 21.0 %copy-start.3 = (f32[58,16,256]{2,1,0:T(8,128)S(1)}, f32[58,16,256]{2,1,0:T(8,128)}, u32[]{:S(2)}) copy-start(f32[58,16,256]{2,1,0:T(8,128)} %refs_6_.1) | copy-start | bytes 2850820
  3.3 10.4 %collective-permute-start = (f32[16,384]{1,0:T(8,128)S(1)}, f32[16,384]{1,0:T(8,128)S(1)}, u32[]{:S(2)}, u32[]{:S(2)}) collective-permute-start(f32[16,384]{1,0:T(8,128)S(1)} %get-tuple-element.16.refs_14_.refs_8_), channel_id=1, source_target_pairs={{1,0},{2,1},{3,2},{4,3},{5,4},{6,5},{7,6},{8,7},{9,8},{10,9},{11,1... | collective-permute-start | bytes 73736 | tf_op jit(solution)/shard_map/ppermute | solution.py:423
  10.0 7.1 %collective-permute-start.1 = (f32[16,384]{1,0:T(8,128)S(1)}, f32[16,384]{1,0:T(8,128)S(1)}, u32[]{:S(2)}, u32[]{:S(2)}) collective-permute-start(f32[16,384]{1,0:T(8,128)S(1)} %get-tuple-element.17.refs_15_.refs_9_), channel_id=1, source_target_pairs={{15,0},{0,1},{1,2},{2,3},{3,4},{4,5},{5,6},{6,7},{7,8},{8,9},{9,10... | collective-permute-start | bytes 73736 | tf_op jit(solution)/shard_map/ppermute | solution.py:423
  10.0 11.7 %collective-permute-start.2 = (f32[384,256]{1,0:T(8,128)S(1)}, f32[384,256]{1,0:T(8,128)S(1)}, u32[]{:S(2)}, u32[]{:S(2)}) collective-permute-start(f32[384,256]{1,0:T(8,128)S(1)} %get-tuple-element.19), channel_id=1, source_target_pairs={{16,0},{32,16},{48,32},{64,48},{80,64},{96,80},{112,96},{0,112},{1... | collective-permute-start | bytes 1179656 | tf_op jit(solution)/shard_map/ppermute | solution.py:423
  11.9 9.7 %collective-permute-start.3 = (f32[384,256]{1,0:T(8,128)S(1)}, f32[384,256]{1,0:T(8,128)S(1)}, u32[]{:S(2)}, u32[]{:S(2)}) collective-permute-start(f32[384,256]{1,0:T(8,128)S(1)} %get-tuple-element.20), channel_id=1, source_target_pairs={{112,0},{0,16},{16,32},{32,48},{48,64},{64,80},{80,96},{96,112},{1... | collective-permute-start | bytes 1179656 | tf_op jit(solution)/shard_map/ppermute | solution.py:423
  11.9 0.7 %copy-start.6 = (s32[16,256]{1,0:T(8,128)S(1)}, s32[16,256]{1,0:T(8,128)}, u32[]{:S(2)}) copy-start(s32[16,256]{1,0:T(8,128)} %span_ref.1) | copy-start | bytes 49156
  13.7 22.8 %copy-start = (f32[58,16,256]{2,1,0:T(8,128)S(1)}, f32[58,16,256]{2,1,0:T(8,128)}, u32[]{:S(2)}) copy-start(f32[58,16,256]{2,1,0:T(8,128)} %refs_1_.3) | copy-start | bytes 2850820
  17.1 4.5 %collective-permute-start.5 = (f32[8,768]{1,0:T(8,128)S(1)}, f32[8,768]{1,0:T(8,128)S(1)}, u32[]{:S(2)}, u32[]{:S(2)}) collective-permute-start(f32[8,768]{1,0:T(8,128)S(1)} %get-tuple-element.27), channel_id=1, source_target_pairs={{112,0},{0,16},{16,32},{32,48},{48,64},{64,80},{80,96},{96,112},{1... | collective-permute-start | bytes 73736 | tf_op jit(solution)/shard_map/ppermute | solution.py:423
  17.1 4.5 %collective-permute-start.4 = (f32[8,768]{1,0:T(8,128)S(1)}, f32[8,768]{1,0:T(8,128)S(1)}, u32[]{:S(2)}, u32[]{:S(2)}) collective-permute-start(f32[8,768]{1,0:T(8,128)S(1)} %get-tuple-element.28), channel_id=1, source_target_pairs={{16,0},{32,16},{48,32},{64,48},{80,64},{96,80},{112,96},{0,112},{1... | collective-permute-start | bytes 73736 | tf_op jit(solution)/shard_map/ppermute | solution.py:423
  31.1 14.1 %all-to-all-start = ((f32[16,32,128]{2,1,0:T(8,128)}), f32[16,32,128]{2,1,0:T(8,128)S(1)}, u32[]{:S(2)}, u32[]{:S(2)}) async-start(f32[16,32,128]{2,1,0:T(8,128)} %bitcast.4), calls=%async_computation | async-start | bytes 524288 | tf_op jit(solution)/shard_map/all_to_all | solution.py:457

commit v6 on v5

--- a/solution.py
+++ b/solution.py
@@ -275,9 +275,9 @@
         right = (jnp.where(last, edge, a[1]) + jnp.where(zero, b[0], b[1])) + c[1]
         return left, right
 
-    def damp(ref, k, field, l):
+    def damp(ref, field, l):
         turn = lax.rem(2 * LANES - 1 - 2 * l, LANES)
-        centre = [ref[k, :, h * LANES : (h + 1) * LANES] for h in range(2)]
+        centre = [ref[l, :, h * LANES : (h + 1) * LANES] for h in range(2)]
         tiles = row_tile(field * levels + l)
         first = lap(
             [jnp.concatenate([centre[h], tiles[h]], axis=0) for h in range(2)],
@@ -289,14 +289,14 @@
         return [centre[h] - rate * second[h] for h in range(2)]
 
     def dry(k):
-        div = damp(div_ref, k, 2, step * BLOCK_LEVELS + k)
+        div = damp(div_ref, 2, step * BLOCK_LEVELS + k)
         for h in range(2):
             div_out[k, :, h * LANES : (h + 1) * LANES] = div[h]
 
     def moist(k):
         l = step * BLOCK_LEVELS + k
-        thetas = damp(theta_ref, k, 0, l)
-        vapors = damp(vapor_ref, k, 1, l)
+        thetas = damp(theta_ref, 0, l)
+        vapors = damp(vapor_ref, 1, l)
         exner = exner_ref[l]
         scale = scale_ref[l]
         mass = mass_ref[l]
@@ -304,7 +304,7 @@
         for h in range(2):
             cols = slice(h * LANES, (h + 1) * LANES)
             theta, vapor = thetas[h], vapors[h]
-            cloud = cloud_ref[k, :, cols]
+            cloud = cloud_ref[l, :, cols]
             temper = theta * exner
             saturation = scale * jnp.exp(temper)
             condensed = (vapor - saturation) / (1.0 + LATENT * saturation)
@@ -386,12 +386,7 @@
         functools.partial(main_kernel, peers, levels, wet),
         grid=(pl.cdiv(levels, BLOCK_LEVELS),),
         in_specs=[SMEM] * len(scalars)
-        + [block] * len(fields)
-        + [VMEM] * len(marks)
-        + [whole(a) for a in geometry]
-        + [VMEM] * 4
-        + [whole(a) for a in halos[4:6]]
-        + [VMEM] * 2,
+        + [VMEM] * (len(fields) + len(marks) + len(geometry) + len(halos)),
         out_specs=out_specs,
         out_shape=out_shape,
         scratch_shapes=scratch,
@@ -443,20 +438,21 @@
         pltpu.with_memory_space_constraint(x, pltpu.VMEM)
         for x in (below, above, colr, coll, corner_below, corner_above)
     )
-    halos = halos[:4] + (left, right) + halos[4:]
-    geometry = (edge, inv_area)
+    near = lambda x: pltpu.with_memory_space_constraint(x, pltpu.VMEM)
+    halos = halos[:4] + (near(left), near(right)) + halos[4:]
+    geometry = (near(edge), near(inv_area))
     theta_next, vapor_next, cloud_next, send = update(
         peers,
         True,
         (damping, exner, sat_scale, layer_mass),
-        (theta, vapor, cloud),
+        (near(theta), near(vapor), near(cloud)),
         (marks,),
         geometry,
         halos,
     )
     got = lax.all_to_all(send.reshape(peers, 32, LANES), "py", split_axis=0, concat_axis=0, tiled=True)
     (divergence_next,) = update(
-        peers, False, (damping,), (divergence,), (), geometry, halos
+        peers, False, (damping,), (near(divergence),), (), geometry, halos
     )
     precip = jnp.sum(got, axis=0).reshape(1, 4096)
     return (theta_next, vapor_next, cloud_next, divergence_next, precip)

time: 46.2 us -> 46.1 us (level)
  no operation moved by 1% of the time
where the time goes in v6:
time: 46.1 us; the launch traced here: 45.8 us
  Pallas kernels  20.4 us (44%)
  starting transfers between devices  16.9 us (37%)
  waiting for transfers between devices  6.24 us (14%)
  between operations  0.84 us (2%)
  local copies, waits for them, and re-layouts  0.77 us (2%)
  other arithmetic  0.63 us (1%)
    pallas_call x2, Pallas kernels, update(): pl.pallas_call(functools.partial(main_kernel, peers, levels, wet), grid=(...  16.7 us
    ppermute x6, starting transfers between devices, fetch(): lax.ppermute(x, axis, [((i + step) % count, i) for i in range(count)])  11.5 us
    all_to_all x1, starting transfers between devices, on_device(): lax.all_to_all(send.reshape(peers, 32, LANES), 'py', split_axis=0, concat...  5.41 us
    ppermute x6, waiting for transfers between devices, fetch(): lax.ppermute(x, axis, [((i + step) % count, i) for i in range(count)])  4.86 us
    pallas_call x1, Pallas kernels, pack(): pl.pallas_call(pack_kernel, in_specs=[pl.BlockSpec(memory_space=pltpu.HBM...  2.58 us
    all_to_all x1, waiting for transfers between devices, on_device(): lax.all_to_all(send.reshape(peers, 32, LANES), 'py', split_axis=0, concat...  1.37 us
    pallas_call x1, Pallas kernels, onehot(): pl.pallas_call(functools.partial(onehot_kernel, high), grid=(2,), in_spec...  1.14 us
  transfers between devices with their start and end apart: 7, of which 3 were waited for; matrix products, arithmetic and copies ran while one was open for 0% of the time, Pallas kernels for 18%

profile of v6, /device:TPU:0, one launch (start us, length us, event | category | flops | bytes accessed | tf_op | source)
XLA Modules:
  0.0 45.8 jit_solution(17736917896140211567)
XLA Ops:
  0.6 0.0 copy-start.5
  0.6 0.0 copy-start.1
  0.7 0.0 copy-start.2
  0.7 0.0 copy-start.4
  0.7 0.0 copy-start.7
  0.7 0.0 copy-start.10
  0.7 0.0 copy-start.9
  0.7 0.0 copy-start.8
  0.7 0.0 copy-start.3
  0.7 2.6 %pack.1 = (f32[384,256]{1,0:T(8,128)S(1)}, f32[384,256]{1,0:T(8,128)S(1)}, f32[16,384]{1,0:T(8,128)S(1)}, f32[16,384]{1,0:T(8,128)S(1)}) custom-call(f32[928,256]{1,0:T(8,128)} %bitcast.7, f32[928,256]{1,0:T(8,128)} %bitcast.8, f32[928,256]{1,0:T(8,128)} %bitcast.6, f32[48,256]{1,0:T(8,128)} %bitcast.9, f32[16,256]{1,0:T(8,128)} %refs_3_.3), custom_call_target="tpu_custom_call" | custom-call | tf_op jit(solution)/shard_map/pack/pallas_call | solution.py:89
  3.3 6.6 %collective-permute-start = (f32[16,384]{1,0:T(8,128)S(1)}, f32[16,384]{1,0:T(8,128)S(1)}, u32[]{:S(2)}, u32[]{:S(2)}) collective-permute-start(f32[16,384]{1,0:T(8,128)S(1)} %get-tuple-element.16.refs_14_.refs_8_), channel_id=1, source_target_pairs={{1,0},{2,1},{3,2},{4,3},{5,4},{6,5},{7,6},{8,7},{9,8},{10,9},{11,1... | collective-permute-start | bytes 73736 | tf_op jit(solution)/shard_map/ppermute | solution.py:418
  10.0 0.0 collective-permute-start.1
  10.0 1.9 %collective-permute-start.2 = (f32[384,256]{1,0:T(8,128)S(1)}, f32[384,256]{1,0:T(8,128)S(1)}, u32[]{:S(2)}, u32[]{:S(2)}) collective-permute-start(f32[384,256]{1,0:T(8,128)S(1)} %get-tuple-element.19), channel_id=1, source_target_pairs={{16,0},{32,16},{48,32},{64,48},{80,64},{96,80},{112,96},{0,112},{1... | collective-permute-start | bytes 1179656 | tf_op jit(solution)/shard_map/ppermute | solution.py:418
  11.9 0.0 collective-permute-start.3
  11.9 0.0 copy-start.6
  11.9 0.7 %copy-done.6 = s32[16,256]{1,0:T(8,128)S(1)} copy-done((s32[16,256]{1,0:T(8,128)S(1)}, s32[16,256]{1,0:T(8,128)}, u32[]{:S(2)}) %copy-start.6) | copy-done | bytes 16408
  12.6 1.1 %onehot.1.refs_7_ = bf16[640,4096]{1,0:T(8,128)(2,1)S(1)} custom-call(s32[16,256]{1,0:T(8,128)S(1)} %copy-done.6), custom_call_target="tpu_custom_call" | custom-call | flops 1000000000 | bytes 5242880 | tf_op jit(solution)/shard_map/onehot/pallas_call | solution.py:125
  13.7 0.0 copy-start
  13.8 0.0 collective-permute-done.refs_12_.refs_6_
  13.8 3.3 %collective-permute-done.1.refs_13_.refs_7_ = f32[16,384]{1,0:T(8,128)S(1)} collective-permute-done((f32[16,384]{1,0:T(8,128)S(1)}, f32[16,384]{1,0:T(8,128)S(1)}, u32[]{:S(2)}, u32[]{:S(2)}) %collective-permute-start.1) | collective-permute-done | bytes 24608 | tf_op jit(solution)/shard_map/ppermute | solution.py:418
  17.1 0.0 collective-permute-start.5
  17.1 2.9 %collective-permute-start.4 = (f32[8,768]{1,0:T(8,128)S(1)}, f32[8,768]{1,0:T(8,128)S(1)}, u32[]{:S(2)}, u32[]{:S(2)}) collective-permute-start(f32[8,768]{1,0:T(8,128)S(1)} %get-tuple-element.28), channel_id=1, source_target_pairs={{16,0},{32,16},{48,32},{64,48},{80,64},{96,80},{112,96},{0,112},{1... | collective-permute-start | bytes 73736 | tf_op jit(solution)/shard_map/ppermute | solution.py:418
  20.1 1.5 %collective-permute-done.5.refs_17_.refs_11_ = f32[8,768]{1,0:T(8,128)S(1)} collective-permute-done((f32[8,768]{1,0:T(8,128)S(1)}, f32[8,768]{1,0:T(8,128)S(1)}, u32[]{:S(2)}, u32[]{:S(2)}) %collective-permute-start.5) | collective-permute-done | bytes 24608 | tf_op jit(solution)/shard_map/ppermute | solution.py:418
  21.6 0.0 collective-permute-done.4.refs_16_.refs_10_
  21.6 0.0 collective-permute-done.2.refs_10_.refs_4_
  21.6 0.0 collective-permute-done.3.refs_11_.refs_5_
  21.6 0.0 copy-done.5
  21.6 0.0 copy-done.1
  21.6 0.0 copy-done.2
  21.6 0.0 copy-done.4
  21.6 0.0 copy-done.7
  21.7 0.0 copy-done.10
  21.7 0.0 copy-done.9
  21.7 0.0 copy-done.8
  21.7 0.0 copy-done.3
  21.7 9.4 %moist.1 = (f32[58,16,256]{2,1,0:T(8,128)}, f32[58,16,256]{2,1,0:T(8,128)}, f32[58,16,256]{2,1,0:T(8,128)}, f32[512,128]{1,0:T(8,128)}) custom-call(f32[3,58]{1,0:T(4,128)S(1)} %copy-done.7, f32[58]{0:T(128)S(1)} %copy-done.8, f32[58]{0:T(128)S(1)} %copy-done.9, f32[58]{0:T(128)S(1)} %copy-done.10, f32[58,16,256]{2,1,0:T(8,128)S(1)} %copy-done.1, ...), custom_call_target="tpu_custom_call" | custom-call | flops 300000000 | bytes 6291456 | tf_op jit(solution)/shard_map/moist/pallas_call | solution.py:385
  31.1 5.4 %all-to-all-start = ((f32[16,32,128]{2,1,0:T(8,128)}), f32[16,32,128]{2,1,0:T(8,128)S(1)}, u32[]{:S(2)}, u32[]{:S(2)}) async-start(f32[16,32,128]{2,1,0:T(8,128)} %bitcast.4), calls=%async_computation | async-start | bytes 524288 | tf_op jit(solution)/shard_map/all_to_all | solution.py:453
  36.5 0.0 copy-done
  36.5 7.3 %dry.1 = f32[58,16,256]{2,1,0:T(8,128)} custom-call(f32[3,58]{1,0:T(4,128)S(1)} %copy-done.7, f32[58,16,256]{2,1,0:T(8,128)S(1)} %copy-done, f32[48,256]{1,0:T(8,128)S(1)} %bitcast.11, f32[16,256]{1,0:T(8,128)S(1)} %copy-done.5, f32[384,256]{1,0:T(8,128)S(1)} %collective-permute-done.2.refs_10_.refs_4_, ...), custom_call_target="tpu_custom_call" | custom-call | flops 100000000 | bytes 2097152 | tf_op jit(solution)/shard_map/dry/pallas_call | solution.py:385
  43.8 1.4 %all-to-all-done = f32[16,32,128]{2,1,0:T(8,128)S(1)} async-done(((f32[16,32,128]{2,1,0:T(8,128)}), f32[16,32,128]{2,1,0:T(8,128)S(1)}, u32[]{:S(2)}, u32[]{:S(2)}) %all-to-all-start) | async-done | bytes 262176 | tf_op jit(solution)/shard_map/all_to_all | solution.py:453
  45.2 0.6 %reduce_sum.9 = f32[32,128]{1,0:T(8,128)} reduce(f32[16,32,128]{2,1,0:T(8,128)S(1)} %all-to-all-done, f32[]{:T(128)} %constant.0.clone.1), dimensions={0}, to_apply=%region_0.0 | reduce | flops 61440 | bytes 278532 | tf_op jit(solution)/shard_map/reduce_sum | solution.py:457
  (3 shorter events, 0.0 us)
Async XLA Ops:
  0.6 21.0 %copy-start.5 = (f32[16,256]{1,0:T(8,128)S(1)}, f32[16,256]{1,0:T(8,128)}, u32[]{:S(2)}) copy-start(f32[16,256]{1,0:T(8,128)} %refs_3_.3) | copy-start | bytes 49156
  0.6 21.0 %copy-start.1 = (f32[58,16,256]{2,1,0:T(8,128)S(1)}, f32[58,16,256]{2,1,0:T(8,128)}, u32[]{:S(2)}) copy-start(f32[58,16,256]{2,1,0:T(8,128)} %refs_4_.1) | copy-start | bytes 2850820
  0.7 21.0 %copy-start.2 = (f32[58,16,256]{2,1,0:T(8,128)S(1)}, f32[58,16,256]{2,1,0:T(8,128)}, u32[]{:S(2)}) copy-start(f32[58,16,256]{2,1,0:T(8,128)} %refs_5_.1) | copy-start | bytes 2850820
  0.7 21.0 %copy-start.4 = (f32[3,16,256]{2,1,0:T(8,128)S(1)}, f32[3,16,256]{2,1,0:T(8,128)}, u32[]{:S(2)}) copy-start(f32[3,16,256]{2,1,0:T(8,128)} %param.15) | copy-start | bytes 147460
  0.7 21.0 %copy-start.7 = (f32[3,58]{1,0:T(4,128)S(1)}, f32[3,58]{1,0:T(4,128)}, u32[]{:S(2)}) copy-start(f32[3,58]{1,0:T(4,128)} %refs_0_.3) | copy-start | bytes 2092
  0.7 21.0 %copy-start.10 = (f32[58]{0:T(128)S(1)}, f32[58]{0:T(128)}, u32[]{:S(2)}) copy-start(f32[58]{0:T(128)} %refs_3_.2) | copy-start | bytes 700
  0.7 21.0 %copy-start.9 = (f32[58]{0:T(128)S(1)}, f32[58]{0:T(128)}, u32[]{:S(2)}) copy-start(f32[58]{0:T(128)} %refs_2_.1) | copy-start | bytes 700
  0.7 21.0 %copy-start.8 = (f32[58]{0:T(128)S(1)}, f32[58]{0:T(128)}, u32[]{:S(2)}) copy-start(f32[58]{0:T(128)} %refs_1_.2) | copy-start | bytes 700
  0.7 21.0 %copy-start.3 = (f32[58,16,256]{2,1,0:T(8,128)S(1)}, f32[58,16,256]{2,1,0:T(8,128)}, u32[]{:S(2)}) copy-start(f32[58,16,256]{2,1,0:T(8,128)} %refs_6_.1) | copy-start | bytes 2850820
  3.3 10.4 %collective-permute-start = (f32[16,384]{1,0:T(8,128)S(1)}, f32[16,384]{1,0:T(8,128)S(1)}, u32[]{:S(2)}, u32[]{:S(2)}) collective-permute-start(f32[16,384]{1,0:T(8,128)S(1)} %get-tuple-element.16.refs_14_.refs_8_), channel_id=1, source_target_pairs={{1,0},{2,1},{3,2},{4,3},{5,4},{6,5},{7,6},{8,7},{9,8},{10,9},{11,1... | collective-permute-start | bytes 73736 | tf_op jit(solution)/shard_map/ppermute | solution.py:418
  10.0 7.1 %collective-permute-start.1 = (f32[16,384]{1,0:T(8,128)S(1)}, f32[16,384]{1,0:T(8,128)S(1)}, u32[]{:S(2)}, u32[]{:S(2)}) collective-permute-start(f32[16,384]{1,0:T(8,128)S(1)} %get-tuple-element.17.refs_15_.refs_9_), channel_id=1, source_target_pairs={{15,0},{0,1},{1,2},{2,3},{3,4},{4,5},{5,6},{6,7},{7,8},{8,9},{9,10... | collective-permute-start | bytes 73736 | tf_op jit(solution)/shard_map/ppermute | solution.py:418
  10.0 11.7 %collective-permute-start.2 = (f32[384,256]{1,0:T(8,128)S(1)}, f32[384,256]{1,0:T(8,128)S(1)}, u32[]{:S(2)}, u32[]{:S(2)}) collective-permute-start(f32[384,256]{1,0:T(8,128)S(1)} %get-tuple-element.19), channel_id=1, source_target_pairs={{16,0},{32,16},{48,32},{64,48},{80,64},{96,80},{112,96},{0,112},{1... | collective-permute-start | bytes 1179656 | tf_op jit(solution)/shard_map/ppermute | solution.py:418
  11.9 9.7 %collective-permute-start.3 = (f32[384,256]{1,0:T(8,128)S(1)}, f32[384,256]{1,0:T(8,128)S(1)}, u32[]{:S(2)}, u32[]{:S(2)}) collective-permute-start(f32[384,256]{1,0:T(8,128)S(1)} %get-tuple-element.20), channel_id=1, source_target_pairs={{112,0},{0,16},{16,32},{32,48},{48,64},{64,80},{80,96},{96,112},{1... | collective-permute-start | bytes 1179656 | tf_op jit(solution)/shard_map/ppermute | solution.py:418
  11.9 0.7 %copy-start.6 = (s32[16,256]{1,0:T(8,128)S(1)}, s32[16,256]{1,0:T(8,128)}, u32[]{:S(2)}) copy-start(s32[16,256]{1,0:T(8,128)} %span_ref.1) | copy-start | bytes 49156
  13.7 22.8 %copy-start = (f32[58,16,256]{2,1,0:T(8,128)S(1)}, f32[58,16,256]{2,1,0:T(8,128)}, u32[]{:S(2)}) copy-start(f32[58,16,256]{2,1,0:T(8,128)} %refs_1_.3) | copy-start | bytes 2850820
  17.1 4.5 %collective-permute-start.5 = (f32[8,768]{1,0:T(8,128)S(1)}, f32[8,768]{1,0:T(8,128)S(1)}, u32[]{:S(2)}, u32[]{:S(2)}) collective-permute-start(f32[8,768]{1,0:T(8,128)S(1)} %get-tuple-element.27), channel_id=1, source_target_pairs={{112,0},{0,16},{16,32},{32,48},{48,64},{64,80},{80,96},{96,112},{1... | collective-permute-start | bytes 73736 | tf_op jit(solution)/shard_map/ppermute | solution.py:418
  17.1 4.5 %collective-permute-start.4 = (f32[8,768]{1,0:T(8,128)S(1)}, f32[8,768]{1,0:T(8,128)S(1)}, u32[]{:S(2)}, u32[]{:S(2)}) collective-permute-start(f32[8,768]{1,0:T(8,128)S(1)} %get-tuple-element.28), channel_id=1, source_target_pairs={{16,0},{32,16},{48,32},{64,48},{80,64},{96,80},{112,96},{0,112},{1... | collective-permute-start | bytes 73736 | tf_op jit(solution)/shard_map/ppermute | solution.py:418
  31.1 14.1 %all-to-all-start = ((f32[16,32,128]{2,1,0:T(8,128)}), f32[16,32,128]{2,1,0:T(8,128)S(1)}, u32[]{:S(2)}, u32[]{:S(2)}) async-start(f32[16,32,128]{2,1,0:T(8,128)} %bitcast.4), calls=%async_computation | async-start | bytes 524288 | tf_op jit(solution)/shard_map/all_to_all | solution.py:453

commit v7 on v6

--- a/solution.py
+++ b/solution.py
@@ -12,9 +12,9 @@
 AUTO_RATE = 0.5
 
 LANES = 128
-BLOCK_LEVELS = 16
+BLOCK_LEVELS = 32
 WET_UNROLL = 4
-DRY_UNROLL = 2
+DRY_UNROLL = 4
 
 
 def pack_kernel(

time: 46.1 us -> 46.2 us (level)
  waiting for transfers between devices: 6.24 us -> 8.48 us
  Pallas kernels: 20.4 us -> 18.2 us
    all_to_all x1, waiting for transfers between devices: 1.37 us -> 3.62 us  [on_device(): lax.all_to_all(send.reshape(peers, 32, LANES), 'py', split_axis=0, concat...]
    pallas_call x2, Pallas kernels: 16.7 us -> 14.5 us  [update(): pl.pallas_call(functools.partial(main_kernel, peers, levels, wet), grid=(...]
  transfers between devices with their start and end apart: 7 -> 7, of which waited for: 3 -> 3; matrix products, arithmetic and copies ran while one was open for 0% -> 0% of each run, Pallas kernels for 18% -> 14%
where the time goes in v7:
time: 46.2 us; the launch traced here: 45.9 us
  Pallas kernels  18.2 us (39%)
  starting transfers between devices  16.9 us (37%)
  waiting for transfers between devices  8.48 us (18%)
  between operations  0.84 us (2%)
  local copies, waits for them, and re-layouts  0.77 us (2%)
  other arithmetic  0.63 us (1%)
    pallas_call x2, Pallas kernels, update(): pl.pallas_call(functools.partial(main_kernel, peers, levels, wet), grid=(...  14.5 us
    ppermute x6, starting transfers between devices, fetch(): lax.ppermute(x, axis, [((i + step) % count, i) for i in range(count)])  11.5 us
    all_to_all x1, starting transfers between devices, on_device(): lax.all_to_all(send.reshape(peers, 32, LANES), 'py', split_axis=0, concat...  5.41 us
    ppermute x6, waiting for transfers between devices, fetch(): lax.ppermute(x, axis, [((i + step) % count, i) for i in range(count)])  4.86 us
    all_to_all x1, waiting for transfers between devices, on_device(): lax.all_to_all(send.reshape(peers, 32, LANES), 'py', split_axis=0, concat...  3.62 us
    pallas_call x1, Pallas kernels, pack(): pl.pallas_call(pack_kernel, in_specs=[pl.BlockSpec(memory_space=pltpu.HBM...  2.58 us
    pallas_call x1, Pallas kernels, onehot(): pl.pallas_call(functools.partial(onehot_kernel, high), grid=(2,), in_spec...  1.14 us
  transfers between devices with their start and end apart: 7, of which 3 were waited for; matrix products, arithmetic and copies ran while one was open for 0% of the time, Pallas kernels for 14%

profile of v7, /device:TPU:0, one launch (start us, length us, event | category | flops | bytes accessed | tf_op | source)
XLA Modules:
  0.0 45.9 jit_solution(9091344694371730435)
XLA Ops:
  0.6 0.0 copy-start.5
  0.6 0.0 copy-start.1
  0.7 0.0 copy-start.2
  0.7 0.0 copy-start.4
  0.7 0.0 copy-start.7
  0.7 0.0 copy-start.10
  0.7 0.0 copy-start.9
  0.7 0.0 copy-start.8
  0.7 0.0 copy-start.3
  0.7 2.6 %pack.1 = (f32[384,256]{1,0:T(8,128)S(1)}, f32[384,256]{1,0:T(8,128)S(1)}, f32[16,384]{1,0:T(8,128)S(1)}, f32[16,384]{1,0:T(8,128)S(1)}) custom-call(f32[928,256]{1,0:T(8,128)} %bitcast.7, f32[928,256]{1,0:T(8,128)} %bitcast.8, f32[928,256]{1,0:T(8,128)} %bitcast.6, f32[48,256]{1,0:T(8,128)} %bitcast.9, f32[16,256]{1,0:T(8,128)} %refs_3_.3), custom_call_target="tpu_custom_call" | custom-call | tf_op jit(solution)/shard_map/pack/pallas_call | solution.py:89
  3.3 6.6 %collective-permute-start = (f32[16,384]{1,0:T(8,128)S(1)}, f32[16,384]{1,0:T(8,128)S(1)}, u32[]{:S(2)}, u32[]{:S(2)}) collective-permute-start(f32[16,384]{1,0:T(8,128)S(1)} %get-tuple-element.16.refs_14_.refs_8_), channel_id=1, source_target_pairs={{1,0},{2,1},{3,2},{4,3},{5,4},{6,5},{7,6},{8,7},{9,8},{10,9},{11,1... | collective-permute-start | bytes 73736 | tf_op jit(solution)/shard_map/ppermute | solution.py:418
  10.0 0.0 collective-permute-start.1
  10.0 1.9 %collective-permute-start.2 = (f32[384,256]{1,0:T(8,128)S(1)}, f32[384,256]{1,0:T(8,128)S(1)}, u32[]{:S(2)}, u32[]{:S(2)}) collective-permute-start(f32[384,256]{1,0:T(8,128)S(1)} %get-tuple-element.19), channel_id=1, source_target_pairs={{16,0},{32,16},{48,32},{64,48},{80,64},{96,80},{112,96},{0,112},{1... | collective-permute-start | bytes 1179656 | tf_op jit(solution)/shard_map/ppermute | solution.py:418
  11.9 0.0 collective-permute-start.3
  11.9 0.0 copy-start.6
  11.9 0.7 %copy-done.6 = s32[16,256]{1,0:T(8,128)S(1)} copy-done((s32[16,256]{1,0:T(8,128)S(1)}, s32[16,256]{1,0:T(8,128)}, u32[]{:S(2)}) %copy-start.6) | copy-done | bytes 16408
  12.6 1.1 %onehot.1.refs_7_ = bf16[640,4096]{1,0:T(8,128)(2,1)S(1)} custom-call(s32[16,256]{1,0:T(8,128)S(1)} %copy-done.6), custom_call_target="tpu_custom_call" | custom-call | flops 1000000000 | bytes 5242880 | tf_op jit(solution)/shard_map/onehot/pallas_call | solution.py:125
  13.7 0.0 copy-start
  13.8 0.0 collective-permute-done.refs_12_.refs_6_
  13.8 3.3 %collective-permute-done.1.refs_13_.refs_7_ = f32[16,384]{1,0:T(8,128)S(1)} collective-permute-done((f32[16,384]{1,0:T(8,128)S(1)}, f32[16,384]{1,0:T(8,128)S(1)}, u32[]{:S(2)}, u32[]{:S(2)}) %collective-permute-start.1) | collective-permute-done | bytes 24608 | tf_op jit(solution)/shard_map/ppermute | solution.py:418
  17.1 0.0 collective-permute-start.5
  17.1 2.9 %collective-permute-start.4 = (f32[8,768]{1,0:T(8,128)S(1)}, f32[8,768]{1,0:T(8,128)S(1)}, u32[]{:S(2)}, u32[]{:S(2)}) collective-permute-start(f32[8,768]{1,0:T(8,128)S(1)} %get-tuple-element.28), channel_id=1, source_target_pairs={{16,0},{32,16},{48,32},{64,48},{80,64},{96,80},{112,96},{0,112},{1... | collective-permute-start | bytes 73736 | tf_op jit(solution)/shard_map/ppermute | solution.py:418
  20.1 1.5 %collective-permute-done.5.refs_17_.refs_11_ = f32[8,768]{1,0:T(8,128)S(1)} collective-permute-done((f32[8,768]{1,0:T(8,128)S(1)}, f32[8,768]{1,0:T(8,128)S(1)}, u32[]{:S(2)}, u32[]{:S(2)}) %collective-permute-start.5) | collective-permute-done | bytes 24608 | tf_op jit(solution)/shard_map/ppermute | solution.py:418
  21.6 0.0 collective-permute-done.4.refs_16_.refs_10_
  21.6 0.0 collective-permute-done.2.refs_10_.refs_4_
  21.6 0.0 collective-permute-done.3.refs_11_.refs_5_
  21.6 0.0 copy-done.5
  21.6 0.0 copy-done.1
  21.6 0.0 copy-done.2
  21.6 0.0 copy-done.4
  21.6 0.0 copy-done.7
  21.7 0.0 copy-done.10
  21.7 0.0 copy-done.9
  21.7 0.0 copy-done.8
  21.7 0.0 copy-done.3
  21.7 9.4 %moist.1 = (f32[58,16,256]{2,1,0:T(8,128)}, f32[58,16,256]{2,1,0:T(8,128)}, f32[58,16,256]{2,1,0:T(8,128)}, f32[512,128]{1,0:T(8,128)}) custom-call(f32[3,58]{1,0:T(4,128)S(1)} %copy-done.7, f32[58]{0:T(128)S(1)} %copy-done.8, f32[58]{0:T(128)S(1)} %copy-done.9, f32[58]{0:T(128)S(1)} %copy-done.10, f32[58,16,256]{2,1,0:T(8,128)S(1)} %copy-done.1, ...), custom_call_target="tpu_custom_call" | custom-call | flops 300000000 | bytes 6291456 | tf_op jit(solution)/shard_map/moist/pallas_call | solution.py:385
  31.2 5.4 %all-to-all-start = ((f32[16,32,128]{2,1,0:T(8,128)}), f32[16,32,128]{2,1,0:T(8,128)S(1)}, u32[]{:S(2)}, u32[]{:S(2)}) async-start(f32[16,32,128]{2,1,0:T(8,128)} %bitcast.4), calls=%async_computation | async-start | bytes 524288 | tf_op jit(solution)/shard_map/all_to_all | solution.py:453
  36.6 0.0 copy-done
  36.6 5.1 %dry.1 = f32[58,16,256]{2,1,0:T(8,128)} custom-call(f32[3,58]{1,0:T(4,128)S(1)} %copy-done.7, f32[58,16,256]{2,1,0:T(8,128)S(1)} %copy-done, f32[48,256]{1,0:T(8,128)S(1)} %bitcast.11, f32[16,256]{1,0:T(8,128)S(1)} %copy-done.5, f32[384,256]{1,0:T(8,128)S(1)} %collective-permute-done.2.refs_10_.refs_4_, ...), custom_call_target="tpu_custom_call" | custom-call | flops 100000000 | bytes 2097152 | tf_op jit(solution)/shard_map/dry/pallas_call | solution.py:385
  41.6 3.6 %all-to-all-done = f32[16,32,128]{2,1,0:T(8,128)S(1)} async-done(((f32[16,32,128]{2,1,0:T(8,128)}), f32[16,32,128]{2,1,0:T(8,128)S(1)}, u32[]{:S(2)}, u32[]{:S(2)}) %all-to-all-start) | async-done | bytes 262176 | tf_op jit(solution)/shard_map/all_to_all | solution.py:453
  45.3 0.6 %reduce_sum.9 = f32[32,128]{1,0:T(8,128)} reduce(f32[16,32,128]{2,1,0:T(8,128)S(1)} %all-to-all-done, f32[]{:T(128)} %constant.0.clone.1), dimensions={0}, to_apply=%region_0.0 | reduce | flops 61440 | bytes 278532 | tf_op jit(solution)/shard_map/reduce_sum | solution.py:457
  (3 shorter events, 0.0 us)
Async XLA Ops:
  0.6 21.0 %copy-start.5 = (f32[16,256]{1,0:T(8,128)S(1)}, f32[16,256]{1,0:T(8,128)}, u32[]{:S(2)}) copy-start(f32[16,256]{1,0:T(8,128)} %refs_3_.3) | copy-start | bytes 49156
  0.6 21.0 %copy-start.1 = (f32[58,16,256]{2,1,0:T(8,128)S(1)}, f32[58,16,256]{2,1,0:T(8,128)}, u32[]{:S(2)}) copy-start(f32[58,16,256]{2,1,0:T(8,128)} %refs_4_.1) | copy-start | bytes 2850820
  0.7 21.0 %copy-start.2 = (f32[58,16,256]{2,1,0:T(8,128)S(1)}, f32[58,16,256]{2,1,0:T(8,128)}, u32[]{:S(2)}) copy-start(f32[58,16,256]{2,1,0:T(8,128)} %refs_5_.1) | copy-start | bytes 2850820
  0.7 21.0 %copy-start.4 = (f32[3,16,256]{2,1,0:T(8,128)S(1)}, f32[3,16,256]{2,1,0:T(8,128)}, u32[]{:S(2)}) copy-start(f32[3,16,256]{2,1,0:T(8,128)} %param.15) | copy-start | bytes 147460
  0.7 21.0 %copy-start.7 = (f32[3,58]{1,0:T(4,128)S(1)}, f32[3,58]{1,0:T(4,128)}, u32[]{:S(2)}) copy-start(f32[3,58]{1,0:T(4,128)} %refs_0_.3) | copy-start | bytes 2092
  0.7 21.0 %copy-start.10 = (f32[58]{0:T(128)S(1)}, f32[58]{0:T(128)}, u32[]{:S(2)}) copy-start(f32[58]{0:T(128)} %refs_3_.2) | copy-start | bytes 700
  0.7 21.0 %copy-start.9 = (f32[58]{0:T(128)S(1)}, f32[58]{0:T(128)}, u32[]{:S(2)}) copy-start(f32[58]{0:T(128)} %refs_2_.1) | copy-start | bytes 700
  0.7 21.0 %copy-start.8 = (f32[58]{0:T(128)S(1)}, f32[58]{0:T(128)}, u32[]{:S(2)}) copy-start(f32[58]{0:T(128)} %refs_1_.2) | copy-start | bytes 700
  0.7 21.0 %copy-start.3 = (f32[58,16,256]{2,1,0:T(8,128)S(1)}, f32[58,16,256]{2,1,0:T(8,128)}, u32[]{:S(2)}) copy-start(f32[58,16,256]{2,1,0:T(8,128)} %refs_6_.1) | copy-start | bytes 2850820
  3.3 10.4 %collective-permute-start = (f32[16,384]{1,0:T(8,128)S(1)}, f32[16,384]{1,0:T(8,128)S(1)}, u32[]{:S(2)}, u32[]{:S(2)}) collective-permute-start(f32[16,384]{1,0:T(8,128)S(1)} %get-tuple-element.16.refs_14_.refs_8_), channel_id=1, source_target_pairs={{1,0},{2,1},{3,2},{4,3},{5,4},{6,5},{7,6},{8,7},{9,8},{10,9},{11,1... | collective-permute-start | bytes 73736 | tf_op jit(solution)/shard_map/ppermute | solution.py:418
  10.0 7.1 %collective-permute-start.1 = (f32[16,384]{1,0:T(8,128)S(1)}, f32[16,384]{1,0:T(8,128)S(1)}, u32[]{:S(2)}, u32[]{:S(2)}) collective-permute-start(f32[16,384]{1,0:T(8,128)S(1)} %get-tuple-element.17.refs_15_.refs_9_), channel_id=1, source_target_pairs={{15,0},{0,1},{1,2},{2,3},{3,4},{4,5},{5,6},{6,7},{7,8},{8,9},{9,10... | collective-permute-start | bytes 73736 | tf_op jit(solution)/shard_map/ppermute | solution.py:418
  10.0 11.7 %collective-permute-start.2 = (f32[384,256]{1,0:T(8,128)S(1)}, f32[384,256]{1,0:T(8,128)S(1)}, u32[]{:S(2)}, u32[]{:S(2)}) collective-permute-start(f32[384,256]{1,0:T(8,128)S(1)} %get-tuple-element.19), channel_id=1, source_target_pairs={{16,0},{32,16},{48,32},{64,48},{80,64},{96,80},{112,96},{0,112},{1... | collective-permute-start | bytes 1179656 | tf_op jit(solution)/shard_map/ppermute | solution.py:418
  11.9 9.7 %collective-permute-start.3 = (f32[384,256]{1,0:T(8,128)S(1)}, f32[384,256]{1,0:T(8,128)S(1)}, u32[]{:S(2)}, u32[]{:S(2)}) collective-permute-start(f32[384,256]{1,0:T(8,128)S(1)} %get-tuple-element.20), channel_id=1, source_target_pairs={{112,0},{0,16},{16,32},{32,48},{48,64},{64,80},{80,96},{96,112},{1... | collective-permute-start | bytes 1179656 | tf_op jit(solution)/shard_map/ppermute | solution.py:418
  11.9 0.7 %copy-start.6 = (s32[16,256]{1,0:T(8,128)S(1)}, s32[16,256]{1,0:T(8,128)}, u32[]{:S(2)}) copy-start(s32[16,256]{1,0:T(8,128)} %span_ref.1) | copy-start | bytes 49156
  13.7 22.8 %copy-start = (f32[58,16,256]{2,1,0:T(8,128)S(1)}, f32[58,16,256]{2,1,0:T(8,128)}, u32[]{:S(2)}) copy-start(f32[58,16,256]{2,1,0:T(8,128)} %refs_1_.3) | copy-start | bytes 2850820
  17.1 4.5 %collective-permute-start.5 = (f32[8,768]{1,0:T(8,128)S(1)}, f32[8,768]{1,0:T(8,128)S(1)}, u32[]{:S(2)}, u32[]{:S(2)}) collective-permute-start(f32[8,768]{1,0:T(8,128)S(1)} %get-tuple-element.27), channel_id=1, source_target_pairs={{112,0},{0,16},{16,32},{32,48},{48,64},{64,80},{80,96},{96,112},{1... | collective-permute-start | bytes 73736 | tf_op jit(solution)/shard_map/ppermute | solution.py:418
  17.1 4.5 %collective-permute-start.4 = (f32[8,768]{1,0:T(8,128)S(1)}, f32[8,768]{1,0:T(8,128)S(1)}, u32[]{:S(2)}, u32[]{:S(2)}) collective-permute-start(f32[8,768]{1,0:T(8,128)S(1)} %get-tuple-element.28), channel_id=1, source_target_pairs={{16,0},{32,16},{48,32},{64,48},{80,64},{96,80},{112,96},{0,112},{1... | collective-permute-start | bytes 73736 | tf_op jit(solution)/shard_map/ppermute | solution.py:418
  31.2 14.1 %all-to-all-start = ((f32[16,32,128]{2,1,0:T(8,128)}), f32[16,32,128]{2,1,0:T(8,128)S(1)}, u32[]{:S(2)}, u32[]{:S(2)}) async-start(f32[16,32,128]{2,1,0:T(8,128)} %bitcast.4), calls=%async_computation | async-start | bytes 524288 | tf_op jit(solution)/shard_map/all_to_all | solution.py:453

commit v8 on v7

--- a/solution.py
+++ b/solution.py
@@ -430,7 +430,6 @@
     below = fetch(top, "px", 1)
     above = fetch(bot, "px", -1)
     marks = pltpu.with_memory_space_constraint(onehot(span_of, peers * 32), pltpu.VMEM)
-    colr, coll, marks = lax.optimization_barrier((colr, coll, marks))
     sides = jnp.concatenate([colr, coll], axis=1)
     corner_below = fetch(sides[:8], "px", 1)
     corner_above = fetch(sides[8:], "px", -1)

time: 46.2 us -> 48 us (1.039)
  waiting for transfers between devices: 8.48 us -> 13.3 us
  starting transfers between devices: 16.9 us -> 13.9 us
    ppermute x6, waiting for transfers between devices: 4.86 us -> 9.71 us  [fetch(): lax.ppermute(x, axis, [((i + step) % count, i) for i in range(count)])]
    all_to_all x1, starting transfers between devices: 5.41 us -> 3.54 us  [on_device(): lax.all_to_all(send.reshape(peers, 32, LANES), 'py', split_axis=0, concat...]
    ppermute x6, starting transfers between devices: 11.5 us -> 10.4 us  [fetch(): lax.ppermute(x, axis, [((i + step) % count, i) for i in range(count)])]
  transfers between devices with their start and end apart: 7 -> 7, of which waited for: 3 -> 3; matrix products, arithmetic and copies ran while one was open for 0% -> 0% of each run, Pallas kernels for 14% -> 13%
where the time goes in v8:
time: 48 us; the launch traced here: 47.7 us
  Pallas kernels  18.2 us (38%)
  starting transfers between devices  13.9 us (29%)
  waiting for transfers between devices  13.3 us (28%)
  between operations  0.84 us (2%)
  local copies, waits for them, and re-layouts  0.77 us (2%)
  other arithmetic  0.63 us (1%)
    pallas_call x2, Pallas kernels, update(): pl.pallas_call(functools.partial(main_kernel, peers, levels, wet), grid=(...  14.5 us
    ppermute x6, starting transfers between devices, fetch(): lax.ppermute(x, axis, [((i + step) % count, i) for i in range(count)])  10.4 us
    ppermute x6, waiting for transfers between devices, fetch(): lax.ppermute(x, axis, [((i + step) % count, i) for i in range(count)])  9.71 us
    all_to_all x1, waiting for transfers between devices, on_device(): lax.all_to_all(send.reshape(peers, 32, LANES), 'py', split_axis=0, concat...  3.58 us
    all_to_all x1, starting transfers between devices, on_device(): lax.all_to_all(send.reshape(peers, 32, LANES), 'py', split_axis=0, concat...  3.54 us
    pallas_call x1, Pallas kernels, pack(): pl.pallas_call(pack_kernel, in_specs=[pl.BlockSpec(memory_space=pltpu.HBM...  2.58 us
    pallas_call x1, Pallas kernels, onehot(): pl.pallas_call(functools.partial(onehot_kernel, high), grid=(2,), in_spec...  1.14 us
  transfers between devices with their start and end apart: 7, of which 3 were waited for; matrix products, arithmetic and copies ran while one was open for 0% of the time, Pallas kernels for 13%

profile of v8, /device:TPU:0, one launch (start us, length us, event | category | flops | bytes accessed | tf_op | source)
XLA Modules:
  0.0 47.7 jit_solution(5290569954154433488)
XLA Ops:
  0.6 0.0 copy-start.4
  0.6 0.0 copy-start.5
  0.7 0.0 copy-start.1
  0.7 0.0 copy-start.2
  0.7 0.0 copy-start.7
  0.7 0.0 copy-start.8
  0.7 0.0 copy-start.9
  0.7 0.0 copy-start.10
  0.7 0.0 copy-start.3
  0.7 2.6 %pack.1 = (f32[384,256]{1,0:T(8,128)S(1)}, f32[384,256]{1,0:T(8,128)S(1)}, f32[16,384]{1,0:T(8,128)S(1)}, f32[16,384]{1,0:T(8,128)S(1)}) custom-call(f32[928,256]{1,0:T(8,128)} %bitcast.7, f32[928,256]{1,0:T(8,128)} %bitcast.8, f32[928,256]{1,0:T(8,128)} %bitcast.6, f32[48,256]{1,0:T(8,128)} %bitcast.9, f32[16,256]{1,0:T(8,128)} %refs_3_.3), custom_call_target="tpu_custom_call" | custom-call | tf_op jit(solution)/shard_map/pack/pallas_call | solution.py:89
  3.3 6.6 %collective-permute-start.2 = (f32[16,384]{1,0:T(8,128)S(1)}, f32[16,384]{1,0:T(8,128)S(1)}, u32[]{:S(2)}, u32[]{:S(2)}) collective-permute-start(f32[16,384]{1,0:T(8,128)S(1)} %get-tuple-element.15.refs_14_.refs_8_), channel_id=1, source_target_pairs={{1,0},{2,1},{3,2},{4,3},{5,4},{6,5},{7,6},{8,7},{9,8},{10,9},{11,1... | collective-permute-start | bytes 73736 | tf_op jit(solution)/shard_map/ppermute | solution.py:418
  10.0 1.9 %collective-permute-start = (f32[384,256]{1,0:T(8,128)S(1)}, f32[384,256]{1,0:T(8,128)S(1)}, u32[]{:S(2)}, u32[]{:S(2)}) collective-permute-start(f32[384,256]{1,0:T(8,128)S(1)} %get-tuple-element.13), channel_id=1, source_target_pairs={{16,0},{32,16},{48,32},{64,48},{80,64},{96,80},{112,96},{0,112},{1... | collective-permute-start | bytes 1179656 | tf_op jit(solution)/shard_map/ppermute | solution.py:418
  11.9 0.0 collective-permute-start.1
  11.9 0.0 collective-permute-start.3
  11.9 0.0 collective-permute-done.2.refs_12_.refs_6_
  11.9 7.1 %collective-permute-done.3.refs_13_.refs_7_ = f32[16,384]{1,0:T(8,128)S(1)} collective-permute-done((f32[16,384]{1,0:T(8,128)S(1)}, f32[16,384]{1,0:T(8,128)S(1)}, u32[]{:S(2)}, u32[]{:S(2)}) %collective-permute-start.3) | collective-permute-done | bytes 24608 | tf_op jit(solution)/shard_map/ppermute | solution.py:418
  19.0 1.8 %collective-permute-start.4 = (f32[8,768]{1,0:T(8,128)S(1)}, f32[8,768]{1,0:T(8,128)S(1)}, u32[]{:S(2)}, u32[]{:S(2)}) collective-permute-start(f32[8,768]{1,0:T(8,128)S(1)} %get-tuple-element.22), channel_id=1, source_target_pairs={{16,0},{32,16},{48,32},{64,48},{80,64},{96,80},{112,96},{0,112},{1... | collective-permute-start | bytes 73736 | tf_op jit(solution)/shard_map/ppermute | solution.py:418
  20.9 0.0 collective-permute-start.5
  20.9 0.0 copy-start.6
  20.9 0.7 %copy-done.6 = s32[16,256]{1,0:T(8,128)S(1)} copy-done((s32[16,256]{1,0:T(8,128)S(1)}, s32[16,256]{1,0:T(8,128)}, u32[]{:S(2)}) %copy-start.6) | copy-done | bytes 16408
  21.6 1.1 %onehot.1.refs_7_ = bf16[640,4096]{1,0:T(8,128)(2,1)S(1)} custom-call(s32[16,256]{1,0:T(8,128)S(1)} %copy-done.6), custom_call_target="tpu_custom_call" | custom-call | flops 1000000000 | bytes 5242880 | tf_op jit(solution)/shard_map/onehot/pallas_call | solution.py:125
  22.7 0.0 copy-start
  22.7 0.0 collective-permute-done.4.refs_16_.refs_10_
  22.7 2.6 %collective-permute-done.5.refs_17_.refs_11_ = f32[8,768]{1,0:T(8,128)S(1)} collective-permute-done((f32[8,768]{1,0:T(8,128)S(1)}, f32[8,768]{1,0:T(8,128)S(1)}, u32[]{:S(2)}, u32[]{:S(2)}) %collective-permute-start.5) | collective-permute-done | bytes 24608 | tf_op jit(solution)/shard_map/ppermute | solution.py:418
  25.3 0.0 collective-permute-done.refs_10_.refs_4_
  25.3 0.0 collective-permute-done.1.refs_11_.refs_5_
  25.3 0.0 copy-done.4
  25.3 0.0 copy-done.5
  25.3 0.0 copy-done.1
  25.3 0.0 copy-done.2
  25.4 0.0 copy-done.7
  25.4 0.0 copy-done.8
  25.4 0.0 copy-done.9
  25.4 0.0 copy-done.10
  25.4 0.0 copy-done.3
  25.4 9.5 %moist.1 = (f32[58,16,256]{2,1,0:T(8,128)}, f32[58,16,256]{2,1,0:T(8,128)}, f32[58,16,256]{2,1,0:T(8,128)}, f32[512,128]{1,0:T(8,128)}) custom-call(f32[3,58]{1,0:T(4,128)S(1)} %copy-done.7, f32[58]{0:T(128)S(1)} %copy-done.8, f32[58]{0:T(128)S(1)} %copy-done.9, f32[58]{0:T(128)S(1)} %copy-done.10, f32[58,16,256]{2,1,0:T(8,128)S(1)} %copy-done.1, ...), custom_call_target="tpu_custom_call" | custom-call | flops 300000000 | bytes 6291456 | tf_op jit(solution)/shard_map/moist/pallas_call | solution.py:385
  34.9 3.5 %all-to-all-start = ((f32[16,32,128]{2,1,0:T(8,128)}), f32[16,32,128]{2,1,0:T(8,128)S(1)}, u32[]{:S(2)}, u32[]{:S(2)}) async-start(f32[16,32,128]{2,1,0:T(8,128)} %bitcast.4), calls=%async_computation | async-start | bytes 524288 | tf_op jit(solution)/shard_map/all_to_all | solution.py:452
  38.4 0.0 copy-done
  38.4 5.1 %dry.1 = f32[58,16,256]{2,1,0:T(8,128)} custom-call(f32[3,58]{1,0:T(4,128)S(1)} %copy-done.7, f32[58,16,256]{2,1,0:T(8,128)S(1)} %copy-done, f32[48,256]{1,0:T(8,128)S(1)} %bitcast.11, f32[16,256]{1,0:T(8,128)S(1)} %copy-done.5, f32[384,256]{1,0:T(8,128)S(1)} %collective-permute-done.refs_10_.refs_4_, ...), custom_call_target="tpu_custom_call" | custom-call | flops 100000000 | bytes 2097152 | tf_op jit(solution)/shard_map/dry/pallas_call | solution.py:385
  43.5 3.6 %all-to-all-done = f32[16,32,128]{2,1,0:T(8,128)S(1)} async-done(((f32[16,32,128]{2,1,0:T(8,128)}), f32[16,32,128]{2,1,0:T(8,128)S(1)}, u32[]{:S(2)}, u32[]{:S(2)}) %all-to-all-start) | async-done | bytes 262176 | tf_op jit(solution)/shard_map/all_to_all | solution.py:452
  47.1 0.6 %reduce_sum.9 = f32[32,128]{1,0:T(8,128)} reduce(f32[16,32,128]{2,1,0:T(8,128)S(1)} %all-to-all-done, f32[]{:T(128)} %constant.0.clone.1), dimensions={0}, to_apply=%region_0.0 | reduce | flops 61440 | bytes 278532 | tf_op jit(solution)/shard_map/reduce_sum | solution.py:456
  (3 shorter events, 0.0 us)
Async XLA Ops:
  0.6 24.7 %copy-start.4 = (f32[3,16,256]{2,1,0:T(8,128)S(1)}, f32[3,16,256]{2,1,0:T(8,128)}, u32[]{:S(2)}) copy-start(f32[3,16,256]{2,1,0:T(8,128)} %param.15) | copy-start | bytes 147460
  0.6 24.7 %copy-start.5 = (f32[16,256]{1,0:T(8,128)S(1)}, f32[16,256]{1,0:T(8,128)}, u32[]{:S(2)}) copy-start(f32[16,256]{1,0:T(8,128)} %refs_3_.3) | copy-start | bytes 49156
  0.7 24.7 %copy-start.1 = (f32[58,16,256]{2,1,0:T(8,128)S(1)}, f32[58,16,256]{2,1,0:T(8,128)}, u32[]{:S(2)}) copy-start(f32[58,16,256]{2,1,0:T(8,128)} %refs_4_.1) | copy-start | bytes 2850820
  0.7 24.7 %copy-start.2 = (f32[58,16,256]{2,1,0:T(8,128)S(1)}, f32[58,16,256]{2,1,0:T(8,128)}, u32[]{:S(2)}) copy-start(f32[58,16,256]{2,1,0:T(8,128)} %refs_5_.1) | copy-start | bytes 2850820
  0.7 24.7 %copy-start.7 = (f32[3,58]{1,0:T(4,128)S(1)}, f32[3,58]{1,0:T(4,128)}, u32[]{:S(2)}) copy-start(f32[3,58]{1,0:T(4,128)} %refs_0_.3) | copy-start | bytes 2092
  0.7 24.7 %copy-start.8 = (f32[58]{0:T(128)S(1)}, f32[58]{0:T(128)}, u32[]{:S(2)}) copy-start(f32[58]{0:T(128)} %refs_1_.2) | copy-start | bytes 700
  0.7 24.7 %copy-start.9 = (f32[58]{0:T(128)S(1)}, f32[58]{0:T(128)}, u32[]{:S(2)}) copy-start(f32[58]{0:T(128)} %refs_2_.1) | copy-start | bytes 700
  0.7 24.7 %copy-start.10 = (f32[58]{0:T(128)S(1)}, f32[58]{0:T(128)}, u32[]{:S(2)}) copy-start(f32[58]{0:T(128)} %refs_3_.2) | copy-start | bytes 700
  0.7 24.7 %copy-start.3 = (f32[58,16,256]{2,1,0:T(8,128)S(1)}, f32[58,16,256]{2,1,0:T(8,128)}, u32[]{:S(2)}) copy-start(f32[58,16,256]{2,1,0:T(8,128)} %refs_6_.1) | copy-start | bytes 2850820
  3.3 8.6 %collective-permute-start.2 = (f32[16,384]{1,0:T(8,128)S(1)}, f32[16,384]{1,0:T(8,128)S(1)}, u32[]{:S(2)}, u32[]{:S(2)}) collective-permute-start(f32[16,384]{1,0:T(8,128)S(1)} %get-tuple-element.15.refs_14_.refs_8_), channel_id=1, source_target_pairs={{1,0},{2,1},{3,2},{4,3},{5,4},{6,5},{7,6},{8,7},{9,8},{10,9},{11,1... | collective-permute-start | bytes 73736 | tf_op jit(solution)/shard_map/ppermute | solution.py:418
  10.0 15.4 %collective-permute-start = (f32[384,256]{1,0:T(8,128)S(1)}, f32[384,256]{1,0:T(8,128)S(1)}, u32[]{:S(2)}, u32[]{:S(2)}) collective-permute-start(f32[384,256]{1,0:T(8,128)S(1)} %get-tuple-element.13), channel_id=1, source_target_pairs={{16,0},{32,16},{48,32},{64,48},{80,64},{96,80},{112,96},{0,112},{1... | collective-permute-start | bytes 1179656 | tf_op jit(solution)/shard_map/ppermute | solution.py:418
  11.9 13.4 %collective-permute-start.1 = (f32[384,256]{1,0:T(8,128)S(1)}, f32[384,256]{1,0:T(8,128)S(1)}, u32[]{:S(2)}, u32[]{:S(2)}) collective-permute-start(f32[384,256]{1,0:T(8,128)S(1)} %get-tuple-element.14), channel_id=1, source_target_pairs={{112,0},{0,16},{16,32},{32,48},{48,64},{64,80},{80,96},{96,112},{1... | collective-permute-start | bytes 1179656 | tf_op jit(solution)/shard_map/ppermute | solution.py:418
  11.9 7.1 %collective-permute-start.3 = (f32[16,384]{1,0:T(8,128)S(1)}, f32[16,384]{1,0:T(8,128)S(1)}, u32[]{:S(2)}, u32[]{:S(2)}) collective-permute-start(f32[16,384]{1,0:T(8,128)S(1)} %get-tuple-element.16.refs_15_.refs_9_), channel_id=1, source_target_pairs={{15,0},{0,1},{1,2},{2,3},{3,4},{4,5},{5,6},{6,7},{7,8},{8,9},{9,10... | collective-permute-start | bytes 73736 | tf_op jit(solution)/shard_map/ppermute | solution.py:418
  19.0 3.7 %collective-permute-start.4 = (f32[8,768]{1,0:T(8,128)S(1)}, f32[8,768]{1,0:T(8,128)S(1)}, u32[]{:S(2)}, u32[]{:S(2)}) collective-permute-start(f32[8,768]{1,0:T(8,128)S(1)} %get-tuple-element.22), channel_id=1, source_target_pairs={{16,0},{32,16},{48,32},{64,48},{80,64},{96,80},{112,96},{0,112},{1... | collective-permute-start | bytes 73736 | tf_op jit(solution)/shard_map/ppermute | solution.py:418
  20.9 4.5 %collective-permute-start.5 = (f32[8,768]{1,0:T(8,128)S(1)}, f32[8,768]{1,0:T(8,128)S(1)}, u32[]{:S(2)}, u32[]{:S(2)}) collective-permute-start(f32[8,768]{1,0:T(8,128)S(1)} %get-tuple-element.21), channel_id=1, source_target_pairs={{112,0},{0,16},{16,32},{32,48},{48,64},{64,80},{80,96},{96,112},{1... | collective-permute-start | bytes 73736 | tf_op jit(solution)/shard_map/ppermute | solution.py:418
  20.9 0.7 %copy-start.6 = (s32[16,256]{1,0:T(8,128)S(1)}, s32[16,256]{1,0:T(8,128)}, u32[]{:S(2)}) copy-start(s32[16,256]{1,0:T(8,128)} %span_ref.1) | copy-start | bytes 49156
  22.7 15.7 %copy-start = (f32[58,16,256]{2,1,0:T(8,128)S(1)}, f32[58,16,256]{2,1,0:T(8,128)}, u32[]{:S(2)}) copy-start(f32[58,16,256]{2,1,0:T(8,128)} %refs_1_.3) | copy-start | bytes 2850820
  34.9 12.2 %all-to-all-start = ((f32[16,32,128]{2,1,0:T(8,128)}), f32[16,32,128]{2,1,0:T(8,128)S(1)}, u32[]{:S(2)}, u32[]{:S(2)}) async-start(f32[16,32,128]{2,1,0:T(8,128)} %bitcast.4), calls=%async_computation | async-start | bytes 524288 | tf_op jit(solution)/shard_map/all_to_all | solution.py:452
